TPU v7x, 128 devices: a whole 4x4x4 slice. The times are simulated.
128 devices in a mesh: region: 8 (over x, core), species: 16 (over z, y).
Axes of the slice: x: 4, y: 4, z: 4, core: 2. Of those that a mesh axis runs over, the one named last changes fastest.
Arguments:
- concentrations: float32 [256, 1024, 256], P('species', 'region'), may hold values from 0.05 to 5
- diffusion: float32 [256], P('species'), may hold values from 0.02 to 0.08
- courant_x: float32 [1024, 256], P('region'), may hold values from -0.2 to 0.2
- courant_y: float32 [1024, 256], P('region'), may hold values from -0.2 to 0.2
- log_rate: float32 [4, 768], replicated, may hold values from -3 to 0
- reactants: int32 [256, 768], replicated, may hold values from 0 to 1, as said below
- products: int32 [768, 256], replicated, may hold values from 0 to 1, as said below
- block_class: int32 [2048], P(('region', 'species')), may hold values from 0 to 3, as said below
- send_slot: int32 [2048], P(('region', 'species')), may hold values from -1 to 15, as said below
Outputs:
- reacted: float32 [256, 1024, 256], P('species', 'region')
Inputs may be any that keep to these rules, and one draw needn't show every extreme that they name: `send_slot`: block n lies on the device with region index n // 256 and species index (n // 16) % 16. A value t >= 0 marks a stiff block and names slot t % 2 of region t // 2; -1 marks the others. Among the blocks of one species index every value from 0 to 15 occurs exactly once; for each species index one device holds exactly 8 marked blocks, and no device holds more. The marked blocks of one device name different regions. `block_class`: A block marked in send_slot has class 3; every other block has a lower class. `reactants`: every column has one or two ones, in different rows. `products`: every row has one or two ones, in different columns.
All inputs are finite; a program needn't handle non-finite values.
Results may differ from a plain program's by a relative error of at most 0.0003.
Values sent between devices are 32-bit elements; how exact they have to be, the bound alone decides.
No kernel may reach another device: no remote copies, remote signals or barrier semaphores. Data moves between devices by JAX's collectives and lax.ppermute only.
A program may use at most 128 MiB of HBM per device.

v0:
```python
import functools

import jax
import jax.numpy as jnp
from jax import lax
from jax.experimental import pallas as pl
from jax.experimental.pallas import tpu as pltpu
from jax.sharding import PartitionSpec as P

STEPS = 3
ITERS = 2
SUB = 2
FLOOR = 0.05
EDGE = 8
DEEP = 2 * STEPS
LANES = 128
TILE = 4
bf16 = jnp.bfloat16
f32 = jnp.float32


def median0(p, r):
    return jnp.maximum(jnp.minimum(p, r), jnp.minimum(jnp.maximum(p, r), 0.0))


def shift_left(pair, lane):
    a, b = (pltpu.roll(v, LANES - 1, 1) for v in pair)
    last = lane == LANES - 1
    return jnp.where(last, b, a), jnp.where(last, 0.0, b)


def shift_right(pair, first, lane):
    a, b = (pltpu.roll(v, 1, 1) for v in pair)
    head = lane == 0
    return jnp.where(head, first, a), jnp.where(head, a, b)


def halves(v):
    return v[:, :LANES], v[:, LANES:]


def face_coefs(a):
    size = jnp.abs(a)
    return 0.5 * size * (1.0 - size)


def store_coefs(cx, cy, coef):
    ax = 0.5 * (cx + jnp.concatenate([cx[1:], cx[:1]], axis=0))
    edge = lax.broadcasted_iota(jnp.int32, cy.shape, 1) == 2 * LANES - 1
    ay = 0.5 * (cy + jnp.where(edge, 0.0, jnp.concatenate([cy[:, 1:], cy[:, :1]], axis=1)))
    al = 0.5 * cy[:, :LANES]
    al_weight = jnp.where(al < 0.0, face_coefs(al), 0.0)
    pairs = [halves(v) for v in (ax, face_coefs(ax), ay, face_coefs(ay))]
    pairs.append((jnp.minimum(al, 0.0), al_weight))
    for k, pair in enumerate(pairs):
        coef[2 * k] = pair[0]
        coef[2 * k + 1] = pair[1]


def one_flux(q, qn, d, m, mn, a, e, nu):
    up = a >= 0.0
    return a * jnp.where(up, q, qn) + e * jnp.where(up, m, mn) - nu * d


def sweep(load, store, coef, nu, lo, hi, unroll, keep=None):
    group = nu.shape[0]
    lane = lax.broadcasted_iota(jnp.int32, (group, LANES), 1)

    def spread(which, row):
        return tuple(coef[2 * which + k, pl.ds(row, group, stride=0), :] for k in (0, 1))

    def x_flux(row, q, qn, d, m, mn):
        a, e = spread(0, row), spread(1, row)
        return tuple(one_flux(q[i], qn[i], d[i], m[i], mn[i], a[i], e[i], nu) for i in (0, 1))

    def diff(q, qn):
        return tuple(y - x for x, y in zip(q, qn))

    def limited(p, r):
        return tuple(median0(x, y) for x, y in zip(p, r))

    qa, qb, qc, qd = (load(lo + k) for k in (-2, -1, 0, 1))
    da, db, dc = diff(qa, qb), diff(qb, qc), diff(qc, qd)
    mb, mc = limited(da, db), limited(db, dc)
    behind = x_flux(lo - 1, qb, qc, db, mb, mc)

    def row_step(row, carry):
        q, qn, d, m, behind = carry
        qnn = load(row + 2)
        dn = diff(qn, qnn)
        mn = limited(d, dn)
        fx = x_flux(row, q, qn, d, m, mn)
        right = shift_left(q, lane)
        g = diff(q, right)
        s = limited(shift_right(g, q[0], lane), g)
        sn = shift_left(s, lane)
        a, e = spread(2, row), spread(3, row)
        fy = tuple(one_flux(q[i], right[i], g[i], s[i], sn[i], a[i], e[i], nu) for i in (0, 1))
        la, le = spread(4, row)
        fl = shift_right(fy, (la - nu) * q[0] + le * s[0], lane)
        new = tuple(q[i] - (fx[i] - behind[i]) - (fy[i] - fl[i]) for i in (0, 1))
        if keep is not None:
            scale = keep(row)
            new = tuple(v * scale for v in new)
        store(row, new)
        return qn, qnn, dn, mn, fx

    def steps(i, carry):
        for k in range(unroll):
            carry = row_step(lo + i * unroll + k, carry)
        return carry

    count = hi - lo
    carry = lax.fori_loop(0, count // unroll, steps, (qc, qd, dc, mc, behind))
    for row in range(lo + count // unroll * unroll, hi):
        carry = row_step(row, carry)


def buffer_access(buf):
    def load(row):
        return buf[row, :, :LANES], buf[row, :, LANES:]

    def store(row, pair):
        buf[row, :, :LANES] = pair[0]
        buf[row, :, LANES:] = pair[1]

    return load, store


def interior_kernel(conc0, conc1, cx, cy, diffuse, left, right, coef, one, two):
    group = diffuse.shape[0]
    rows = cx.shape[0]
    nu = jnp.broadcast_to(diffuse[...], (group, LANES))
    store_coefs(cx[...], cy[...], coef)
    load1, store1 = buffer_access(one)
    load2, store2 = buffer_access(two)

    def load0(row):
        return tuple(c[pl.ds(row, group, stride=rows), :] for c in (conc0, conc1))

    def store3(row, pair):
        left[row] = pair[0]
        right[row] = pair[1]

    sweep(load0, store1, coef, nu, 2, rows - 2, 4)
    sweep(load1, store2, coef, nu, 4, rows - 4, 4)
    sweep(load2, store3, coef, nu, 6, rows - 6, 4)


def edge_kernel(
    place,
    conc0,
    conc1,
    cx,
    cy,
    before0,
    before1,
    after0,
    after1,
    diffuse,
    left_in,
    right_in,
    left,
    right,
    coef,
    one,
    two,
    three,
):
    group = diffuse.shape[0]
    top = pl.program_id(0) == 0
    nu = jnp.broadcast_to(diffuse[...], (group, LANES))
    own = 2 * EDGE
    slab = own + EDGE

    def fill(first, halo, halo_first):
        for side, (conc, rim) in enumerate(zip((conc0, conc1), halo)):
            lanes = slice(side * LANES, (side + 1) * LANES)
            for k in range(own):
                one[first + k, :, lanes] = conc[:, k, :]
            for k in range(EDGE):
                one[halo_first + k, :, lanes] = rim[pl.ds(k, group, stride=EDGE), :]
        winds = jnp.concatenate([h[group * EDGE :] for h in halo], axis=1)
        rim = winds[:EDGE], winds[EDGE:]
        order = (lambda a, b: (a, b)) if halo_first else (lambda a, b: (b, a))
        store_coefs(
            jnp.concatenate(order(cx[...], rim[0]), axis=0),
            jnp.concatenate(order(cy[...], rim[1]), axis=0),
            coef,
        )

    @pl.when(top)
    def _():
        fill(EDGE, (before0, before1), 0)

    @pl.when(jnp.logical_not(top))
    def _():
        fill(0, (after0, after1), own)

    open_top = jnp.logical_and(top, place[0] == 0)
    open_end = jnp.logical_and(jnp.logical_not(top), place[0] == place[1] - 1)

    def keep(row):
        out = jnp.logical_or(
            jnp.logical_and(open_top, row < EDGE), jnp.logical_and(open_end, row >= own)
        )
        return jnp.where(out, 0.0, 1.0)

    load1, store1 = buffer_access(one)
    load2, store2 = buffer_access(two)
    load3, store3 = buffer_access(three)
    sweep(load1, store2, coef, nu, 4, slab - 4, 4, keep)
    sweep(load2, store3, coef, nu, 6, slab - 6, 4, keep)
    sweep(load3, store1, coef, nu, 8, slab - 8, 4)
    left[...] = left_in[...]
    right[...] = right_in[...]

    @pl.when(top)
    def _():
        for k in range(DEEP):
            left[k] = one[EDGE + k, :, :LANES]
            right[k] = one[EDGE + k, :, LANES:]

    @pl.when(jnp.logical_not(top))
    def _():
        for k in range(EDGE - DEEP, EDGE):
            left[k] = one[EDGE + k, :, :LANES]
            right[k] = one[EDGE + k, :, LANES:]


def split(x):
    high = x.astype(bf16)
    return high, (x - high.astype(f32)).astype(bf16)


def table_dot(table, x):
    high, low = split(x)
    return jnp.dot(table, high, preferred_element_type=f32) + jnp.dot(
        table, low, preferred_element_type=f32
    )


def euler(state, logs, step, reac, both):
    species = state.shape[0]
    g = state
    for _ in range(ITERS):
        rates = jnp.exp(logs + table_dot(reac, jnp.log(g)))
        made_lost = table_dot(both, rates)
        g = (state + step * made_lost[:species]) / (1.0 + step * made_lost[species:] / g)
    return g


def chemistry_kernel(classes, slots, x, log_table, reac, both, out, result, listed):
    peers, blocks, group, _ = x.shape
    species = peers * group
    count = jnp.int32(0)
    for b in range(blocks):
        listed[count] = b
        count = count + (slots[b] >= 0).astype(jnp.int32)

    def tile(chosen, first):
        states, logs, lengths = [], [], []
        for b in chosen:
            if first:
                states.append(jnp.maximum(x[:, b].reshape(species, LANES), FLOOR))
                length = jnp.where(slots[b] >= 0, 1.0 / SUB, 1.0)
            else:
                states.append(result[b])
                length = 1.0 / SUB
            lengths.append(jnp.full((1, LANES), length, f32))
            logs.append(log_table[classes[b]])
        g = euler(
            jnp.concatenate(states, axis=1),
            jnp.concatenate(logs, axis=1),
            jnp.concatenate(lengths, axis=1),
            reac[...],
            both[...],
        )
        for i, b in enumerate(chosen):
            piece = g[:, i * LANES : (i + 1) * LANES]
            result[b] = piece
            for k in range(0, species, 8):
                out[pl.ds(k * blocks + b, 8, stride=blocks), :] = piece[k : k + 8]

    @pl.loop(0, blocks // TILE)
    def _(i):
        tile([i * TILE + j for j in range(TILE)], True)

    for _ in range(SUB - 1):

        @pl.loop(0, (count + TILE - 1) // TILE)
        def _(i):
            tile([listed[jnp.minimum(i * TILE + j, count - 1)] for j in range(TILE)], False)


def chemistry(x, classes, slots, log_table, reac, both):
    peers, blocks, group, _ = x.shape
    species = peers * group
    vmem = pl.BlockSpec(memory_space=pltpu.VMEM)
    smem = pl.BlockSpec(memory_space=pltpu.SMEM)
    return pl.pallas_call(
        chemistry_kernel,
        out_shape=jax.ShapeDtypeStruct((species * blocks, LANES), f32),
        in_specs=[smem, smem, vmem, vmem, vmem, vmem],
        out_specs=vmem,
        scratch_shapes=[
            pltpu.VMEM((blocks, species, LANES), f32),
            pltpu.SMEM((blocks,), jnp.int32),
        ],
        compiler_params=pltpu.CompilerParams(vmem_limit_bytes=40 << 20),
        name="chemistry",
    )(classes, slots, x, log_table, reac, both)


def per_device(
    concentrations,
    diffusion,
    courant_x,
    courant_y,
    log_rate,
    reactants,
    products,
    block_class,
    send_slot,
):
    group, rows, columns = concentrations.shape
    species, reactions = reactants.shape
    peers = species // group
    regions = lax.axis_size("region")
    up = [(i, (i + 1) % regions) for i in range(regions - 1)]
    down = [(j, i) for i, j in up]
    winds = jnp.stack([courant_x, courant_y])
    last = jnp.concatenate([concentrations[:, rows - EDGE :], winds[:, rows - EDGE :]], axis=0)
    leading = jnp.concatenate([concentrations[:, :EDGE], winds[:, :EDGE]], axis=0)
    before = lax.ppermute(last, "region", up)
    after = lax.ppermute(leading, "region", down)
    diffuse = diffusion[:, None]
    vmem = pl.BlockSpec(memory_space=pltpu.VMEM)
    half = jax.ShapeDtypeStruct((rows, group, LANES), f32)
    row_buffer = pltpu.VMEM((rows, group, columns), f32)
    left, right = pl.pallas_call(
        interior_kernel,
        out_shape=(half, half),
        grid=(1,),
        in_specs=[
            pl.BlockSpec((group * rows, LANES), lambda i: (0, 0)),
            pl.BlockSpec((group * rows, LANES), lambda i: (0, 1)),
            vmem,
            vmem,
            vmem,
        ],
        out_specs=(vmem, vmem),
        scratch_shapes=[pltpu.VMEM((10, rows, LANES), f32), row_buffer, row_buffer],
        compiler_params=pltpu.CompilerParams(vmem_limit_bytes=40 << 20),
        name="interior",
    )(*[concentrations.reshape(group * rows, columns)] * 2, courant_x, courant_y, diffuse)

    place = jnp.stack([lax.axis_index("region"), jnp.int32(regions)]).astype(jnp.int32)
    own = 2 * EDGE
    far = rows // own - 1
    far_out = rows // EDGE - 1
    slab_buffer = pltpu.VMEM((own + EDGE, group, columns), f32)

    def conc_spec(side):
        return pl.BlockSpec((group, own, LANES), lambda i: (0, i * far, side))

    def halo_spec(side):
        return pl.BlockSpec(((group + 2) * EDGE, LANES), lambda i: (0, side))

    wind_spec = pl.BlockSpec((own, columns), lambda i: (i * far, 0))
    half_spec = pl.BlockSpec((EDGE, group, LANES), lambda i: (i * far_out, 0, 0))
    left, right = pl.pallas_call(
        edge_kernel,
        grid=(2,),
        out_shape=(half, half),
        in_specs=[
            pl.BlockSpec(memory_space=pltpu.SMEM),
            conc_spec(0),
            conc_spec(1),
            wind_spec,
            wind_spec,
            halo_spec(0),
            halo_spec(1),
            halo_spec(0),
            halo_spec(1),
            pl.BlockSpec((group, 1), lambda i: (0, 0)),
            half_spec,
            half_spec,
        ],
        out_specs=(half_spec, half_spec),
        scratch_shapes=[pltpu.VMEM((10, own + EDGE, LANES), f32)] + [slab_buffer] * 3,
        input_output_aliases={10: 0, 11: 1},
        name="edges",
    )(
        place,
        concentrations,
        concentrations,
        courant_x,
        courant_y,
        *[before.reshape((group + 2) * EDGE, columns)] * 2,
        *[after.reshape((group + 2) * EDGE, columns)] * 2,
        diffuse,
        left,
        right,
    )

    reac = reactants.T.astype(bf16)
    both = jnp.concatenate([products.T, reactants], axis=0).astype(bf16)
    log_table = jnp.broadcast_to(log_rate[:, :, None], log_rate.shape + (LANES,))
    blocks = rows // peers
    classes = block_class.reshape(blocks, 2)
    slots = send_slot.reshape(blocks, 2)
    done = []
    for side, part in enumerate((left, right)):
        mine = lax.all_to_all(part, "species", split_axis=0, concat_axis=0, tiled=True)
        reacted = chemistry(
            mine.reshape(peers, blocks, group, LANES),
            classes[:, side],
            slots[:, side],
            log_table,
            reac,
            both,
        )
        done.append(
            lax.all_to_all(
                reacted.reshape(peers, group, blocks, LANES),
                "species",
                split_axis=0,
                concat_axis=0,
                tiled=True,
            )
        )
    whole = jnp.concatenate(done, axis=3)
    return whole.transpose(1, 0, 2, 3).reshape(group, rows, columns)


def solution(mesh):
    in_specs = (
        P("species", "region", None),
        P("species"),
        P("region", None),
        P("region", None),
        P(),
        P(),
        P(),
        P(("region", "species")),
        P(("region", "species")),
    )
    out_specs = P("species", "region", None)
    return jax.shard_map(
        per_device, mesh=mesh, in_specs=in_specs, out_specs=out_specs, check_vma=False
    )
```

profile of v0, /device:TPU:0, one launch (start us, length us, event | category | flops | bytes accessed | tf_op | source)
XLA Modules:
  0.0 144.1 jit_solution(13276606737638367834)
XLA Ops:
  0.0 1.0 fusion.2
  1.0 0.8 fusion
  1.8 1.3 collective-permute-start
  3.1 1.3 collective-permute-start.1
  4.4 0.7 copy.19.diffuse
  5.1 1.6 %copy-done = f32[16,128,256]{2,1,0:T(8,128)S(1)} copy-done((f32[16,128,256]{2,1,0:T(8,128)S(1)}, f32[16,128,256]{2,1,0:T(8,128)}, u32[]{:S(2)}) %copy-start) | copy-done | bytes 2097176
  6.7 0.9 copy-done.7
  7.6 0.9 copy-done.8
  8.5 28.8 %interior.1 = (f32[128,16,128]{2,1,0:T(8,128)S(1)}, f32[128,16,128]{2,1,0:T(8,128)}) custom-call(f32[2048,256]{1,0:T(8,128)S(1)} %bitcast.20, f32[2048,256]{1,0:T(8,128)S(1)} %bitcast.21, f32[128,256]{1,0:T(8,128)S(1)} %copy-done.7, f32[128,256]{1,0:T(8,128)S(1)} %copy-done.8, f32[16,1]{1,0:T(8,128)S(1)} %copy.19.diffuse), custom_call_target="tpu_custom_call" | custom-call | tf_op jit(solution)/shard_map/interior/pallas_call | solution.py:341
  37.4 1.0 copy-done.3
  39.6 8.0 %edges.1 = (f32[128,16,128]{2,1,0:T(8,128)}, f32[128,16,128]{2,1,0:T(8,128)}) custom-call(s32[2]{0:T(128)} %pad_add_fusion.place, f32[16,128,256]{2,1,0:T(8,128)} %conc1.1, f32[16,128,256]{2,1,0:T(8,128)} %conc1.1, f32[128,256]{1,0:T(8,128)} %cx.3, f32[128,256]{1,0:T(8,128)} %cy.3, ...), custom_call_target="tpu_custom_call", output_to_operand_aliasing={{0}: (10, {}), {1}: (11, {})} | custom-call | tf_op jit(solution)/shard_map/edges/pallas_call | solution.py:372
  47.7 26.3 %all_to_all.20 = f32[128,16,128]{2,1,0:T(8,128)} all-to-all(f32[128,16,128]{2,1,0:T(8,128)} %get-tuple-element.11), channel_id=1, replica_groups=mesh['region'=8,'species'=16] {'species'}, dimensions={0} | all-to-all | bytes 2097152 | tf_op jit(solution)/shard_map/all_to_all | solution.py:415
  73.9 3.9 %all-to-all-start.2 = ((f32[128,16,128]{2,1,0:T(8,128)}), f32[128,16,128]{2,1,0:T(8,128)S(1)}, u32[]{:S(2)}, u32[]{:S(2)}) async-start(f32[128,16,128]{2,1,0:T(8,128)} %get-tuple-element.12), calls=%async_computation.2 | async-start | bytes 2097152 | tf_op jit(solution)/shard_map/all_to_all | solution.py:415
  78.4 0.9 copy.21.reac
  80.9 10.2 %chemistry.2 = f32[2048,128]{1,0:T(8,128)S(1)} custom-call(s32[8]{0:T(128)S(1)} %get-tuple-element.22.classes, s32[8]{0:T(128)S(1)} %get-tuple-element.13.slots, f32[16,8,16,128]{3,2,1,0:T(8,128)S(1)} %bitcast.23, f32[4,768,128]{2,1,0:T(8,128)S(1)} %broadcast_in_dim.10.log_table, bf16[768,256]{1,0:T(8,128)(2,1)S(1)} %copy-done.5, ...), custom_call_target="tpu_custom_call" | custom-call | tf_op jit(solution)/shard_map/chemistry/pallas_call | solution.py:301
  91.1 1.0 copy-done.2
  92.1 6.5 %all-to-all-done.2 = f32[128,16,128]{2,1,0:T(8,128)S(1)} async-done(((f32[128,16,128]{2,1,0:T(8,128)}), f32[128,16,128]{2,1,0:T(8,128)S(1)}, u32[]{:S(2)}, u32[]{:S(2)}) %all-to-all-start.2) | async-done | bytes 1048608 | tf_op jit(solution)/shard_map/all_to_all | solution.py:415
  98.6 4.3 %all-to-all-start.1 = ((f32[16,16,8,128]{3,2,1,0:T(8,128)}), f32[16,16,8,128]{3,2,1,0:T(8,128)}, u32[]{:S(2)}, u32[]{:S(2)}) async-start(f32[16,16,8,128]{3,2,1,0:T(8,128)} %bitcast.24), calls=%async_computation.1 | async-start | bytes 2097152 | tf_op jit(solution)/shard_map/all_to_all | solution.py:425
  103.0 1.0 copy-done.6
  104.0 7.1 %chemistry.3 = f32[2048,128]{1,0:T(8,128)S(1)} custom-call(s32[8]{0:T(128)S(1)} %get-tuple-element.21.classes, s32[8]{0:T(128)S(1)} %get-tuple-element.14.slots, f32[16,8,16,128]{3,2,1,0:T(8,128)S(1)} %bitcast.22, f32[4,768,128]{2,1,0:T(8,128)S(1)} %broadcast_in_dim.10.log_table, bf16[768,256]{1,0:T(8,128)(2,1)S(1)} %copy-done.6, ...), custom_call_target="tpu_custom_call" | custom-call | tf_op jit(solution)/shard_map/chemistry/pallas_call | solution.py:301
  111.1 1.0 copy-done.4
  112.1 8.7 %all-to-all-done.1 = f32[16,16,8,128]{3,2,1,0:T(8,128)} async-done(((f32[16,16,8,128]{3,2,1,0:T(8,128)}), f32[16,16,8,128]{3,2,1,0:T(8,128)}, u32[]{:S(2)}, u32[]{:S(2)}) %all-to-all-start.1) | async-done | bytes 1048608 | tf_op jit(solution)/shard_map/all_to_all | solution.py:425
  120.8 20.6 %all_to_all.21 = f32[16,16,8,128]{3,2,1,0:T(8,128)S(1)} all-to-all(f32[16,16,8,128]{3,2,1,0:T(8,128)} %bitcast.25), channel_id=1, replica_groups=mesh['region'=8,'species'=16] {'species'}, dimensions={0} | all-to-all | bytes 2097152 | tf_op jit(solution)/shard_map/all_to_all | solution.py:425
  141.4 2.7 %copy_bitcast_fusion = f32[16,128,256]{2,1,0:T(8,128)} fusion(f32[16,16,8,128]{3,2,1,0:T(8,128)S(1)} %all_to_all.21, f32[16,16,8,128]{3,2,1,0:T(8,128)} %all-to-all-done.1), kind=kLoop, calls=%fused_computation.1 | loop fusion | flops 524288 | bytes 4194304 | tf_op jit(solution)/shard_map/reshape | solution.py:434
  (39 shorter events, 3.3 us)
Async XLA Ops:
  1.8 37.1 %collective-permute-start = (f32[18,8,256]{2,1,0:T(8,128)S(1)}, f32[18,8,256]{2,1,0:T(8,128)S(1)}, u32[]{:S(2)}, u32[]{:S(2)}) collective-permute-start(f32[18,8,256]{2,1,0:T(8,128)S(1)} %get-tuple-element.20), channel_id=1, source_target_pairs={{0,16},{16,32},{32,48},{48,64},{64,80},{80,96},{96,112},{1,17},{17... | collective-permute-start | bytes 442376 | tf_op jit(solution)/shard_map/ppermute | solution.py:335
  3.1 35.8 %collective-permute-start.1 = (f32[18,8,256]{2,1,0:T(8,128)S(1)}, f32[18,8,256]{2,1,0:T(8,128)S(1)}, u32[]{:S(2)}, u32[]{:S(2)}) collective-permute-start(f32[18,8,256]{2,1,0:T(8,128)S(1)} %get-tuple-element.19), channel_id=1, source_target_pairs={{16,0},{32,16},{48,32},{64,48},{80,64},{96,80},{112,96},{17,1},{33... | collective-permute-start | bytes 442376 | tf_op jit(solution)/shard_map/ppermute | solution.py:336
  5.1 32.3 %copy-start.9 = (f32[16,1]{1,0:T(8,128)}, f32[16,1]{1,0:T(8,128)S(1)}, u32[]{:S(2)}) copy-start(f32[16,1]{1,0:T(8,128)S(1)} %copy.19.diffuse) | copy-start | bytes 196
  5.1 1.6 %copy-start = (f32[16,128,256]{2,1,0:T(8,128)S(1)}, f32[16,128,256]{2,1,0:T(8,128)}, u32[]{:S(2)}) copy-start(f32[16,128,256]{2,1,0:T(8,128)} %conc1.1) | copy-start | bytes 6291460
  6.7 0.9 copy-start.7
  7.6 0.9 copy-start.8
  37.4 1.0 copy-start.3
  38.9 0.7 copy-start.12
  38.9 0.7 copy-start.13
  47.6 30.2 %copy-start.15 = (s32[16]{0:T(128)S(1)}, s32[16]{0:T(128)}, u32[]{:S(2)}) copy-start(s32[16]{0:T(128)} %param.16) | copy-start | bytes 196
  47.6 30.3 %copy-start.16 = (s32[16]{0:T(128)S(1)}, s32[16]{0:T(128)}, u32[]{:S(2)}) copy-start(s32[16]{0:T(128)} %param.17) | copy-start | bytes 196
  47.7 30.4 %copy-start.11 = (s32[768,256]{1,0:T(8,128)S(1)}, s32[768,256]{1,0:T(8,128)}, u32[]{:S(2)}) copy-start(s32[768,256]{1,0:T(8,128)} %param.15) | copy-start | bytes 2359300
  73.9 4.4 %copy-start.10 = (s32[256,768]{1,0:T(8,128)S(1)}, s32[256,768]{1,0:T(8,128)}, u32[]{:S(2)}) copy-start(s32[256,768]{1,0:T(8,128)} %param.14) | copy-start | bytes 2359300
  73.9 24.7 %all-to-all-start.2 = ((f32[128,16,128]{2,1,0:T(8,128)}), f32[128,16,128]{2,1,0:T(8,128)S(1)}, u32[]{:S(2)}, u32[]{:S(2)}) async-start(f32[128,16,128]{2,1,0:T(8,128)} %get-tuple-element.12), calls=%async_computation.2 | async-start | bytes 2097152 | tf_op jit(solution)/shard_map/all_to_all | solution.py:415
  78.4 1.3 copy-start.14
  79.6 1.2 copy-start.1
  79.6 1.3 copy-start.5
  91.1 1.0 copy-start.2
  98.6 22.2 %all-to-all-start.1 = ((f32[16,16,8,128]{3,2,1,0:T(8,128)}), f32[16,16,8,128]{3,2,1,0:T(8,128)}, u32[]{:S(2)}, u32[]{:S(2)}) async-start(f32[16,16,8,128]{3,2,1,0:T(8,128)} %bitcast.24), calls=%async_computation.1 | async-start | bytes 2097152 | tf_op jit(solution)/shard_map/all_to_all | solution.py:425
  103.0 1.0 copy-start.6
  111.1 1.0 copy-start.4
where the time goes:
time: 145 us; the launch traced here: 144 us
  Pallas kernels  54.2 us (37%)
  blocking collectives  46.9 us (32%)
  waiting for transfers between devices  15.3 us (11%)
  local copies, waits for them, and re-layouts  12.5 us (9%)
  starting transfers between devices  10.8 us (7%)
  other arithmetic  4.19 us (3%)
    pallas_call x1, Pallas kernels, per_device(): pl.pallas_call(interior_kernel, out_shape=(half, half), grid=(1,), in_spe...  28.8 us
    all_to_all x1, blocking collectives, per_device(): lax.all_to_all(part, 'species', split_axis=0, concat_axis=0, tiled=True)  26.3 us
    all_to_all x1, blocking collectives, per_device(): lax.all_to_all(reacted.reshape(peers, group, blocks, LANES), 'species', s...  20.6 us
    pallas_call x2, Pallas kernels, chemistry(): pl.pallas_call(chemistry_kernel, out_shape=jax.ShapeDtypeStruct((species...  17.4 us
    unnamed x35, local copies, waits for them, and re-layouts  9.04 us
    all_to_all x1, waiting for transfers between devices, per_device(): lax.all_to_all(reacted.reshape(peers, group, blocks, LANES), 'species', s...  8.73 us
    pallas_call x1, Pallas kernels, per_device(): pl.pallas_call(edge_kernel, grid=(2,), out_shape=(half, half), in_specs=[...  8.01 us
    all_to_all x1, waiting for transfers between devices, per_device(): lax.all_to_all(part, 'species', split_axis=0, concat_axis=0, tiled=True)  6.54 us
  transfers between devices with their start and end apart: 4, of which 2 were waited for; matrix products, arithmetic and copies ran while one was open for 2% of the time, Pallas kernels for 32%

commit v1 on v0

v1 whole, which is shorter than its diff:
```python
import functools

import jax
import jax.numpy as jnp
from jax import lax
from jax.experimental import pallas as pl
from jax.experimental.pallas import tpu as pltpu
from jax.sharding import PartitionSpec as P

STEPS = 3
ITERS = 2
SUB = 2
FLOOR = 0.05
EDGE = 8
LANES = 128
TILE = 4
bf16 = jnp.bfloat16
f32 = jnp.float32


def median0(p, r):
    return jnp.maximum(jnp.minimum(p, r), jnp.minimum(jnp.maximum(p, r), 0.0))


def shift_left(pair, lane):
    a, b = (pltpu.roll(v, LANES - 1, 1) for v in pair)
    last = lane == LANES - 1
    return jnp.where(last, b, a), jnp.where(last, 0.0, b)


def shift_right(pair, first, lane):
    a, b = (pltpu.roll(v, 1, 1) for v in pair)
    head = lane == 0
    return jnp.where(head, first, a), jnp.where(head, a, b)


def halves(v):
    return v[:, :LANES], v[:, LANES:]


def face_coefs(a):
    size = jnp.abs(a)
    return 0.5 * size * (1.0 - size)


def store_coefs(cx, cy, coef):
    ax = 0.5 * (cx + jnp.concatenate([cx[1:], cx[:1]], axis=0))
    edge = lax.broadcasted_iota(jnp.int32, cy.shape, 1) == 2 * LANES - 1
    ay = 0.5 * (cy + jnp.where(edge, 0.0, jnp.concatenate([cy[:, 1:], cy[:, :1]], axis=1)))
    al = 0.5 * cy[:, :LANES]
    al_weight = jnp.where(al < 0.0, face_coefs(al), 0.0)
    pairs = [halves(v) for v in (ax, face_coefs(ax), ay, face_coefs(ay))]
    pairs.append((jnp.minimum(al, 0.0), al_weight))
    for k, pair in enumerate(pairs):
        coef[2 * k] = pair[0]
        coef[2 * k + 1] = pair[1]


def one_flux(q, qn, d, m, mn, a, e, nu):
    up = a >= 0.0
    return a * jnp.where(up, q, qn) + e * jnp.where(up, m, mn) - nu * d


def sweep(load, store, coef, nu, lo, hi, unroll, keep=None):
    group = nu.shape[0]
    lane = lax.broadcasted_iota(jnp.int32, (group, LANES), 1)

    def spread(which, row):
        return tuple(coef[2 * which + k, pl.ds(row, group, stride=0), :] for k in (0, 1))

    def x_flux(row, q, qn, d, m, mn):
        a, e = spread(0, row), spread(1, row)
        return tuple(one_flux(q[i], qn[i], d[i], m[i], mn[i], a[i], e[i], nu) for i in (0, 1))

    def diff(q, qn):
        return tuple(y - x for x, y in zip(q, qn))

    def limited(p, r):
        return tuple(median0(x, y) for x, y in zip(p, r))

    qa, qb, qc, qd = (load(lo + k) for k in (-2, -1, 0, 1))
    da, db, dc = diff(qa, qb), diff(qb, qc), diff(qc, qd)
    mb, mc = limited(da, db), limited(db, dc)
    behind = x_flux(lo - 1, qb, qc, db, mb, mc)

    def row_step(row, carry):
        q, qn, d, m, behind = carry
        qnn = load(row + 2)
        dn = diff(qn, qnn)
        mn = limited(d, dn)
        fx = x_flux(row, q, qn, d, m, mn)
        right = shift_left(q, lane)
        g = diff(q, right)
        s = limited(shift_right(g, q[0], lane), g)
        sn = shift_left(s, lane)
        a, e = spread(2, row), spread(3, row)
        fy = tuple(one_flux(q[i], right[i], g[i], s[i], sn[i], a[i], e[i], nu) for i in (0, 1))
        la, le = spread(4, row)
        fl = shift_right(fy, (la - nu) * q[0] + le * s[0], lane)
        new = tuple(q[i] - (fx[i] - behind[i]) - (fy[i] - fl[i]) for i in (0, 1))
        if keep is not None:
            scale = keep(row)
            new = tuple(v * scale for v in new)
        store(row, new)
        return qn, qnn, dn, mn, fx

    def steps(i, carry):
        for k in range(unroll):
            carry = row_step(lo + i * unroll + k, carry)
        return carry

    count = hi - lo
    carry = lax.fori_loop(0, count // unroll, steps, (qc, qd, dc, mc, behind))
    for row in range(lo + count // unroll * unroll, hi):
        carry = row_step(row, carry)


def buffer_access(buf):
    def load(row):
        return buf[row, :, :LANES], buf[row, :, LANES:]

    def store(row, pair):
        buf[row, :, :LANES] = pair[0]
        buf[row, :, LANES:] = pair[1]

    return load, store


def start_all(copies):
    for copy in copies:
        copy.start()


def wait_all(copies):
    for copy in copies:
        copy.wait()


def spread_species(diffuse, group):
    lane = lax.broadcasted_iota(jnp.int32, (group, LANES), 0)
    nu = jnp.zeros((group, LANES), f32)
    for k in range(group):
        nu = jnp.where(lane == k, diffuse[k], nu)
    return nu


def raw_access(block):
    group, rows, _ = block.shape[1:]
    flat = [block.at[k].reshape(group * rows, LANES) for k in (0, 1)]

    def load(row):
        return tuple(part[pl.ds(row, group, stride=rows), :] for part in flat)

    return load


def three_sweeps(load, store, coef, nu, one, two, rows, unrolls, keep=None):
    load1, store1 = buffer_access(one)
    load2, store2 = buffer_access(two)
    sweep(load, store1, coef, nu, 4, rows - 4, unrolls[0], keep)
    sweep(load1, store2, coef, nu, 6, rows - 6, unrolls[1], keep)
    sweep(load2, store, coef, nu, 8, rows - 8, unrolls[2])


def store_grouped(out, base):
    def store(row, pair):
        at = row - EDGE
        place, inner = base + lax.shift_right_logical(at, 3), lax.bitwise_and(at, 7)
        out[place, 0, inner] = pair[0]
        out[place, 1, inner] = pair[1]

    return store


def middle_kernel(diffuse, conc, cx, cy, out, raw, wx, wy, coef, one, two, sems):
    group, rows = raw.shape[1:3]
    first = conc.shape[1] // 4 - EDGE
    copies = [
        pltpu.make_async_copy(src.at[pl.ds(first, rows)], dst, sems.at[k])
        for k, (src, dst) in enumerate(((cx, wx), (cy, wy)))
    ]
    copies += [
        pltpu.make_async_copy(
            conc.at[:, pl.ds(first, rows), pl.ds(k * LANES, LANES)], raw.at[k], sems.at[2 + k]
        )
        for k in (0, 1)
    ]
    start_all(copies)
    nu = spread_species(diffuse, group)
    wait_all(copies[:2])
    store_coefs(wx[...], wy[...], coef)
    wait_all(copies[2:])
    three_sweeps(
        raw_access(raw), store_grouped(out, 0), coef, nu, one, two, rows, (18, 17, 16)
    )


def edge_kernel(
    diffuse, place, conc, cx, cy, before, after, out, raw, wx, wy, coef, one, two, sems
):
    group, rows = raw.shape[2:4]
    total = conc.shape[1]
    own = rows - EDGE
    copies = []

    def copy(src, dst):
        copies.append(pltpu.make_async_copy(src, dst, sems.at[len(copies)]))

    for slab, halo, own_first, own_at, halo_at in (
        (0, before, 0, EDGE, 0),
        (1, after, total - own, 0, own),
    ):
        for k, (wind, dst) in enumerate(((cx, wx), (cy, wy))):
            copy(wind.at[pl.ds(own_first, own)], dst.at[slab, pl.ds(own_at, own)])
            copy(halo.at[group + k], dst.at[slab, pl.ds(halo_at, EDGE)])
        for k in (0, 1):
            lanes = pl.ds(k * LANES, LANES)
            dst = raw.at[slab, k]
            copy(conc.at[:, pl.ds(own_first, own), lanes], dst.at[:, pl.ds(own_at, own)])
            copy(halo.at[pl.ds(0, group), :, lanes], dst.at[:, pl.ds(halo_at, EDGE)])
    start_all(copies)
    nu = spread_species(diffuse, group)
    wait_all(copies)

    @pl.loop(0, 2)
    def _(slab):
        store_coefs(wx[slab], wy[slab], coef)
        open_top = jnp.logical_and(slab == 0, place[0] == 0)
        open_end = jnp.logical_and(slab == 1, place[0] == place[1] - 1)

        def keep(row):
            outside = jnp.logical_or(
                jnp.logical_and(open_top, row < EDGE), jnp.logical_and(open_end, row >= own)
            )
            return jnp.where(outside, 0.0, 1.0)

        three_sweeps(
            raw_access(raw.at[slab]),
            store_grouped(out, slab * 4),
            coef,
            nu,
            one,
            two,
            rows,
            (10, 12, 16),
            keep,
        )


def split(x):
    high = x.astype(bf16)
    return high, (x - high.astype(f32)).astype(bf16)


def table_dot(table, x):
    high, low = split(x)
    return jnp.dot(table, high, preferred_element_type=f32) + jnp.dot(
        table, low, preferred_element_type=f32
    )


def euler(state, logs, step, reac, both):
    species = state.shape[0]
    g = state
    for _ in range(ITERS):
        rates = jnp.exp(logs + table_dot(reac, jnp.log(g)))
        made_lost = table_dot(both, rates)
        g = (state + step * made_lost[:species]) / (1.0 + step * made_lost[species:] / g)
    return g


def chemistry_kernel(info, start, x, log_table, reac, both, out, result, answer, listed, sem):
    peers, blocks, group, _ = x.shape
    species = peers * group
    codes = [info[start[0] + 2 * b] for b in range(blocks)]
    count = jnp.int32(0)
    for b in range(blocks):
        listed[1, b] = lax.bitwise_and(codes[b], 3)
        listed[2, b] = lax.shift_right_logical(codes[b], 2)
        listed[0, count] = b
        count = count + lax.shift_right_logical(codes[b], 2)

    def tile(chosen, first):
        states, logs, lengths = [], [], []
        for b in chosen:
            if first:
                states.append(jnp.maximum(x[:, b].reshape(species, LANES), FLOOR))
                length = jnp.where(listed[2, b] > 0, 1.0 / SUB, 1.0)
            else:
                states.append(result[b])
                length = 1.0 / SUB
            lengths.append(jnp.full((1, LANES), length, f32))
            logs.append(log_table[listed[1, b]])
        g = euler(
            jnp.concatenate(states, axis=1),
            jnp.concatenate(logs, axis=1),
            jnp.concatenate(lengths, axis=1),
            reac[...],
            both[...],
        )
        for i, b in enumerate(chosen):
            piece = g[:, i * LANES : (i + 1) * LANES]
            result[b] = piece
            for k in range(0, species, 8):
                answer[pl.ds(k * blocks + b, 8, stride=blocks), :] = piece[k : k + 8]

    @pl.loop(0, blocks // TILE)
    def _(i):
        tile([i * TILE + j for j in range(TILE)], True)

    for _ in range(SUB - 1):

        @pl.loop(0, (count + TILE - 1) // TILE)
        def _(i):
            tile([listed[0, jnp.minimum(i * TILE + j, count - 1)] for j in range(TILE)], False)


    copy = pltpu.make_async_copy(answer, out, sem)
    copy.start()
    copy.wait()


def chemistry(x, info, start, log_table, reac, both):
    peers, blocks, group, _ = x.shape
    species = peers * group
    vmem = pl.BlockSpec(memory_space=pltpu.VMEM)
    smem = pl.BlockSpec(memory_space=pltpu.SMEM)
    return pl.pallas_call(
        chemistry_kernel,
        out_shape=jax.ShapeDtypeStruct((species * blocks, LANES), f32),
        in_specs=[smem, smem, vmem, vmem, vmem, vmem],
        out_specs=pl.BlockSpec(memory_space=pltpu.HBM),
        scratch_shapes=[
            pltpu.VMEM((blocks, species, LANES), f32),
            pltpu.VMEM((species * blocks, LANES), f32),
            pltpu.SMEM((3, blocks), jnp.int32),
            pltpu.SemaphoreType.DMA,
        ],
        compiler_params=pltpu.CompilerParams(vmem_limit_bytes=20 << 20),
        name="chemistry",
    )(info, start, x, log_table, reac, both)


def per_device(
    concentrations,
    diffusion,
    courant_x,
    courant_y,
    log_rate,
    reactants,
    products,
    block_class,
    send_slot,
):
    group, rows, columns = concentrations.shape
    species, reactions = reactants.shape
    peers = species // group
    regions = lax.axis_size("region")
    up = [(i, (i + 1) % regions) for i in range(regions - 1)]
    down = [(j, i) for i, j in up]
    hbm = pl.BlockSpec(memory_space=pltpu.HBM)
    smem = pl.BlockSpec(memory_space=pltpu.SMEM)
    places = rows // (2 * EDGE)
    part = jax.ShapeDtypeStruct((places, 2, EDGE, group, LANES), f32)

    def buffers(slab_rows):
        row_buffer = pltpu.VMEM((slab_rows, group, columns), f32)
        return [pltpu.VMEM((10, slab_rows, LANES), f32), row_buffer, row_buffer]

    code = block_class + 4 * (send_slot >= 0).astype(jnp.int32)
    info = lax.all_gather(code, "species", tiled=True)

    slab_rows = rows // 2 + 2 * EDGE
    middle = pl.pallas_call(
        middle_kernel,
        out_shape=part,
        in_specs=[smem, hbm, hbm, hbm],
        out_specs=pl.BlockSpec(memory_space=pltpu.VMEM),
        scratch_shapes=[
            pltpu.VMEM((2, group, slab_rows, LANES), f32),
            pltpu.VMEM((slab_rows, columns), f32),
            pltpu.VMEM((slab_rows, columns), f32),
            *buffers(slab_rows),
            pltpu.SemaphoreType.DMA((4,)),
        ],
        compiler_params=pltpu.CompilerParams(vmem_limit_bytes=16 << 20),
        name="middle",
    )(diffusion, concentrations, courant_x, courant_y)

    winds = jnp.stack([courant_x, courant_y])
    last = jnp.concatenate([concentrations[:, rows - EDGE :], winds[:, rows - EDGE :]], axis=0)
    leading = jnp.concatenate([concentrations[:, :EDGE], winds[:, :EDGE]], axis=0)
    before = lax.ppermute(last, "region", up)
    after = lax.ppermute(leading, "region", down)
    place = jnp.stack([lax.axis_index("region"), jnp.int32(regions)]).astype(jnp.int32)
    slab_rows = rows // 4 + 2 * EDGE
    edges = pl.pallas_call(
        edge_kernel,
        out_shape=part,
        in_specs=[smem, smem, hbm, hbm, hbm, hbm, hbm],
        out_specs=pl.BlockSpec(memory_space=pltpu.VMEM),
        scratch_shapes=[
            pltpu.VMEM((2, 2, group, slab_rows, LANES), f32),
            pltpu.VMEM((2, slab_rows, columns), f32),
            pltpu.VMEM((2, slab_rows, columns), f32),
            *buffers(slab_rows),
            pltpu.SemaphoreType.DMA((16,)),
        ],
        compiler_params=pltpu.CompilerParams(vmem_limit_bytes=16 << 20),
        name="edges",
    )(diffusion, place, concentrations, courant_x, courant_y, before, after)

    reac = reactants.T.astype(bf16)
    both = jnp.concatenate([products.T, reactants], axis=0).astype(bf16)
    log_table = jnp.broadcast_to(log_rate[:, :, None], log_rate.shape + (LANES,))
    mine = lax.axis_index("species").astype(jnp.int32)
    lower, parity = mine // 2, mine % 2
    done = []
    for slab, source in (
        (middle, lower + peers // 4),
        (edges, lower + jnp.where(lower < peers // 4, 0, peers // 2)),
    ):
        gathered = lax.all_to_all(
            slab.reshape(peers, EDGE, group, LANES), "species", split_axis=0, concat_axis=0, tiled=True
        )
        start = (source * 2 * EDGE + parity).reshape(1)
        reacted = chemistry(gathered, info, start, log_table, reac, both)
        done.append(
            lax.all_to_all(
                reacted.reshape(peers, group, EDGE, LANES),
                "species",
                split_axis=0,
                concat_axis=0,
                tiled=True,
            )
        )
    tiles = [v.reshape(places, 2, group, EDGE, LANES) for v in done]
    whole = jnp.concatenate([tiles[1][: places // 2], tiles[0], tiles[1][places // 2 :]], axis=0)
    return whole.transpose(2, 0, 3, 1, 4).reshape(group, rows, columns)


def solution(mesh):
    in_specs = (
        P("species", "region", None),
        P("species"),
        P("region", None),
        P("region", None),
        P(),
        P(),
        P(),
        P(("region", "species")),
        P(("region", "species")),
    )
    out_specs = P("species", "region", None)
    return jax.shard_map(
        per_device, mesh=mesh, in_specs=in_specs, out_specs=out_specs, check_vma=False
    )
```

time: 145 us -> 135 us (0.931); the launches traced: 144 us -> 136 us
  blocking collectives: 46.9 us -> 23 us
  Pallas kernels: 54.2 us -> 34.3 us
  waiting for transfers between devices: 15.3 us -> 34.1 us
  starting transfers between devices: 10.8 us -> 26.6 us
  local copies, waits for them, and re-layouts: 12.5 us -> 14.3 us
  other arithmetic: 4.19 us -> 2.66 us
    all_to_all x2 -> x0, blocking collectives: 46.9 us -> none  [the longest x1 26.3 us: per_device(): lax.all_to_all(part, 'species', split_axis=0, concat_axis=0, tiled=True)]
    unnamed x0 -> x1, blocking collectives: none -> 23 us
    pallas_call x2, Pallas kernels: 36.9 us -> 16.9 us  [the longest x1 8.63 us: per_device(): pl.pallas_call(edge_kernel, out_shape=part, in_specs=[smem, smem, hbm, hb...]
    all_to_all x2 -> x4, waiting for transfers between devices: 15.3 us -> 33.2 us  [the longest x2 23.8 us: per_device(): lax.all_to_all(reacted.reshape(peers, group, EDGE, LANES), 'species', spl...]
    all_to_all x2 -> x4, starting transfers between devices: 8.23 us -> 22.3 us  [the longest x2 12.6 us: per_device(): lax.all_to_all(slab.reshape(peers, EDGE, group, LANES), 'species', split_...]
    ppermute x1, starting transfers between devices: 1.3 us -> 3.04 us  [per_device(): before = lax.ppermute(last, 'region', up)]
    unnamed x35 -> x45, local copies, waits for them, and re-layouts: 9.04 us -> 10.6 us
  transfers between devices with their start and end apart: 4 -> 6, of which waited for: 2 -> 4; matrix products, arithmetic and copies ran while one was open for 2% -> 3% of each run, Pallas kernels for 32% -> 19%
where the time goes in v1:
time: 135 us; the launch traced here: 136 us
  Pallas kernels  34.3 us (25%)
  waiting for transfers between devices  34.1 us (25%)
  starting transfers between devices  26.6 us (20%)
  blocking collectives  23 us (17%)
  local copies, waits for them, and re-layouts  14.3 us (11%)
  other arithmetic  2.66 us (2%)
    all_to_all x2, waiting for transfers between devices, per_device(): lax.all_to_all(reacted.reshape(peers, group, EDGE, LANES), 'species', spl...  23.8 us
    unnamed x1, blocking collectives  23 us
    pallas_call x2, Pallas kernels, chemistry(): pl.pallas_call(chemistry_kernel, out_shape=jax.ShapeDtypeStruct((species...  17.4 us
    all_to_all x2, starting transfers between devices, per_device(): lax.all_to_all(slab.reshape(peers, EDGE, group, LANES), 'species', split_...  12.6 us
    unnamed x45, local copies, waits for them, and re-layouts  10.6 us
    all_to_all x2, starting transfers between devices, per_device(): lax.all_to_all(reacted.reshape(peers, group, EDGE, LANES), 'species', spl...  9.74 us
    all_to_all x2, waiting for transfers between devices, per_device(): lax.all_to_all(slab.reshape(peers, EDGE, group, LANES), 'species', split_...  9.4 us
    pallas_call x1, Pallas kernels, per_device(): pl.pallas_call(edge_kernel, out_shape=part, in_specs=[smem, smem, hbm, hb...  8.63 us
  transfers between devices with their start and end apart: 6, of which 4 were waited for; matrix products, arithmetic and copies ran while one was open for 3% of the time, Pallas kernels for 19%

profile of v1, /device:TPU:0, one launch (start us, length us, event | category | flops | bytes accessed | tf_op | source)
XLA Modules:
  0.0 135.9 jit_solution(11676337308326732800)
XLA Ops:
  0.0 1.0 fusion.4
  1.8 1.3 collective-permute-start.1
  3.1 3.0 %collective-permute-start = (f32[18,8,256]{2,1,0:T(8,128)S(1)}, f32[18,8,256]{2,1,0:T(8,128)S(1)}, u32[]{:S(2)}, u32[]{:S(2)}) collective-permute-start(f32[18,8,256]{2,1,0:T(8,128)S(1)} %get-tuple-element.10), channel_id=1, source_target_pairs={{0,16},{16,32},{32,48},{48,64},{64,80},{80,96},{96,112},{1,17},{17... | collective-permute-start | bytes 442376 | tf_op jit(solution)/shard_map/ppermute | solution.py:393
  7.1 1.6 %copy-done = f32[16,128,256]{2,1,0:T(8,128)S(1)} copy-done((f32[16,128,256]{2,1,0:T(8,128)S(1)}, f32[16,128,256]{2,1,0:T(8,128)}, u32[]{:S(2)}) %copy-start) | copy-done | bytes 2097176
  11.2 8.6 %edges.1 = f32[8,2,8,16,128]{4,3,2,1,0:T(8,128)S(1)} custom-call(f32[16]{0:T(128)S(1)} %copy-done.13, s32[2]{0:T(128)S(1)} %pad_add_fusion.place, f32[16,128,256]{2,1,0:T(8,128)S(1)} %copy-done, f32[128,256]{1,0:T(8,128)S(1)} %copy-done.9, f32[128,256]{1,0:T(8,128)S(1)} %copy-done.11, f32[18,8,256]{2,1,0:T(8,128)S(1)} %collective-permute-done.before, ...), custom_call_target="tpu_custom_call" | custom-call | tf_op jit(solution)/shard_map/edges/pallas_call | solution.py:397
  19.8 1.0 copy-done.6
  20.8 8.1 %all-to-all-start = ((f32[16,8,16,128]{3,2,1,0:T(8,128)}), f32[16,8,16,128]{3,2,1,0:T(8,128)S(1)}, u32[]{:S(2)}, u32[]{:S(2)}) async-start(f32[16,8,16,128]{3,2,1,0:T(8,128)} %bitcast.23), calls=%async_computation | async-start | bytes 2097152 | tf_op jit(solution)/shard_map/all_to_all | solution.py:423
  28.9 8.3 %middle.1 = f32[8,2,8,16,128]{4,3,2,1,0:T(8,128)} custom-call(f32[16]{0:T(128)S(1)} %copy-done.14, f32[16,128,256]{2,1,0:T(8,128)S(1)} %copy-done.1, f32[128,256]{1,0:T(8,128)S(1)} %copy-done.10, f32[128,256]{1,0:T(8,128)S(1)} %copy-done.12), custom_call_target="tpu_custom_call" | custom-call | tf_op jit(solution)/shard_map/middle/pallas_call | solution.py:374
  37.2 9.4 %all-to-all-done.x = f32[16,8,16,128]{3,2,1,0:T(8,128)S(1)} async-done(((f32[16,8,16,128]{3,2,1,0:T(8,128)}), f32[16,8,16,128]{3,2,1,0:T(8,128)S(1)}, u32[]{:S(2)}, u32[]{:S(2)}) %all-to-all-start) | async-done | bytes 1048608 | tf_op jit(solution)/shard_map/all_to_all | solution.py:423
  46.6 1.0 copy-done.2
  47.6 4.4 %all-to-all-start.2 = ((f32[16,8,16,128]{3,2,1,0:T(8,128)}), f32[16,8,16,128]{3,2,1,0:T(8,128)S(1)}, u32[]{:S(2)}, u32[]{:S(2)}) async-start(f32[16,8,16,128]{3,2,1,0:T(8,128)} %bitcast.11), calls=%async_computation.2 | async-start | bytes 2097152 | tf_op jit(solution)/shard_map/all_to_all | solution.py:423
  52.2 0.9 copy.11.reac
  54.9 23.0 %all-reduce.info = s32[256]{0:T(256)S(1)} all-reduce(s32[256]{0:T(256)S(1)} %fusion.3), channel_id=1, replica_groups=mesh['region'=8,'species'=16] {'species'}, use_global_device_ids=true, to_apply=%add | all-reduce | flops 256 | bytes 2048
  79.2 7.1 %chemistry.2 = f32[2048,128]{1,0:T(8,128)S(1)} custom-call(s32[256]{0:T(256)S(1)} %all-reduce.info, s32[1]{0:T(128)} %bitcast.1.start, f32[16,8,16,128]{3,2,1,0:T(8,128)S(1)} %copy-done.3, f32[4,768,128]{2,1,0:T(8,128)S(1)} %broadcast_in_dim.2.log_table, bf16[768,256]{1,0:T(8,128)(2,1)S(1)} %copy-done.7, bf16[512,768]{1,0:T(8,128)(2,1)S(1)} %pad_maximum_fusion.1.both), custom_call_target="tpu_custom_call" | custom-call | tf_op jit(solution)/shard_map/chemistry/pallas_call | solution.py:328
  86.3 1.0 copy-done.4
  87.3 6.1 %all-to-all-start.1 = ((f32[16,16,8,128]{3,2,1,0:T(8,128)}), f32[16,16,8,128]{3,2,1,0:T(8,128)}, u32[]{:S(2)}, u32[]{:S(2)}) async-start(f32[16,16,8,128]{3,2,1,0:T(8,128)} %bitcast.21), calls=%async_computation.1 | async-start | bytes 2097152 | tf_op jit(solution)/shard_map/all_to_all | solution.py:429
  93.4 1.0 copy-done.8
  94.4 10.3 %chemistry.3 = f32[2048,128]{1,0:T(8,128)S(1)} custom-call(s32[256]{0:T(256)S(1)} %all-reduce.info, s32[1]{0:T(128)} %bitcast.10.start, f32[16,8,16,128]{3,2,1,0:T(8,128)S(1)} %all-to-all-done.2.x, f32[4,768,128]{2,1,0:T(8,128)S(1)} %broadcast_in_dim.2.log_table, bf16[768,256]{1,0:T(8,128)(2,1)S(1)} %copy-done.8, bf16[512,768]{1,0:T(8,128)(2,1)S(1)} %pad_maximum_fusion.1.both), custom_call_target="tpu_custom_call" | custom-call | tf_op jit(solution)/shard_map/chemistry/pallas_call | solution.py:328
  104.7 1.0 copy-done.5
  105.7 5.4 %all-to-all-done.1 = f32[16,16,8,128]{3,2,1,0:T(8,128)} async-done(((f32[16,16,8,128]{3,2,1,0:T(8,128)}), f32[16,16,8,128]{3,2,1,0:T(8,128)}, u32[]{:S(2)}, u32[]{:S(2)}) %all-to-all-start.1) | async-done | bytes 1048608 | tf_op jit(solution)/shard_map/all_to_all | solution.py:429
  111.0 3.7 %all-to-all-start.3 = ((f32[16,16,8,128]{3,2,1,0:T(8,128)}), f32[16,16,8,128]{3,2,1,0:T(8,128)S(1)}, u32[]{:S(2)}, u32[]{:S(2)}) async-start(f32[16,16,8,128]{3,2,1,0:T(8,128)} %bitcast.22), calls=%async_computation.3 | async-start | bytes 2097152 | tf_op jit(solution)/shard_map/all_to_all | solution.py:429
  114.7 1.3 fusion.5
  116.0 18.4 %all-to-all-done.3 = f32[16,16,8,128]{3,2,1,0:T(8,128)S(1)} async-done(((f32[16,16,8,128]{3,2,1,0:T(8,128)}), f32[16,16,8,128]{3,2,1,0:T(8,128)S(1)}, u32[]{:S(2)}, u32[]{:S(2)}) %all-to-all-start.3) | async-done | bytes 1048608 | tf_op jit(solution)/shard_map/all_to_all | solution.py:429
  134.4 1.5 %copy_bitcast_fusion = f32[16,128,256]{2,1,0:T(8,128)} fusion(f32[4,2,16,8,128]{4,3,2,1,0:T(8,128)S(1)} %bitcast.28, f32[8,2,16,8,128]{4,3,2,1,0:T(8,128)S(1)} %bitcast.26, f32[4,2,16,8,128]{4,3,2,1,0:T(8,128)S(1)} %bitcast.27), kind=kLoop, calls=%fused_computation.1 | loop fusion | flops 1048576 | bytes 4194304 | tf_op jit(solution)/shard_map/reshape | solution.py:439
  (50 shorter events, 6.7 us)
Async XLA Ops:
  1.8 4.4 %collective-permute-start.1 = (f32[18,8,256]{2,1,0:T(8,128)S(1)}, f32[18,8,256]{2,1,0:T(8,128)S(1)}, u32[]{:S(2)}, u32[]{:S(2)}) collective-permute-start(f32[18,8,256]{2,1,0:T(8,128)S(1)} %get-tuple-element.9), channel_id=1, source_target_pairs={{16,0},{32,16},{48,32},{64,48},{80,64},{96,80},{112,96},{17,1},{33... | collective-permute-start | bytes 442376 | tf_op jit(solution)/shard_map/ppermute | solution.py:394
  3.1 4.0 %collective-permute-start = (f32[18,8,256]{2,1,0:T(8,128)S(1)}, f32[18,8,256]{2,1,0:T(8,128)S(1)}, u32[]{:S(2)}, u32[]{:S(2)}) collective-permute-start(f32[18,8,256]{2,1,0:T(8,128)S(1)} %get-tuple-element.10), channel_id=1, source_target_pairs={{0,16},{16,32},{32,48},{48,64},{64,80},{80,96},{96,112},{1,17},{17... | collective-permute-start | bytes 442376 | tf_op jit(solution)/shard_map/ppermute | solution.py:393
  6.1 22.8 %copy-start.14 = (f32[16]{0:T(128)S(1)}, f32[16]{0:T(128)}, u32[]{:S(2)}) copy-start(f32[16]{0:T(128)} %diffuse.3) | copy-start | bytes 196
  7.1 1.6 %copy-start = (f32[16,128,256]{2,1,0:T(8,128)S(1)}, f32[16,128,256]{2,1,0:T(8,128)}, u32[]{:S(2)}) copy-start(f32[16,128,256]{2,1,0:T(8,128)} %conc.3) | copy-start | bytes 6291460
  11.2 17.8 %copy-start.1 = (f32[16,128,256]{2,1,0:T(8,128)S(1)}, f32[16,128,256]{2,1,0:T(8,128)}, u32[]{:S(2)}) copy-start(f32[16,128,256]{2,1,0:T(8,128)} %conc.3) | copy-start | bytes 6291460
  11.2 17.8 %copy-start.10 = (f32[128,256]{1,0:T(8,128)S(1)}, f32[128,256]{1,0:T(8,128)}, u32[]{:S(2)}) copy-start(f32[128,256]{1,0:T(8,128)} %cx.3) | copy-start | bytes 393220
  11.2 17.8 %copy-start.12 = (f32[128,256]{1,0:T(8,128)S(1)}, f32[128,256]{1,0:T(8,128)}, u32[]{:S(2)}) copy-start(f32[128,256]{1,0:T(8,128)} %cy.3) | copy-start | bytes 393220
  19.8 1.0 copy-start.6
  20.8 25.9 %all-to-all-start = ((f32[16,8,16,128]{3,2,1,0:T(8,128)}), f32[16,8,16,128]{3,2,1,0:T(8,128)S(1)}, u32[]{:S(2)}, u32[]{:S(2)}) async-start(f32[16,8,16,128]{3,2,1,0:T(8,128)} %bitcast.23), calls=%async_computation | async-start | bytes 2097152 | tf_op jit(solution)/shard_map/all_to_all | solution.py:423
  37.2 14.9 %copy-start.15 = (s32[256,768]{1,0:T(8,128)S(1)}, s32[256,768]{1,0:T(8,128)}, u32[]{:S(2)}) copy-start(s32[256,768]{1,0:T(8,128)} %param.14) | copy-start | bytes 2359300
  46.6 1.0 copy-start.2
  47.6 39.7 %all-to-all-start.2 = ((f32[16,8,16,128]{3,2,1,0:T(8,128)}), f32[16,8,16,128]{3,2,1,0:T(8,128)S(1)}, u32[]{:S(2)}, u32[]{:S(2)}) async-start(f32[16,8,16,128]{3,2,1,0:T(8,128)} %bitcast.11), calls=%async_computation.2 | async-start | bytes 2097152 | tf_op jit(solution)/shard_map/all_to_all | solution.py:423
  52.0 1.1 copy-start.16
  52.1 1.4 %copy-start.20 = (u32[128]{0:T(128)S(1)}, u32[128]{0:T(128)}, u32[]{:S(2)}) copy-start(u32[128]{0:T(128)} %constant.50) | copy-start | bytes 1540
  52.1 2.7 %copy-start.18 = (s32[16]{0:T(128)S(1)}, s32[16]{0:T(128)}, u32[]{:S(2)}) copy-start(s32[16]{0:T(128)} %param.16) | copy-start | bytes 196
  52.1 2.7 %copy-start.19 = (s32[16]{0:T(128)S(1)}, s32[16]{0:T(128)}, u32[]{:S(2)}) copy-start(s32[16]{0:T(128)} %param.17) | copy-start | bytes 196
  53.2 24.8 %copy-start.17 = (f32[4,768]{1,0:T(4,128)S(1)}, f32[4,768]{1,0:T(4,128)}, u32[]{:S(2)}) copy-start(f32[4,768]{1,0:T(4,128)} %param.13) | copy-start | bytes 36868
  77.9 1.2 copy-start.3
  77.9 1.3 copy-start.7
  86.3 1.0 copy-start.4
  87.3 23.8 %all-to-all-start.1 = ((f32[16,16,8,128]{3,2,1,0:T(8,128)}), f32[16,16,8,128]{3,2,1,0:T(8,128)}, u32[]{:S(2)}, u32[]{:S(2)}) async-start(f32[16,16,8,128]{3,2,1,0:T(8,128)} %bitcast.21), calls=%async_computation.1 | async-start | bytes 2097152 | tf_op jit(solution)/shard_map/all_to_all | solution.py:429
  93.4 1.0 copy-start.8
  104.7 1.0 copy-start.5
  111.0 23.3 %all-to-all-start.3 = ((f32[16,16,8,128]{3,2,1,0:T(8,128)}), f32[16,16,8,128]{3,2,1,0:T(8,128)S(1)}, u32[]{:S(2)}, u32[]{:S(2)}) async-start(f32[16,16,8,128]{3,2,1,0:T(8,128)} %bitcast.22), calls=%async_computation.3 | async-start | bytes 2097152 | tf_op jit(solution)/shard_map/all_to_all | solution.py:429
  (3 other events, 2.5 us)

commit v2 on v1

--- a/solution.py
+++ b/solution.py
@@ -162,17 +162,18 @@
     sweep(load2, store, coef, nu, 8, rows - 8, unrolls[2])
 
 
-def store_grouped(out, base):
+def store_grouped(out, base, group):
     def store(row, pair):
         at = row - EDGE
-        place, inner = base + lax.shift_right_logical(at, 3), lax.bitwise_and(at, 7)
-        out[place, 0, inner] = pair[0]
-        out[place, 1, inner] = pair[1]
+        place = 2 * (base + lax.shift_right_logical(at, 3))
+        line = pl.multiple_of(lax.bitwise_and(at, EDGE - 1) * group, group)
+        out[place, pl.ds(line, group), :] = pair[0]
+        out[place + 1, pl.ds(line, group), :] = pair[1]
 
     return store
 
 
-def middle_kernel(diffuse, conc, cx, cy, out, raw, wx, wy, coef, one, two, sems):
+def middle_kernel(diffuse, classes, slots, conc, cx, cy, out, raw, wx, wy, coef, one, two, sems):
     group, rows = raw.shape[1:3]
     first = conc.shape[1] // 4 - EDGE
     copies = [
@@ -187,11 +188,18 @@
     ]
     start_all(copies)
     nu = spread_species(diffuse, group)
+    lane = lax.broadcasted_iota(jnp.int32, (EDGE, LANES), 1)
+    codes = jnp.zeros((EDGE, LANES), f32)
+    for k in range(classes.shape[0]):
+        code = classes[k] + jnp.where(slots[k] >= 0, 4, 0)
+        codes = jnp.where(lane == k, code.astype(f32), codes)
+    for k in range(out.shape[0]):
+        out[k, EDGE * group :, :] = codes
     wait_all(copies[:2])
     store_coefs(wx[...], wy[...], coef)
     wait_all(copies[2:])
     three_sweeps(
-        raw_access(raw), store_grouped(out, 0), coef, nu, one, two, rows, (18, 17, 16)
+        raw_access(raw), store_grouped(out, 0, group), coef, nu, one, two, rows, (18, 17, 16)
     )
 
 
@@ -236,7 +244,7 @@
 
         three_sweeps(
             raw_access(raw.at[slab]),
-            store_grouped(out, slab * 4),
+            store_grouped(out, slab * 4, group),
             coef,
             nu,
             one,
@@ -269,9 +277,14 @@
     return g
 
 
+def first_line(block, group):
+    return block * group if isinstance(block, int) else pl.multiple_of(block * group, group)
+
+
 def chemistry_kernel(info, start, x, log_table, reac, both, out, result, answer, listed, sem):
-    peers, blocks, group, _ = x.shape
-    species = peers * group
+    peers, blocks = x.shape[0], EDGE
+    species = reac.shape[1]
+    group = species // peers
     codes = [info[start[0] + 2 * b] for b in range(blocks)]
     count = jnp.int32(0)
     for b in range(blocks):
@@ -284,7 +297,7 @@
         states, logs, lengths = [], [], []
         for b in chosen:
             if first:
-                states.append(jnp.maximum(x[:, b].reshape(species, LANES), FLOOR))
+                states.append(jnp.maximum(x[:, pl.ds(first_line(b, group), group), :].reshape(species, LANES), FLOOR))
                 length = jnp.where(listed[2, b] > 0, 1.0 / SUB, 1.0)
             else:
                 states.append(result[b])
@@ -321,13 +334,12 @@
 
 
 def chemistry(x, info, start, log_table, reac, both):
-    peers, blocks, group, _ = x.shape
-    species = peers * group
+    species, blocks = reac.shape[1], EDGE
     vmem = pl.BlockSpec(memory_space=pltpu.VMEM)
     smem = pl.BlockSpec(memory_space=pltpu.SMEM)
     return pl.pallas_call(
         chemistry_kernel,
-        out_shape=jax.ShapeDtypeStruct((species * blocks, LANES), f32),
+        out_shape=pltpu.HBM((species * blocks, LANES), f32),
         in_specs=[smem, smem, vmem, vmem, vmem, vmem],
         out_specs=pl.BlockSpec(memory_space=pltpu.HBM),
         scratch_shapes=[
@@ -337,6 +349,11 @@
             pltpu.SemaphoreType.DMA,
         ],
         compiler_params=pltpu.CompilerParams(vmem_limit_bytes=20 << 20),
+        cost_estimate=pl.CostEstimate(
+            flops=24 * species * reac.shape[0] * 2 * blocks * LANES,
+            transcendentals=4 * (species + reac.shape[0]) * blocks * LANES,
+            bytes_accessed=8 << 20,
+        ),
         name="chemistry",
     )(info, start, x, log_table, reac, both)
 
@@ -361,21 +378,23 @@
     hbm = pl.BlockSpec(memory_space=pltpu.HBM)
     smem = pl.BlockSpec(memory_space=pltpu.SMEM)
     places = rows // (2 * EDGE)
-    part = jax.ShapeDtypeStruct((places, 2, EDGE, group, LANES), f32)
+    lines = EDGE * group
 
     def buffers(slab_rows):
         row_buffer = pltpu.VMEM((slab_rows, group, columns), f32)
         return [pltpu.VMEM((10, slab_rows, LANES), f32), row_buffer, row_buffer]
 
-    code = block_class + 4 * (send_slot >= 0).astype(jnp.int32)
-    info = lax.all_gather(code, "species", tiled=True)
-
+    def in_hbm(*arrays):
+        return [pltpu.with_memory_space_constraint(v, pltpu.HBM) for v in arrays]
+
+    fields = in_hbm(concentrations, courant_x, courant_y)
     slab_rows = rows // 2 + 2 * EDGE
     middle = pl.pallas_call(
         middle_kernel,
-        out_shape=part,
-        in_specs=[smem, hbm, hbm, hbm],
-        out_specs=pl.BlockSpec(memory_space=pltpu.VMEM),
+        grid=(1,),
+        out_shape=pltpu.HBM((peers, lines + EDGE, LANES), f32),
+        in_specs=[smem, smem, smem, hbm, hbm, hbm],
+        out_specs=pl.BlockSpec((peers, lines + EDGE, LANES), lambda i: (0, 0, 0)),
         scratch_shapes=[
             pltpu.VMEM((2, group, slab_rows, LANES), f32),
             pltpu.VMEM((slab_rows, columns), f32),
@@ -385,20 +404,22 @@
         ],
         compiler_params=pltpu.CompilerParams(vmem_limit_bytes=16 << 20),
         name="middle",
-    )(diffusion, concentrations, courant_x, courant_y)
+    )(diffusion, block_class, send_slot, *fields)
 
     winds = jnp.stack([courant_x, courant_y])
     last = jnp.concatenate([concentrations[:, rows - EDGE :], winds[:, rows - EDGE :]], axis=0)
     leading = jnp.concatenate([concentrations[:, :EDGE], winds[:, :EDGE]], axis=0)
     before = lax.ppermute(last, "region", up)
     after = lax.ppermute(leading, "region", down)
+    before, after, _ = lax.optimization_barrier((before, after, middle))
     place = jnp.stack([lax.axis_index("region"), jnp.int32(regions)]).astype(jnp.int32)
     slab_rows = rows // 4 + 2 * EDGE
     edges = pl.pallas_call(
         edge_kernel,
-        out_shape=part,
+        grid=(1,),
+        out_shape=pltpu.HBM((peers, lines, LANES), f32),
         in_specs=[smem, smem, hbm, hbm, hbm, hbm, hbm],
-        out_specs=pl.BlockSpec(memory_space=pltpu.VMEM),
+        out_specs=pl.BlockSpec((peers, lines, LANES), lambda i: (0, 0, 0)),
         scratch_shapes=[
             pltpu.VMEM((2, 2, group, slab_rows, LANES), f32),
             pltpu.VMEM((2, slab_rows, columns), f32),
@@ -408,7 +429,7 @@
         ],
         compiler_params=pltpu.CompilerParams(vmem_limit_bytes=16 << 20),
         name="edges",
-    )(diffusion, place, concentrations, courant_x, courant_y, before, after)
+    )(diffusion, place, *fields, before, after)
 
     reac = reactants.T.astype(bf16)
     both = jnp.concatenate([products.T, reactants], axis=0).astype(bf16)
@@ -416,24 +437,22 @@
     mine = lax.axis_index("species").astype(jnp.int32)
     lower, parity = mine // 2, mine % 2
     done = []
+    exchange = functools.partial(
+        lax.all_to_all, axis_name="species", split_axis=0, concat_axis=0, tiled=True
+    )
+    info = None
     for slab, source in (
         (middle, lower + peers // 4),
         (edges, lower + jnp.where(lower < peers // 4, 0, peers // 2)),
     ):
-        gathered = lax.all_to_all(
-            slab.reshape(peers, EDGE, group, LANES), "species", split_axis=0, concat_axis=0, tiled=True
-        )
+        gathered = exchange(slab)
+        if info is None:
+            info = gathered[:, lines, : 2 * EDGE].astype(jnp.int32).reshape(-1)
         start = (source * 2 * EDGE + parity).reshape(1)
+        if done:
+            start, _ = lax.optimization_barrier((start, reacted))
         reacted = chemistry(gathered, info, start, log_table, reac, both)
-        done.append(
-            lax.all_to_all(
-                reacted.reshape(peers, group, EDGE, LANES),
-                "species",
-                split_axis=0,
-                concat_axis=0,
-                tiled=True,
-            )
-        )
+        done.append(exchange(reacted.reshape(peers, group, EDGE, LANES)))
     tiles = [v.reshape(places, 2, group, EDGE, LANES) for v in done]
     whole = jnp.concatenate([tiles[1][: places // 2], tiles[0], tiles[1][places // 2 :]], axis=0)
     return whole.transpose(2, 0, 3, 1, 4).reshape(group, rows, columns)

time: 135 us -> 130 us (0.963)
  the two profiles are of different devices: /device:TPU:0 before, /device:TPU:2 now
where the time goes in v2:
time: 130 us; the launch traced here: 131 us
  Pallas kernels  39.9 us (31%)
  waiting for transfers between devices  31.8 us (24%)
  starting transfers between devices  23.4 us (18%)
  blocking collectives  22.5 us (17%)
  local copies, waits for them, and re-layouts  7.95 us (6%)
  other arithmetic  5.15 us (4%)
    all_to_all x1, blocking collectives, per_device(): done.append(exchange(reacted.reshape(peers, group, EDGE, LANES)))  22.5 us
    all_to_all x1, waiting for transfers between devices, per_device(): done.append(exchange(reacted.reshape(peers, group, EDGE, LANES)))  20.7 us
    pallas_call x2, Pallas kernels, chemistry(): pl.pallas_call(chemistry_kernel, out_shape=pltpu.HBM((species * blocks, L...  20.1 us
    all_to_all x2, starting transfers between devices, per_device(): gathered = exchange(slab)  15.5 us
    all_to_all x2, waiting for transfers between devices, per_device(): gathered = exchange(slab)  11.1 us
    pallas_call x1, Pallas kernels, per_device(): pl.pallas_call(edge_kernel, grid=(1,), out_shape=pltpu.HBM((peers, lines,...  10.6 us
    pallas_call x1, Pallas kernels, per_device(): pl.pallas_call(middle_kernel, grid=(1,), out_shape=pltpu.HBM((peers, line...  9.26 us
    unnamed x21, local copies, waits for them, and re-layouts  5.38 us
  transfers between devices with their start and end apart: 5, of which 2 were waited for; matrix products, arithmetic and copies ran while one was open for 6% of the time, Pallas kernels for 14%

profile of v2, /device:TPU:2, one launch (start us, length us, event | category | flops | bytes accessed | tf_op | source)
XLA Modules:
  0.0 131.0 jit_solution(13671360094185729735)
XLA Ops:
  0.0 0.7 copy-done.2
  0.7 0.7 copy-done.4
  2.0 9.3 %middle.1 = f32[16,136,128]{2,1,0:T(8,128)} custom-call(f32[16]{0:T(128)S(1)} %copy-done.2, s32[16]{0:T(128)S(1)} %copy-done.4, s32[16]{0:T(128)S(1)} %copy-done.5, f32[16,128,256]{2,1,0:T(8,128)} %conc.3, f32[128,256]{1,0:T(8,128)} %cx.3, f32[128,256]{1,0:T(8,128)} %cy.3), custom_call_target="tpu_custom_call" | custom-call | tf_op jit(solution)/shard_map/middle/pallas_call | solution.py:392
  11.3 8.2 %all-to-all-start = ((f32[16,136,128]{2,1,0:T(8,128)}), f32[16,136,128]{2,1,0:T(8,128)S(1)}, u32[]{:S(2)}, u32[]{:S(2)}) async-start(f32[16,136,128]{2,1,0:T(8,128)} %middle.1), calls=%async_computation | async-start | bytes 2228224 | tf_op jit(solution)/shard_map/all_to_all | solution.py:448
  19.5 1.0 fusion.3
  20.5 0.7 fusion
  21.2 1.9 %collective-permute-start.1 = (f32[18,8,256]{2,1,0:T(8,128)}, f32[18,8,256]{2,1,0:T(8,128)S(1)}, u32[]{:S(2)}, u32[]{:S(2)}) collective-permute-start(f32[18,8,256]{2,1,0:T(8,128)} %get-tuple-element.15), channel_id=1, source_target_pairs={{16,0},{32,16},{48,32},{64,48},{80,64},{96,80},{112,96},{17,1},{33... | collective-permute-start | bytes 442376 | tf_op jit(solution)/shard_map/ppermute | solution.py:413
  23.1 2.4 %collective-permute-start = (f32[18,8,256]{2,1,0:T(8,128)}, f32[18,8,256]{2,1,0:T(8,128)S(1)}, u32[]{:S(2)}, u32[]{:S(2)}) collective-permute-start(f32[18,8,256]{2,1,0:T(8,128)} %get-tuple-element.16), channel_id=1, source_target_pairs={{0,16},{16,32},{32,48},{48,64},{64,80},{80,96},{96,112},{1,17},{17... | collective-permute-start | bytes 442376 | tf_op jit(solution)/shard_map/ppermute | solution.py:412
  25.6 1.4 %copy.10 = s32[768,256]{0,1:T(8,128)S(1)} copy(s32[768,256]{1,0:T(8,128)} %param.15) | data formatting | bytes 1572864 | tf_op args[6]
  27.0 0.8 convert_bitcast_fusion
  27.9 0.8 convert_element_type.15
  28.7 0.9 copy.11.reac
  29.6 1.2 pad_maximum_fusion.1.both
  30.8 10.6 %edges.1 = f32[16,128,128]{2,1,0:T(8,128)} custom-call(f32[16]{0:T(128)S(1)} %copy-done.3, s32[2]{0:T(128)S(1)} %pad_add_fusion.place, f32[16,128,256]{2,1,0:T(8,128)} %conc.3, f32[128,256]{1,0:T(8,128)} %cx.3, f32[128,256]{1,0:T(8,128)} %cy.3, f32[18,8,256]{2,1,0:T(8,128)S(1)} %collective-permute-done.before, f32[18,8,256]{2,1,0:T(8,128)S(1)} %collective-permute-done.1.after), custom_call_target="tpu_custom_call" | custom-call | tf_op jit(solution)/shard_map/edges/pallas_call | solution.py:417
  41.4 7.3 %all-to-all-start.1 = ((f32[16,128,128]{2,1,0:T(8,128)}), f32[16,128,128]{2,1,0:T(8,128)}, u32[]{:S(2)}, u32[]{:S(2)}) async-start(f32[16,128,128]{2,1,0:T(8,128)} %edges.1), calls=%async_computation.1 | async-start | bytes 2097152 | tf_op jit(solution)/shard_map/all_to_all | solution.py:448
  49.3 1.0 copy-done
  50.3 8.2 %chemistry.2 = f32[2048,128]{1,0:T(8,128)} custom-call(s32[256]{0:T(256)S(1)} %convert_element_type.14.info, s32[1]{0:T(128)} %bitcast.1.start, f32[16,136,128]{2,1,0:T(8,128)S(1)} %all-to-all-done.x, f32[4,768,128]{2,1,0:T(8,128)S(1)} %broadcast_in_dim.2.log_table, bf16[768,256]{1,0:T(8,128)(2,1)S(1)} %copy-done, bf16[512,768]{1,0:T(8,128)(2,1)S(1)} %pad_maximum_fusion.1.both), custom_call_target="tpu_custom_call" | custom-call | flops 9663676416 | bytes 8388608 | tf_op jit(solution)/shard_map/chemistry/pallas_call | solution.py:340
  58.5 11.1 %all-to-all-done.1.x = f32[16,128,128]{2,1,0:T(8,128)} async-done(((f32[16,128,128]{2,1,0:T(8,128)}), f32[16,128,128]{2,1,0:T(8,128)}, u32[]{:S(2)}, u32[]{:S(2)}) %all-to-all-start.1) | async-done | bytes 1048608 | tf_op jit(solution)/shard_map/all_to_all | solution.py:448
  69.6 1.0 copy-done.1
  70.6 11.9 %chemistry.3 = f32[2048,128]{1,0:T(8,128)} custom-call(s32[256]{0:T(256)S(1)} %convert_element_type.14.info, s32[1]{0:T(128)} %bitcast.start, f32[16,128,128]{2,1,0:T(8,128)} %all-to-all-done.1.x, f32[4,768,128]{2,1,0:T(8,128)S(1)} %broadcast_in_dim.2.log_table, bf16[768,256]{1,0:T(8,128)(2,1)S(1)} %copy-done.1, bf16[512,768]{1,0:T(8,128)(2,1)S(1)} %pad_maximum_fusion.1.both), custom_call_target="tpu_custom_call" | custom-call | flops 9663676416 | bytes 8388608 | tf_op jit(solution)/shard_map/chemistry/pallas_call | solution.py:340
  82.5 22.5 %all_to_all.20 = f32[16,16,8,128]{3,2,1,0:T(8,128)S(1)} all-to-all(f32[16,16,8,128]{3,2,1,0:T(8,128)} %bitcast.23), channel_id=1, replica_groups=mesh['region'=8,'species'=16] {'species'}, dimensions={0} | all-to-all | bytes 2097152 | tf_op jit(solution)/shard_map/all_to_all | solution.py:455
  105.0 3.7 %all-to-all-start.3 = ((f32[16,16,8,128]{3,2,1,0:T(8,128)}), f32[16,16,8,128]{3,2,1,0:T(8,128)S(1)}, u32[]{:S(2)}, u32[]{:S(2)}) async-start(f32[16,16,8,128]{3,2,1,0:T(8,128)} %bitcast.9), calls=%async_computation.3 | async-start | bytes 2097152 | tf_op jit(solution)/shard_map/all_to_all | solution.py:455
  108.8 20.7 %all-to-all-done.3 = f32[16,16,8,128]{3,2,1,0:T(8,128)S(1)} async-done(((f32[16,16,8,128]{3,2,1,0:T(8,128)}), f32[16,16,8,128]{3,2,1,0:T(8,128)S(1)}, u32[]{:S(2)}, u32[]{:S(2)}) %all-to-all-start.3) | async-done | bytes 1048608 | tf_op jit(solution)/shard_map/all_to_all | solution.py:455
  129.4 1.5 %copy_bitcast_fusion = f32[16,128,256]{2,1,0:T(8,128)} fusion(f32[4,2,16,8,128]{4,3,2,1,0:T(8,128)S(1)} %bitcast.20, f32[8,2,16,8,128]{4,3,2,1,0:T(8,128)S(1)} %bitcast.18, f32[4,2,16,8,128]{4,3,2,1,0:T(8,128)S(1)} %bitcast.19), kind=kLoop, calls=%fused_computation.1 | loop fusion | flops 1048576 | bytes 4194304 | tf_op jit(solution)/shard_map/reshape | solution.py:458
  (25 shorter events, 1.5 us)
Async XLA Ops:
  0.0 0.7 copy-start.2
  0.7 0.7 copy-start.4
  1.3 0.7 copy-start.5
  11.2 9.2 %copy-start.7 = (f32[128,256]{1,0:T(8,128)S(1)}, f32[128,256]{1,0:T(8,128)}, u32[]{:S(2)}) copy-start(f32[128,256]{1,0:T(8,128)} %cx.3) | copy-start | bytes 393220
  11.2 9.2 %copy-start.8 = (f32[128,256]{1,0:T(8,128)S(1)}, f32[128,256]{1,0:T(8,128)}, u32[]{:S(2)}) copy-start(f32[128,256]{1,0:T(8,128)} %cy.3) | copy-start | bytes 393220
  11.3 15.7 %copy-start.6 = (s32[256,768]{1,0:T(8,128)S(1)}, s32[256,768]{1,0:T(8,128)}, u32[]{:S(2)}) copy-start(s32[256,768]{1,0:T(8,128)} %param.14) | copy-start | bytes 2359300
  11.3 30.1 %all-to-all-start = ((f32[16,136,128]{2,1,0:T(8,128)}), f32[16,136,128]{2,1,0:T(8,128)S(1)}, u32[]{:S(2)}, u32[]{:S(2)}) async-start(f32[16,136,128]{2,1,0:T(8,128)} %middle.1), calls=%async_computation | async-start | bytes 2228224 | tf_op jit(solution)/shard_map/all_to_all | solution.py:448
  21.2 9.6 %collective-permute-start.1 = (f32[18,8,256]{2,1,0:T(8,128)}, f32[18,8,256]{2,1,0:T(8,128)S(1)}, u32[]{:S(2)}, u32[]{:S(2)}) collective-permute-start(f32[18,8,256]{2,1,0:T(8,128)} %get-tuple-element.15), channel_id=1, source_target_pairs={{16,0},{32,16},{48,32},{64,48},{80,64},{96,80},{112,96},{17,1},{33... | collective-permute-start | bytes 442376 | tf_op jit(solution)/shard_map/ppermute | solution.py:413
  23.1 7.7 %collective-permute-start = (f32[18,8,256]{2,1,0:T(8,128)}, f32[18,8,256]{2,1,0:T(8,128)S(1)}, u32[]{:S(2)}, u32[]{:S(2)}) collective-permute-start(f32[18,8,256]{2,1,0:T(8,128)} %get-tuple-element.16), channel_id=1, source_target_pairs={{0,16},{16,32},{32,48},{48,64},{64,80},{80,96},{96,112},{1,17},{17... | collective-permute-start | bytes 442376 | tf_op jit(solution)/shard_map/ppermute | solution.py:412
  27.0 3.8 %copy-start.3 = (f32[16]{0:T(128)S(1)}, f32[16]{0:T(128)}, u32[]{:S(2)}) copy-start(f32[16]{0:T(128)} %diffuse.3) | copy-start | bytes 196
  30.8 18.0 %copy-start.9 = (f32[4,768]{1,0:T(4,128)S(1)}, f32[4,768]{1,0:T(4,128)}, u32[]{:S(2)}) copy-start(f32[4,768]{1,0:T(4,128)} %param.13) | copy-start | bytes 36868
  41.4 28.2 %all-to-all-start.1 = ((f32[16,128,128]{2,1,0:T(8,128)}), f32[16,128,128]{2,1,0:T(8,128)}, u32[]{:S(2)}, u32[]{:S(2)}) async-start(f32[16,128,128]{2,1,0:T(8,128)} %edges.1), calls=%async_computation.1 | async-start | bytes 2097152 | tf_op jit(solution)/shard_map/all_to_all | solution.py:448
  49.3 1.0 copy-start
  69.6 1.0 copy-start.1
  105.0 24.4 %all-to-all-start.3 = ((f32[16,16,8,128]{3,2,1,0:T(8,128)}), f32[16,16,8,128]{3,2,1,0:T(8,128)S(1)}, u32[]{:S(2)}, u32[]{:S(2)}) async-start(f32[16,16,8,128]{3,2,1,0:T(8,128)} %bitcast.9), calls=%async_computation.3 | async-start | bytes 2097152 | tf_op jit(solution)/shard_map/all_to_all | solution.py:455

commit v3 on v2

--- a/solution.py
+++ b/solution.py
@@ -173,20 +173,42 @@
     return store
 
 
-def middle_kernel(diffuse, classes, slots, conc, cx, cy, out, raw, wx, wy, coef, one, two, sems):
+def middle_kernel(
+    diffuse_in,
+    classes_in,
+    slots_in,
+    conc,
+    cx,
+    cy,
+    out,
+    last,
+    leading,
+    diffuse,
+    classes,
+    slots,
+    raw,
+    wx,
+    wy,
+    coef,
+    one,
+    two,
+    sems,
+):
     group, rows = raw.shape[1:3]
-    first = conc.shape[1] // 4 - EDGE
-    copies = [
-        pltpu.make_async_copy(src.at[pl.ds(first, rows)], dst, sems.at[k])
-        for k, (src, dst) in enumerate(((cx, wx), (cy, wy)))
+    total = conc.shape[1]
+    first = total // 4 - EDGE
+    pairs = [(cx.at[pl.ds(first, rows)], wx), (cy.at[pl.ds(first, rows)], wy)]
+    pairs += [
+        (conc.at[:, pl.ds(first, rows), pl.ds(k * LANES, LANES)], raw.at[k]) for k in (0, 1)
     ]
-    copies += [
-        pltpu.make_async_copy(
-            conc.at[:, pl.ds(first, rows), pl.ds(k * LANES, LANES)], raw.at[k], sems.at[2 + k]
-        )
-        for k in (0, 1)
-    ]
+    pairs += [(diffuse_in, diffuse), (classes_in, classes), (slots_in, slots)]
+    for rim, at in ((last, total - EDGE), (leading, 0)):
+        pairs.append((conc.at[:, pl.ds(at, EDGE)], rim.at[pl.ds(0, group)]))
+        pairs.append((cx.at[pl.ds(at, EDGE)], rim.at[group]))
+        pairs.append((cy.at[pl.ds(at, EDGE)], rim.at[group + 1]))
+    copies = [pltpu.make_async_copy(*pair, sems.at[k]) for k, pair in enumerate(pairs)]
     start_all(copies)
+    wait_all(copies[4:7])
     nu = spread_species(diffuse, group)
     lane = lax.broadcasted_iota(jnp.int32, (EDGE, LANES), 1)
     codes = jnp.zeros((EDGE, LANES), f32)
@@ -197,14 +219,15 @@
         out[k, EDGE * group :, :] = codes
     wait_all(copies[:2])
     store_coefs(wx[...], wy[...], coef)
-    wait_all(copies[2:])
+    wait_all(copies[2:4])
     three_sweeps(
         raw_access(raw), store_grouped(out, 0, group), coef, nu, one, two, rows, (18, 17, 16)
     )
+    wait_all(copies[7:])
 
 
 def edge_kernel(
-    diffuse, place, conc, cx, cy, before, after, out, raw, wx, wy, coef, one, two, sems
+    place, diffuse_in, conc, cx, cy, before, after, out, diffuse, raw, wx, wy, coef, one, two, sems
 ):
     group, rows = raw.shape[2:4]
     total = conc.shape[1]
@@ -214,6 +237,7 @@
     def copy(src, dst):
         copies.append(pltpu.make_async_copy(src, dst, sems.at[len(copies)]))
 
+    copy(diffuse_in, diffuse)
     for slab, halo, own_first, own_at, halo_at in (
         (0, before, 0, EDGE, 0),
         (1, after, total - own, 0, own),
@@ -227,8 +251,8 @@
             copy(conc.at[:, pl.ds(own_first, own), lanes], dst.at[:, pl.ds(own_at, own)])
             copy(halo.at[pl.ds(0, group), :, lanes], dst.at[:, pl.ds(halo_at, EDGE)])
     start_all(copies)
+    wait_all(copies)
     nu = spread_species(diffuse, group)
-    wait_all(copies)
 
     @pl.loop(0, 2)
     def _(slab):
@@ -279,6 +303,33 @@
 
 def first_line(block, group):
     return block * group if isinstance(block, int) else pl.multiple_of(block * group, group)
+
+
+def table_kernel(log_rate, reactants, products, log_table, reac, both):
+    species, reactions = reactants.shape
+    reactant = reactants[...].astype(f32)
+    reac[...] = reactant.T.astype(bf16)
+    both[:species] = products[...].astype(f32).T.astype(bf16)
+    both[species:] = reactant.astype(bf16)
+    for k in range(log_rate.shape[0]):
+        log_table[k] = jnp.broadcast_to(log_rate[k : k + 1, :], (LANES, reactions)).T
+
+
+def tables_of(log_rate, reactants, products):
+    species, reactions = reactants.shape
+    vmem = pl.BlockSpec(memory_space=pltpu.VMEM)
+    return pl.pallas_call(
+        table_kernel,
+        out_shape=[
+            jax.ShapeDtypeStruct((log_rate.shape[0], reactions, LANES), f32),
+            jax.ShapeDtypeStruct((reactions, species), bf16),
+            jax.ShapeDtypeStruct((2 * species, reactions), bf16),
+        ],
+        in_specs=[vmem] * 3,
+        out_specs=[vmem] * 3,
+        compiler_params=pltpu.CompilerParams(vmem_limit_bytes=20 << 20),
+        name="tables",
+    )(log_rate, reactants, products)
 
 
 def chemistry_kernel(info, start, x, log_table, reac, both, out, result, answer, listed, sem):
@@ -349,13 +400,37 @@
             pltpu.SemaphoreType.DMA,
         ],
         compiler_params=pltpu.CompilerParams(vmem_limit_bytes=20 << 20),
-        cost_estimate=pl.CostEstimate(
-            flops=24 * species * reac.shape[0] * 2 * blocks * LANES,
-            transcendentals=4 * (species + reac.shape[0]) * blocks * LANES,
-            bytes_accessed=8 << 20,
-        ),
         name="chemistry",
     )(info, start, x, log_table, reac, both)
+
+
+def place_kernel(groups, parts, *rest):
+    whole, sems = rest[-2:]
+    copies = [
+        pltpu.make_async_copy(
+            parts.at[2 * k + side],
+            whole.at[:, pl.ds(at * EDGE, EDGE), pl.ds(side * LANES, LANES)],
+            sems.at[2 * k + side],
+        )
+        for k, at in enumerate(groups)
+        for side in (0, 1)
+    ]
+    start_all(copies)
+    wait_all(copies)
+
+
+def place_rows(parts, groups, rows, *whole):
+    peers, group = parts.shape[:2]
+    hbm = pl.BlockSpec(memory_space=pltpu.HBM)
+    return pl.pallas_call(
+        functools.partial(place_kernel, groups),
+        out_shape=pltpu.HBM((group, rows, 2 * LANES), f32),
+        in_specs=[pl.BlockSpec(memory_space=pltpu.VMEM)] + [hbm] * len(whole),
+        out_specs=hbm,
+        scratch_shapes=[pltpu.SemaphoreType.DMA((peers,))],
+        input_output_aliases={1: 0} if whole else {},
+        name="place",
+    )(parts, *whole)
 
 
 def per_device(
@@ -377,6 +452,7 @@
     down = [(j, i) for i, j in up]
     hbm = pl.BlockSpec(memory_space=pltpu.HBM)
     smem = pl.BlockSpec(memory_space=pltpu.SMEM)
+    vmem = pl.BlockSpec(memory_space=pltpu.VMEM)
     places = rows // (2 * EDGE)
     lines = EDGE * group
 
@@ -389,51 +465,50 @@
 
     fields = in_hbm(concentrations, courant_x, courant_y)
     slab_rows = rows // 2 + 2 * EDGE
-    middle = pl.pallas_call(
+    rim = pltpu.HBM((group + 2, EDGE, columns), f32)
+    middle, last, leading = pl.pallas_call(
         middle_kernel,
         grid=(1,),
-        out_shape=pltpu.HBM((peers, lines + EDGE, LANES), f32),
-        in_specs=[smem, smem, smem, hbm, hbm, hbm],
-        out_specs=pl.BlockSpec((peers, lines + EDGE, LANES), lambda i: (0, 0, 0)),
+        out_shape=(pltpu.HBM((peers, lines + EDGE, LANES), f32), rim, rim),
+        in_specs=[hbm] * 6,
+        out_specs=(pl.BlockSpec((peers, lines + EDGE, LANES), lambda i: (0, 0, 0)), hbm, hbm),
         scratch_shapes=[
+            pltpu.SMEM((group,), f32),
+            pltpu.SMEM((2 * EDGE,), jnp.int32),
+            pltpu.SMEM((2 * EDGE,), jnp.int32),
             pltpu.VMEM((2, group, slab_rows, LANES), f32),
             pltpu.VMEM((slab_rows, columns), f32),
             pltpu.VMEM((slab_rows, columns), f32),
             *buffers(slab_rows),
-            pltpu.SemaphoreType.DMA((4,)),
+            pltpu.SemaphoreType.DMA((13,)),
         ],
         compiler_params=pltpu.CompilerParams(vmem_limit_bytes=16 << 20),
         name="middle",
-    )(diffusion, block_class, send_slot, *fields)
-
-    winds = jnp.stack([courant_x, courant_y])
-    last = jnp.concatenate([concentrations[:, rows - EDGE :], winds[:, rows - EDGE :]], axis=0)
-    leading = jnp.concatenate([concentrations[:, :EDGE], winds[:, :EDGE]], axis=0)
+    )(*in_hbm(diffusion, block_class, send_slot), *fields)
+
     before = lax.ppermute(last, "region", up)
     after = lax.ppermute(leading, "region", down)
-    before, after, _ = lax.optimization_barrier((before, after, middle))
     place = jnp.stack([lax.axis_index("region"), jnp.int32(regions)]).astype(jnp.int32)
     slab_rows = rows // 4 + 2 * EDGE
     edges = pl.pallas_call(
         edge_kernel,
         grid=(1,),
         out_shape=pltpu.HBM((peers, lines, LANES), f32),
-        in_specs=[smem, smem, hbm, hbm, hbm, hbm, hbm],
+        in_specs=[smem] + [hbm] * 4 + [vmem] * 2,
         out_specs=pl.BlockSpec((peers, lines, LANES), lambda i: (0, 0, 0)),
         scratch_shapes=[
+            pltpu.SMEM((group,), f32),
             pltpu.VMEM((2, 2, group, slab_rows, LANES), f32),
             pltpu.VMEM((2, slab_rows, columns), f32),
             pltpu.VMEM((2, slab_rows, columns), f32),
             *buffers(slab_rows),
-            pltpu.SemaphoreType.DMA((16,)),
+            pltpu.SemaphoreType.DMA((17,)),
         ],
         compiler_params=pltpu.CompilerParams(vmem_limit_bytes=16 << 20),
         name="edges",
-    )(diffusion, place, *fields, before, after)
-
-    reac = reactants.T.astype(bf16)
-    both = jnp.concatenate([products.T, reactants], axis=0).astype(bf16)
-    log_table = jnp.broadcast_to(log_rate[:, :, None], log_rate.shape + (LANES,))
+    )(place, *in_hbm(diffusion), *fields, before, after)
+
+    tables = tables_of(log_rate, reactants, products)
     mine = lax.axis_index("species").astype(jnp.int32)
     lower, parity = mine // 2, mine % 2
     done = []
@@ -449,13 +524,12 @@
         if info is None:
             info = gathered[:, lines, : 2 * EDGE].astype(jnp.int32).reshape(-1)
         start = (source * 2 * EDGE + parity).reshape(1)
-        if done:
-            start, _ = lax.optimization_barrier((start, reacted))
-        reacted = chemistry(gathered, info, start, log_table, reac, both)
+        reacted = chemistry(gathered, info, start, *tables)
         done.append(exchange(reacted.reshape(peers, group, EDGE, LANES)))
-    tiles = [v.reshape(places, 2, group, EDGE, LANES) for v in done]
-    whole = jnp.concatenate([tiles[1][: places // 2], tiles[0], tiles[1][places // 2 :]], axis=0)
-    return whole.transpose(2, 0, 3, 1, 4).reshape(group, rows, columns)
+    quarter = places // 2
+    filled = place_rows(done[0], range(quarter, 3 * quarter), rows)
+    sides = (*range(quarter), *range(3 * quarter, 4 * quarter))
+    return place_rows(done[1], sides, rows, filled)
 
 
 def solution(mesh):

time: 130 us -> 116 us (0.89)
  the two profiles are of different devices: /device:TPU:2 before, /device:TPU:0 now
where the time goes in v3:
time: 116 us; the launch traced here: 115 us
  Pallas kernels  50.7 us (44%)
  waiting for transfers between devices  32.7 us (28%)
  starting transfers between devices  26.3 us (23%)
  local copies, waits for them, and re-layouts  5.08 us (4%)
    all_to_all x2, waiting for transfers between devices, per_device(): done.append(exchange(reacted.reshape(peers, group, EDGE, LANES)))  27.8 us
    pallas_call x2, Pallas kernels, chemistry(): pl.pallas_call(chemistry_kernel, out_shape=pltpu.HBM((species * blocks, L...  23.7 us
    all_to_all x2, starting transfers between devices, per_device(): gathered = exchange(slab)  14.1 us
    pallas_call x1, Pallas kernels, per_device(): pl.pallas_call(middle_kernel, grid=(1,), out_shape=(pltpu.HBM((peers, lin...  11.1 us
    pallas_call x1, Pallas kernels, per_device(): pl.pallas_call(edge_kernel, grid=(1,), out_shape=pltpu.HBM((peers, lines,...  10.6 us
    all_to_all x2, starting transfers between devices, per_device(): done.append(exchange(reacted.reshape(peers, group, EDGE, LANES)))  9.49 us
    unnamed x18, local copies, waits for them, and re-layouts  5 us
    pallas_call x2, Pallas kernels, place_rows(): pl.pallas_call(functools.partial(place_kernel, groups), out_shape=pltpu.H...  4.62 us
  transfers between devices with their start and end apart: 6, of which 4 were waited for; matrix products, arithmetic and copies ran while one was open for 0% of the time, Pallas kernels for 32%

profile of v3, /device:TPU:0, one launch (start us, length us, event | category | flops | bytes accessed | tf_op | source)
XLA Modules:
  0.0 115.4 jit_solution(18133492809826812031)
XLA Ops:
  0.0 11.1 %middle.1 = (f32[16,136,128]{2,1,0:T(8,128)}, f32[18,8,256]{2,1,0:T(8,128)}, f32[18,8,256]{2,1,0:T(8,128)}) custom-call(f32[16]{0:T(128)} %diffuse_in.3, s32[16]{0:T(128)} %classes_in.1, s32[16]{0:T(128)} %slots_in.1, f32[16,128,256]{2,1,0:T(8,128)} %conc.3, f32[128,256]{1,0:T(8,128)} %cx.3, f32[128,256]{1,0:T(8,128)} %cy.3), custom_call_target="tpu_custom_call" | custom-call | tf_op jit(solution)/shard_map/middle/pallas_call | solution.py:469
  11.2 8.3 %all-to-all-start = ((f32[16,136,128]{2,1,0:T(8,128)}), f32[16,136,128]{2,1,0:T(8,128)S(1)}, u32[]{:S(2)}, u32[]{:S(2)}) async-start(f32[16,136,128]{2,1,0:T(8,128)} %get-tuple-element.11), calls=%async_computation | async-start | bytes 2228224 | tf_op jit(solution)/shard_map/all_to_all | solution.py:523
  19.5 1.5 %collective-permute-start = (f32[18,8,256]{2,1,0:T(8,128)S(1)}, f32[18,8,256]{2,1,0:T(8,128)S(1)}, u32[]{:S(2)}, u32[]{:S(2)}) collective-permute-start(f32[18,8,256]{2,1,0:T(8,128)S(1)} %copy-done.8), channel_id=1, source_target_pairs={{0,16},{16,32},{32,48},{48,64},{64,80},{80,96},{96,112},{1,17},{17... | collective-permute-start | bytes 442376 | tf_op jit(solution)/shard_map/ppermute | solution.py:489
  21.0 1.3 %collective-permute-start.1 = (f32[18,8,256]{2,1,0:T(8,128)S(1)}, f32[18,8,256]{2,1,0:T(8,128)S(1)}, u32[]{:S(2)}, u32[]{:S(2)}) collective-permute-start(f32[18,8,256]{2,1,0:T(8,128)S(1)} %copy-done.7), channel_id=1, source_target_pairs={{16,0},{32,16},{48,32},{64,48},{80,64},{96,80},{112,96},{17,1},{33... | collective-permute-start | bytes 442376 | tf_op jit(solution)/shard_map/ppermute | solution.py:490
  22.3 0.1 pad_add_fusion.place
  22.3 3.4 %collective-permute-done.1.after = f32[18,8,256]{2,1,0:T(8,128)S(1)} collective-permute-done((f32[18,8,256]{2,1,0:T(8,128)S(1)}, f32[18,8,256]{2,1,0:T(8,128)S(1)}, u32[]{:S(2)}, u32[]{:S(2)}) %collective-permute-start.1) | collective-permute-done | bytes 147488 | tf_op jit(solution)/shard_map/ppermute | solution.py:490
  25.8 10.6 %edges.1 = f32[16,128,128]{2,1,0:T(8,128)} custom-call(s32[2]{0:T(128)S(1)} %pad_add_fusion.place, f32[16]{0:T(128)} %diffuse_in.3, f32[16,128,256]{2,1,0:T(8,128)} %conc.3, f32[128,256]{1,0:T(8,128)} %cx.3, f32[128,256]{1,0:T(8,128)} %cy.3, f32[18,8,256]{2,1,0:T(8,128)S(1)} %collective-permute-done.before, f32[18,8,256]{2,1,0:T(8,128)S(1)} %collective-permute-done.1.after), custom_call_target="tpu_custom_call" | custom-call | tf_op jit(solution)/shard_map/edges/pallas_call | solution.py:493
  36.4 1.5 %all-to-all-done.x = f32[16,136,128]{2,1,0:T(8,128)S(1)} async-done(((f32[16,136,128]{2,1,0:T(8,128)}), f32[16,136,128]{2,1,0:T(8,128)S(1)}, u32[]{:S(2)}, u32[]{:S(2)}) %all-to-all-start) | async-done | bytes 1114144 | tf_op jit(solution)/shard_map/all_to_all | solution.py:523
  37.9 5.8 %all-to-all-start.1 = ((f32[16,128,128]{2,1,0:T(8,128)}), f32[16,128,128]{2,1,0:T(8,128)}, u32[]{:S(2)}, u32[]{:S(2)}) async-start(f32[16,128,128]{2,1,0:T(8,128)} %edges.1), calls=%async_computation.1 | async-start | bytes 2097152 | tf_op jit(solution)/shard_map/all_to_all | solution.py:523
  43.7 1.1 copy-done.3
  44.9 1.1 copy-done.4
  46.0 0.7 tables.1
  46.7 0.7 copy-done
  47.4 0.1 convert_element_type.8.info
  47.5 1.0 copy-done.1
  48.5 14.9 %chemistry.3 = f32[2048,128]{1,0:T(8,128)} custom-call(s32[256]{0:T(256)S(1)} %convert_element_type.8.info, s32[1]{0:T(128)} %bitcast.3.start, f32[16,136,128]{2,1,0:T(8,128)S(1)} %all-to-all-done.x, f32[4,768,128]{2,1,0:T(8,128)S(1)} %get-tuple-element.14.log_table, bf16[768,256]{1,0:T(8,128)(2,1)S(1)} %copy-done.1, bf16[512,768]{1,0:T(8,128)(2,1)S(1)} %get-tuple-element.16.both), custom_call_target="tpu_custom_call" | custom-call | tf_op jit(solution)/shard_map/chemistry/pallas_call | solution.py:391
  63.4 5.8 %all-to-all-start.3 = ((f32[16,16,8,128]{3,2,1,0:T(8,128)}), f32[16,16,8,128]{3,2,1,0:T(8,128)}, u32[]{:S(2)}, u32[]{:S(2)}) async-start(f32[16,16,8,128]{3,2,1,0:T(8,128)} %bitcast.5), calls=%async_computation.3 | async-start | bytes 2097152 | tf_op jit(solution)/shard_map/all_to_all | solution.py:528
  69.3 8.8 %chemistry.2 = f32[2048,128]{1,0:T(8,128)} custom-call(s32[256]{0:T(256)S(1)} %convert_element_type.8.info, s32[1]{0:T(128)} %bitcast.start, f32[16,128,128]{2,1,0:T(8,128)} %all-to-all-done.1.x, f32[4,768,128]{2,1,0:T(8,128)S(1)} %get-tuple-element.14.log_table, bf16[768,256]{1,0:T(8,128)(2,1)S(1)} %copy-done.2, bf16[512,768]{1,0:T(8,128)(2,1)S(1)} %get-tuple-element.16.both), custom_call_target="tpu_custom_call" | custom-call | tf_op jit(solution)/shard_map/chemistry/pallas_call | solution.py:391
  78.1 11.7 %all-to-all-done.3.parts = f32[16,16,8,128]{3,2,1,0:T(8,128)} async-done(((f32[16,16,8,128]{3,2,1,0:T(8,128)}), f32[16,16,8,128]{3,2,1,0:T(8,128)}, u32[]{:S(2)}, u32[]{:S(2)}) %all-to-all-start.3) | async-done | bytes 1048608 | tf_op jit(solution)/shard_map/all_to_all | solution.py:528
  89.9 3.7 %all-to-all-start.2 = ((f32[16,16,8,128]{3,2,1,0:T(8,128)}), f32[16,16,8,128]{3,2,1,0:T(8,128)S(1)}, u32[]{:S(2)}, u32[]{:S(2)}) async-start(f32[16,16,8,128]{3,2,1,0:T(8,128)} %bitcast.6), calls=%async_computation.2 | async-start | bytes 2097152 | tf_op jit(solution)/shard_map/all_to_all | solution.py:528
  93.5 2.3 %place.2.rest_0_ = f32[16,128,256]{2,1,0:T(8,128)} custom-call(f32[16,16,8,128]{3,2,1,0:T(8,128)} %all-to-all-done.3.parts), custom_call_target="tpu_custom_call" | custom-call | tf_op jit(solution)/shard_map/place/pallas_call | solution.py:425
  95.9 16.1 %all-to-all-done.2.parts = f32[16,16,8,128]{3,2,1,0:T(8,128)S(1)} async-done(((f32[16,16,8,128]{3,2,1,0:T(8,128)}), f32[16,16,8,128]{3,2,1,0:T(8,128)S(1)}, u32[]{:S(2)}, u32[]{:S(2)}) %all-to-all-start.2) | async-done | bytes 1048608 | tf_op jit(solution)/shard_map/all_to_all | solution.py:528
  111.9 1.0 copy-done.6
  112.9 2.3 %place.3 = f32[16,128,256]{2,1,0:T(8,128)} custom-call(f32[16,16,8,128]{3,2,1,0:T(8,128)} %copy-done.6, f32[16,128,256]{2,1,0:T(8,128)} %place.2.rest_0_), custom_call_target="tpu_custom_call", output_to_operand_aliasing={{}: (1, {})} | custom-call | tf_op jit(solution)/shard_map/place/pallas_call | solution.py:425
  (16 shorter events, 0.1 us)
Async XLA Ops:
  11.2 8.3 %copy-start.8 = (f32[18,8,256]{2,1,0:T(8,128)S(1)}, f32[18,8,256]{2,1,0:T(8,128)}, u32[]{:S(2)}) copy-start(f32[18,8,256]{2,1,0:T(8,128)} %get-tuple-element.12) | copy-start | bytes 442372
  11.2 9.8 %copy-start.7 = (f32[18,8,256]{2,1,0:T(8,128)S(1)}, f32[18,8,256]{2,1,0:T(8,128)}, u32[]{:S(2)}) copy-start(f32[18,8,256]{2,1,0:T(8,128)} %get-tuple-element.13) | copy-start | bytes 442372
  11.2 26.7 %all-to-all-start = ((f32[16,136,128]{2,1,0:T(8,128)}), f32[16,136,128]{2,1,0:T(8,128)S(1)}, u32[]{:S(2)}, u32[]{:S(2)}) async-start(f32[16,136,128]{2,1,0:T(8,128)} %get-tuple-element.11), calls=%async_computation | async-start | bytes 2228224 | tf_op jit(solution)/shard_map/all_to_all | solution.py:523
  19.5 2.9 %collective-permute-start = (f32[18,8,256]{2,1,0:T(8,128)S(1)}, f32[18,8,256]{2,1,0:T(8,128)S(1)}, u32[]{:S(2)}, u32[]{:S(2)}) collective-permute-start(f32[18,8,256]{2,1,0:T(8,128)S(1)} %copy-done.8), channel_id=1, source_target_pairs={{0,16},{16,32},{32,48},{48,64},{64,80},{80,96},{96,112},{1,17},{17... | collective-permute-start | bytes 442376 | tf_op jit(solution)/shard_map/ppermute | solution.py:489
  21.0 4.8 %collective-permute-start.1 = (f32[18,8,256]{2,1,0:T(8,128)S(1)}, f32[18,8,256]{2,1,0:T(8,128)S(1)}, u32[]{:S(2)}, u32[]{:S(2)}) collective-permute-start(f32[18,8,256]{2,1,0:T(8,128)S(1)} %copy-done.7), channel_id=1, source_target_pairs={{16,0},{32,16},{48,32},{64,48},{80,64},{96,80},{112,96},{17,1},{33... | collective-permute-start | bytes 442376 | tf_op jit(solution)/shard_map/ppermute | solution.py:490
  36.4 7.3 %copy-start.5 = (f32[4,768]{1,0:T(4,128)S(1)}, f32[4,768]{1,0:T(4,128)}, u32[]{:S(2)}) copy-start(f32[4,768]{1,0:T(4,128)} %log_rate.1) | copy-start | bytes 36868
  37.9 25.5 %all-to-all-start.1 = ((f32[16,128,128]{2,1,0:T(8,128)}), f32[16,128,128]{2,1,0:T(8,128)}, u32[]{:S(2)}, u32[]{:S(2)}) async-start(f32[16,128,128]{2,1,0:T(8,128)} %edges.1), calls=%async_computation.1 | async-start | bytes 2097152 | tf_op jit(solution)/shard_map/all_to_all | solution.py:523
  43.7 1.1 copy-start.3
  44.9 1.1 copy-start.4
  46.7 0.7 copy-start
  47.5 1.0 copy-start.1
  63.4 5.9 %copy-start.2 = (bf16[768,256]{1,0:T(8,128)(2,1)S(1)}, bf16[768,256]{1,0:T(8,128)(2,1)}, u32[]{:S(2)}) copy-start(bf16[768,256]{1,0:T(8,128)(2,1)} %copy-done) | copy-start | bytes 1179652
  63.4 26.5 %all-to-all-start.3 = ((f32[16,16,8,128]{3,2,1,0:T(8,128)}), f32[16,16,8,128]{3,2,1,0:T(8,128)}, u32[]{:S(2)}, u32[]{:S(2)}) async-start(f32[16,16,8,128]{3,2,1,0:T(8,128)} %bitcast.5), calls=%async_computation.3 | async-start | bytes 2097152 | tf_op jit(solution)/shard_map/all_to_all | solution.py:528
  89.9 22.0 %all-to-all-start.2 = ((f32[16,16,8,128]{3,2,1,0:T(8,128)}), f32[16,16,8,128]{3,2,1,0:T(8,128)S(1)}, u32[]{:S(2)}, u32[]{:S(2)}) async-start(f32[16,16,8,128]{3,2,1,0:T(8,128)} %bitcast.6), calls=%async_computation.2 | async-start | bytes 2097152 | tf_op jit(solution)/shard_map/all_to_all | solution.py:528
  111.9 1.0 copy-start.6

commit v4 on v3

--- a/solution.py
+++ b/solution.py
@@ -165,10 +165,10 @@
 def store_grouped(out, base, group):
     def store(row, pair):
         at = row - EDGE
-        place = 2 * (base + lax.shift_right_logical(at, 3))
-        line = pl.multiple_of(lax.bitwise_and(at, EDGE - 1) * group, group)
-        out[place, pl.ds(line, group), :] = pair[0]
-        out[place + 1, pl.ds(line, group), :] = pair[1]
+        line = pl.multiple_of((base + lax.shift_right_logical(at, 3)) * group, group)
+        peer = 2 * lax.bitwise_and(at, EDGE - 1)
+        out[peer, pl.ds(line, group), :] = pair[0]
+        out[peer + 1, pl.ds(line, group), :] = pair[1]
 
     return store
 
@@ -227,7 +227,25 @@
 
 
 def edge_kernel(
-    place, diffuse_in, conc, cx, cy, before, after, out, diffuse, raw, wx, wy, coef, one, two, sems
+    place,
+    diffuse_in,
+    conc,
+    cx,
+    cy,
+    before,
+    after,
+    _log_table,
+    _reac,
+    _both,
+    out,
+    diffuse,
+    raw,
+    wx,
+    wy,
+    coef,
+    one,
+    two,
+    sems,
 ):
     group, rows = raw.shape[2:4]
     total = conc.shape[1]
@@ -317,17 +335,23 @@
 
 def tables_of(log_rate, reactants, products):
     species, reactions = reactants.shape
+    classes = log_rate.shape[0]
     vmem = pl.BlockSpec(memory_space=pltpu.VMEM)
     return pl.pallas_call(
         table_kernel,
+        grid=(1,),
         out_shape=[
-            jax.ShapeDtypeStruct((log_rate.shape[0], reactions, LANES), f32),
-            jax.ShapeDtypeStruct((reactions, species), bf16),
-            jax.ShapeDtypeStruct((2 * species, reactions), bf16),
+            pltpu.VMEM((classes, reactions, LANES), f32),
+            pltpu.VMEM((reactions, species), bf16),
+            pltpu.VMEM((2 * species, reactions), bf16),
         ],
-        in_specs=[vmem] * 3,
+        in_specs=[
+            pl.BlockSpec((classes, reactions), lambda i: (0, 0)),
+            pl.BlockSpec((species, reactions), lambda i: (0, 0)),
+            pl.BlockSpec((reactions, species), lambda i: (0, 0)),
+        ],
         out_specs=[vmem] * 3,
-        compiler_params=pltpu.CompilerParams(vmem_limit_bytes=20 << 20),
+        compiler_params=pltpu.CompilerParams(vmem_limit_bytes=12 << 20),
         name="tables",
     )(log_rate, reactants, products)
 
@@ -336,7 +360,7 @@
     peers, blocks = x.shape[0], EDGE
     species = reac.shape[1]
     group = species // peers
-    codes = [info[start[0] + 2 * b] for b in range(blocks)]
+    codes = [info[start[b]] for b in range(blocks)]
     count = jnp.int32(0)
     for b in range(blocks):
         listed[1, b] = lax.bitwise_and(codes[b], 3)
@@ -399,38 +423,49 @@
             pltpu.SMEM((3, blocks), jnp.int32),
             pltpu.SemaphoreType.DMA,
         ],
-        compiler_params=pltpu.CompilerParams(vmem_limit_bytes=20 << 20),
+        compiler_params=pltpu.CompilerParams(vmem_limit_bytes=14 << 20),
         name="chemistry",
     )(info, start, x, log_table, reac, both)
 
 
-def place_kernel(groups, parts, *rest):
-    whole, sems = rest[-2:]
-    copies = [
-        pltpu.make_async_copy(
-            parts.at[2 * k + side],
-            whole.at[:, pl.ds(at * EDGE, EDGE), pl.ds(side * LANES, LANES)],
-            sems.at[2 * k + side],
-        )
-        for k, at in enumerate(groups)
-        for side in (0, 1)
-    ]
-    start_all(copies)
+def place_kernel(firsts, parts, *rest):
+    whole, stage, sems = rest[-3:]
+    peers, group, blocks, _ = parts.shape
+    count = blocks // len(firsts)
+    rows = count * EDGE
+    copies = []
+    for k, first in enumerate(firsts):
+        for side in (0, 1):
+            for peer in range(side, peers, 2):
+                for s in range(group):
+                    at = pl.ds(s * rows + peer // 2, count, stride=EDGE)
+                    stage[k, side, at, :] = parts[peer, s, k * count : (k + 1) * count]
+            copy = pltpu.make_async_copy(
+                stage.at[k, side].reshape(group, rows, LANES),
+                whole.at[:, pl.ds(first, rows), pl.ds(side * LANES, LANES)],
+                sems.at[2 * k + side],
+            )
+            copy.start()
+            copies.append(copy)
     wait_all(copies)
 
 
-def place_rows(parts, groups, rows, *whole):
-    peers, group = parts.shape[:2]
+def place_rows(parts, firsts, rows, *whole):
+    peers, group, blocks, _ = parts.shape
     hbm = pl.BlockSpec(memory_space=pltpu.HBM)
+    count = len(firsts)
     return pl.pallas_call(
-        functools.partial(place_kernel, groups),
+        functools.partial(place_kernel, firsts),
         out_shape=pltpu.HBM((group, rows, 2 * LANES), f32),
         in_specs=[pl.BlockSpec(memory_space=pltpu.VMEM)] + [hbm] * len(whole),
         out_specs=hbm,
-        scratch_shapes=[pltpu.SemaphoreType.DMA((peers,))],
+        scratch_shapes=[
+            pltpu.VMEM((count, 2, group * blocks // count * EDGE, LANES), f32),
+            pltpu.SemaphoreType.DMA((2 * count,)),
+        ],
         input_output_aliases={1: 0} if whole else {},
         name="place",
-    )(parts, *whole)
+    )(pltpu.with_memory_space_constraint(parts, pltpu.VMEM), *whole)
 
 
 def per_device(
@@ -463,15 +498,18 @@
     def in_hbm(*arrays):
         return [pltpu.with_memory_space_constraint(v, pltpu.HBM) for v in arrays]
 
+    def in_vmem(*arrays):
+        return [pltpu.with_memory_space_constraint(v, pltpu.VMEM) for v in arrays]
+
     fields = in_hbm(concentrations, courant_x, courant_y)
     slab_rows = rows // 2 + 2 * EDGE
-    rim = pltpu.HBM((group + 2, EDGE, columns), f32)
+    rim = pltpu.VMEM((group + 2, EDGE, columns), f32)
     middle, last, leading = pl.pallas_call(
         middle_kernel,
         grid=(1,),
         out_shape=(pltpu.HBM((peers, lines + EDGE, LANES), f32), rim, rim),
         in_specs=[hbm] * 6,
-        out_specs=(pl.BlockSpec((peers, lines + EDGE, LANES), lambda i: (0, 0, 0)), hbm, hbm),
+        out_specs=(pl.BlockSpec((peers, lines + EDGE, LANES), lambda i: (0, 0, 0)), vmem, vmem),
         scratch_shapes=[
             pltpu.SMEM((group,), f32),
             pltpu.SMEM((2 * EDGE,), jnp.int32),
@@ -488,13 +526,14 @@
 
     before = lax.ppermute(last, "region", up)
     after = lax.ppermute(leading, "region", down)
+    tables = tables_of(*in_hbm(log_rate, reactants, products))
     place = jnp.stack([lax.axis_index("region"), jnp.int32(regions)]).astype(jnp.int32)
     slab_rows = rows // 4 + 2 * EDGE
     edges = pl.pallas_call(
         edge_kernel,
         grid=(1,),
         out_shape=pltpu.HBM((peers, lines, LANES), f32),
-        in_specs=[smem] + [hbm] * 4 + [vmem] * 2,
+        in_specs=[smem] + [hbm] * 4 + [vmem] * 5,
         out_specs=pl.BlockSpec((peers, lines, LANES), lambda i: (0, 0, 0)),
         scratch_shapes=[
             pltpu.SMEM((group,), f32),
@@ -506,30 +545,29 @@
         ],
         compiler_params=pltpu.CompilerParams(vmem_limit_bytes=16 << 20),
         name="edges",
-    )(place, *in_hbm(diffusion), *fields, before, after)
-
-    tables = tables_of(log_rate, reactants, products)
+    )(place, *in_hbm(diffusion), *fields, *in_vmem(before, after), *in_vmem(*tables))
+
     mine = lax.axis_index("species").astype(jnp.int32)
-    lower, parity = mine // 2, mine % 2
-    done = []
     exchange = functools.partial(
         lax.all_to_all, axis_name="species", split_axis=0, concat_axis=0, tiled=True
     )
     info = None
+    done = []
+    order = jnp.arange(EDGE, dtype=jnp.int32)
+    half = peers // 2
     for slab, source in (
-        (middle, lower + peers // 4),
-        (edges, lower + jnp.where(lower < peers // 4, 0, peers // 2)),
+        (middle, order + half // 2),
+        (edges, jnp.where(order < half // 2, order, order + half)),
     ):
         gathered = exchange(slab)
         if info is None:
             info = gathered[:, lines, : 2 * EDGE].astype(jnp.int32).reshape(-1)
-        start = (source * 2 * EDGE + parity).reshape(1)
-        reacted = chemistry(gathered, info, start, *tables)
+        start = source * 2 * EDGE + mine
+        reacted = chemistry(*in_vmem(gathered), info, start, *in_vmem(*tables))
         done.append(exchange(reacted.reshape(peers, group, EDGE, LANES)))
-    quarter = places // 2
-    filled = place_rows(done[0], range(quarter, 3 * quarter), rows)
-    sides = (*range(quarter), *range(3 * quarter, 4 * quarter))
-    return place_rows(done[1], sides, rows, filled)
+    quarter = rows // 4
+    filled = place_rows(done[0], (quarter,), rows)
+    return place_rows(done[1], (0, 3 * quarter), rows, filled)
 
 
 def solution(mesh):

time: 116 us -> 110 us (0.948)
  the two profiles are of different devices: /device:TPU:0 before, /device:TPU:2 now
where the time goes in v4:
time: 110 us
  Pallas kernels  44 us (40%)
  waiting for transfers between devices  34 us (31%)
  starting transfers between devices  28.4 us (26%)
  local copies, waits for them, and re-layouts  2.8 us (3%)
    all_to_all x2, waiting for transfers between devices, per_device(): done.append(exchange(reacted.reshape(peers, group, EDGE, LANES)))  26.5 us
    pallas_call x2, Pallas kernels, chemistry(): pl.pallas_call(chemistry_kernel, out_shape=pltpu.HBM((species * blocks, L...  19.9 us
    all_to_all x2, starting transfers between devices, per_device(): gathered = exchange(slab)  15.3 us
    pallas_call x1, Pallas kernels, per_device(): pl.pallas_call(edge_kernel, grid=(1,), out_shape=pltpu.HBM((peers, lines,...  11 us
    pallas_call x1, Pallas kernels, per_device(): pl.pallas_call(middle_kernel, grid=(1,), out_shape=(pltpu.HBM((peers, lin...  8.88 us
    all_to_all x2, starting transfers between devices, per_device(): done.append(exchange(reacted.reshape(peers, group, EDGE, LANES)))  7.49 us
    all_to_all x2, waiting for transfers between devices, per_device(): gathered = exchange(slab)  6.62 us
    ppermute x1, starting transfers between devices, per_device(): after = lax.ppermute(leading, 'region', down)  3.64 us
  transfers between devices with their start and end apart: 6, of which 4 were waited for; matrix products, arithmetic and copies ran while one was open for 0% of the time, Pallas kernels for 31%

profile of v4, /device:TPU:2, one launch (start us, length us, event | category | flops | bytes accessed | tf_op | source)
XLA Modules:
  0.0 109.6 jit_solution(953582851409937177)
XLA Ops:
  0.0 8.9 %middle.1 = (f32[16,136,128]{2,1,0:T(8,128)}, f32[18,8,256]{2,1,0:T(8,128)}, f32[18,8,256]{2,1,0:T(8,128)}) custom-call(f32[16]{0:T(128)} %diffuse_in.3, s32[16]{0:T(128)} %classes_in.1, s32[16]{0:T(128)} %slots_in.1, f32[16,128,256]{2,1,0:T(8,128)} %conc.3, f32[128,256]{1,0:T(8,128)} %cx.3, f32[128,256]{1,0:T(8,128)} %cy.3), custom_call_target="tpu_custom_call" | custom-call | tf_op jit(solution)/shard_map/middle/pallas_call | solution.py:507
  8.9 8.1 %all-to-all-start = ((f32[16,136,128]{2,1,0:T(8,128)}), f32[16,136,128]{2,1,0:T(8,128)S(1)}, u32[]{:S(2)}, u32[]{:S(2)}) async-start(f32[16,136,128]{2,1,0:T(8,128)} %get-tuple-element.11), calls=%async_computation | async-start | bytes 2228224 | tf_op jit(solution)/shard_map/all_to_all | solution.py:562
  17.0 1.9 %collective-permute-start = (f32[18,8,256]{2,1,0:T(8,128)}, f32[18,8,256]{2,1,0:T(8,128)}, u32[]{:S(2)}, u32[]{:S(2)}) collective-permute-start(f32[18,8,256]{2,1,0:T(8,128)} %get-tuple-element.12), channel_id=1, source_target_pairs={{0,16},{16,32},{32,48},{48,64},{64,80},{80,96},{96,112},{1,17},{17... | collective-permute-start | bytes 442376 | tf_op jit(solution)/shard_map/ppermute | solution.py:527
  18.9 3.6 %collective-permute-start.1 = (f32[18,8,256]{2,1,0:T(8,128)}, f32[18,8,256]{2,1,0:T(8,128)}, u32[]{:S(2)}, u32[]{:S(2)}) collective-permute-start(f32[18,8,256]{2,1,0:T(8,128)} %get-tuple-element.13), channel_id=1, source_target_pairs={{16,0},{32,16},{48,32},{64,48},{80,64},{96,80},{112,96},{17,1},{33... | collective-permute-start | bytes 442376 | tf_op jit(solution)/shard_map/ppermute | solution.py:528
  22.5 2.1 %tables.1 = (f32[4,768,128]{2,1,0:T(8,128)S(1)}, bf16[768,256]{1,0:T(8,128)(2,1)S(1)}, bf16[512,768]{1,0:T(8,128)(2,1)S(1)}) custom-call(f32[4,768]{1,0:T(4,128)} %log_rate.1, s32[256,768]{1,0:T(8,128)} %reactants.1, s32[768,256]{1,0:T(8,128)} %products.1), custom_call_target="tpu_custom_call" | custom-call | tf_op jit(solution)/shard_map/tables/pallas_call | solution.py:340
  24.6 0.1 pad_add_fusion.place
  24.7 0.0 collective-permute-done.before
  24.7 0.8 collective-permute-done.1.after
  25.5 11.0 %edges.1 = f32[16,128,128]{2,1,0:T(8,128)} custom-call(s32[2]{0:T(128)S(1)} %pad_add_fusion.place, f32[16]{0:T(128)} %diffuse_in.3, f32[16,128,256]{2,1,0:T(8,128)} %conc.3, f32[128,256]{1,0:T(8,128)} %cx.3, f32[128,256]{1,0:T(8,128)} %cy.3, f32[18,8,256]{2,1,0:T(8,128)} %collective-permute-done.before, f32[18,8,256]{2,1,0:T(8,128)} %collective-permute-done.1.after, ...), custom_call_target="tpu_custom_call" | custom-call | tf_op jit(solution)/shard_map/edges/pallas_call | solution.py:532
  36.6 0.7 copy-done
  37.3 0.0 all-to-all-done.x
  37.3 7.3 %all-to-all-start.1 = ((f32[16,128,128]{2,1,0:T(8,128)}), f32[16,128,128]{2,1,0:T(8,128)}, u32[]{:S(2)}, u32[]{:S(2)}) async-start(f32[16,128,128]{2,1,0:T(8,128)} %edges.1), calls=%async_computation.1 | async-start | bytes 2097152 | tf_op jit(solution)/shard_map/all_to_all | solution.py:562
  44.6 0.1 convert_element_type.8.info
  44.7 1.0 copy-done.1
  45.7 11.2 %chemistry.3 = f32[2048,128]{1,0:T(8,128)} custom-call(s32[256]{0:T(256)S(1)} %convert_element_type.8.info, s32[8]{0:T(128)S(1)} %multiply_add_fusion.start, f32[16,136,128]{2,1,0:T(8,128)S(1)} %all-to-all-done.x, f32[4,768,128]{2,1,0:T(8,128)S(1)} %get-tuple-element.14._log_table.log_table, bf16[768,256]{1,0:T(8,128)(2,1)S(1)} %copy-done.1, ...), custom_call_target="tpu_custom_call" | custom-call | tf_op jit(solution)/shard_map/chemistry/pallas_call | solution.py:415
  56.9 6.6 %all-to-all-done.1.x = f32[16,128,128]{2,1,0:T(8,128)} async-done(((f32[16,128,128]{2,1,0:T(8,128)}), f32[16,128,128]{2,1,0:T(8,128)}, u32[]{:S(2)}, u32[]{:S(2)}) %all-to-all-start.1) | async-done | bytes 1048608 | tf_op jit(solution)/shard_map/all_to_all | solution.py:562
  63.5 3.8 %all-to-all-start.3 = ((f32[16,16,8,128]{3,2,1,0:T(8,128)}), f32[16,16,8,128]{3,2,1,0:T(8,128)S(1)}, u32[]{:S(2)}, u32[]{:S(2)}) async-start(f32[16,16,8,128]{3,2,1,0:T(8,128)} %bitcast.3), calls=%async_computation.3 | async-start | bytes 2097152 | tf_op jit(solution)/shard_map/all_to_all | solution.py:567
  67.4 1.0 copy-done.2
  68.4 8.6 %chemistry.2 = f32[2048,128]{1,0:T(8,128)} custom-call(s32[256]{0:T(256)S(1)} %convert_element_type.8.info, s32[8]{0:T(128)S(1)} %fusion.2.start, f32[16,128,128]{2,1,0:T(8,128)} %all-to-all-done.1.x, f32[4,768,128]{2,1,0:T(8,128)S(1)} %get-tuple-element.14._log_table.log_table, bf16[768,256]{1,0:T(8,128)(2,1)S(1)} %copy-done.2, ...), custom_call_target="tpu_custom_call" | custom-call | tf_op jit(solution)/shard_map/chemistry/pallas_call | solution.py:415
  77.1 9.9 %all-to-all-done.3.parts = f32[16,16,8,128]{3,2,1,0:T(8,128)S(1)} async-done(((f32[16,16,8,128]{3,2,1,0:T(8,128)}), f32[16,16,8,128]{3,2,1,0:T(8,128)S(1)}, u32[]{:S(2)}, u32[]{:S(2)}) %all-to-all-start.3) | async-done | bytes 1048608 | tf_op jit(solution)/shard_map/all_to_all | solution.py:567
  87.0 3.7 %all-to-all-start.2 = ((f32[16,16,8,128]{3,2,1,0:T(8,128)}), f32[16,16,8,128]{3,2,1,0:T(8,128)S(1)}, u32[]{:S(2)}, u32[]{:S(2)}) async-start(f32[16,16,8,128]{3,2,1,0:T(8,128)} %bitcast.4), calls=%async_computation.2 | async-start | bytes 2097152 | tf_op jit(solution)/shard_map/all_to_all | solution.py:567
  90.6 1.1 %place.2.rest_0_ = f32[16,128,256]{2,1,0:T(8,128)} custom-call(f32[16,16,8,128]{3,2,1,0:T(8,128)S(1)} %all-to-all-done.3.parts), custom_call_target="tpu_custom_call" | custom-call | tf_op jit(solution)/shard_map/place/pallas_call | solution.py:457
  91.8 16.6 %all-to-all-done.2.parts = f32[16,16,8,128]{3,2,1,0:T(8,128)S(1)} async-done(((f32[16,16,8,128]{3,2,1,0:T(8,128)}), f32[16,16,8,128]{3,2,1,0:T(8,128)S(1)}, u32[]{:S(2)}, u32[]{:S(2)}) %all-to-all-start.2) | async-done | bytes 1048608 | tf_op jit(solution)/shard_map/all_to_all | solution.py:567
  108.4 1.1 place.3
  (6 shorter events, 0.0 us)
Async XLA Ops:
  8.9 28.4 %all-to-all-start = ((f32[16,136,128]{2,1,0:T(8,128)}), f32[16,136,128]{2,1,0:T(8,128)S(1)}, u32[]{:S(2)}, u32[]{:S(2)}) async-start(f32[16,136,128]{2,1,0:T(8,128)} %get-tuple-element.11), calls=%async_computation | async-start | bytes 2228224 | tf_op jit(solution)/shard_map/all_to_all | solution.py:562
  17.0 7.7 %collective-permute-start = (f32[18,8,256]{2,1,0:T(8,128)}, f32[18,8,256]{2,1,0:T(8,128)}, u32[]{:S(2)}, u32[]{:S(2)}) collective-permute-start(f32[18,8,256]{2,1,0:T(8,128)} %get-tuple-element.12), channel_id=1, source_target_pairs={{0,16},{16,32},{32,48},{48,64},{64,80},{80,96},{96,112},{1,17},{17... | collective-permute-start | bytes 442376 | tf_op jit(solution)/shard_map/ppermute | solution.py:527
  18.9 6.6 %collective-permute-start.1 = (f32[18,8,256]{2,1,0:T(8,128)}, f32[18,8,256]{2,1,0:T(8,128)}, u32[]{:S(2)}, u32[]{:S(2)}) collective-permute-start(f32[18,8,256]{2,1,0:T(8,128)} %get-tuple-element.13), channel_id=1, source_target_pairs={{16,0},{32,16},{48,32},{64,48},{80,64},{96,80},{112,96},{17,1},{33... | collective-permute-start | bytes 442376 | tf_op jit(solution)/shard_map/ppermute | solution.py:528
  36.5 0.7 copy-start
  37.3 26.3 %all-to-all-start.1 = ((f32[16,128,128]{2,1,0:T(8,128)}), f32[16,128,128]{2,1,0:T(8,128)}, u32[]{:S(2)}, u32[]{:S(2)}) async-start(f32[16,128,128]{2,1,0:T(8,128)} %edges.1), calls=%async_computation.1 | async-start | bytes 2097152 | tf_op jit(solution)/shard_map/all_to_all | solution.py:562
  44.7 1.0 copy-start.1
  63.5 23.4 %all-to-all-start.3 = ((f32[16,16,8,128]{3,2,1,0:T(8,128)}), f32[16,16,8,128]{3,2,1,0:T(8,128)S(1)}, u32[]{:S(2)}, u32[]{:S(2)}) async-start(f32[16,16,8,128]{3,2,1,0:T(8,128)} %bitcast.3), calls=%async_computation.3 | async-start | bytes 2097152 | tf_op jit(solution)/shard_map/all_to_all | solution.py:567
  67.4 1.0 copy-start.2
  87.0 21.4 %all-to-all-start.2 = ((f32[16,16,8,128]{3,2,1,0:T(8,128)}), f32[16,16,8,128]{3,2,1,0:T(8,128)S(1)}, u32[]{:S(2)}, u32[]{:S(2)}) async-start(f32[16,16,8,128]{3,2,1,0:T(8,128)} %bitcast.4), calls=%async_computation.2 | async-start | bytes 2097152 | tf_op jit(solution)/shard_map/all_to_all | solution.py:567

commit v5 on v4

--- a/solution.py
+++ b/solution.py
@@ -173,6 +173,21 @@
     return store
 
 
+def rim_kernel(conc, cx, cy, last, leading, sems):
+    group, total, _ = conc.shape
+    copies = []
+
+    def copy(src, dst):
+        copies.append(pltpu.make_async_copy(src, dst, sems.at[len(copies)]))
+
+    for rim, at in ((last, total - EDGE), (leading, 0)):
+        copy(conc.at[:, pl.ds(at, EDGE)], rim.at[pl.ds(0, group)])
+        copy(cx.at[pl.ds(at, EDGE)], rim.at[group])
+        copy(cy.at[pl.ds(at, EDGE)], rim.at[group + 1])
+    start_all(copies)
+    wait_all(copies)
+
+
 def middle_kernel(
     diffuse_in,
     classes_in,
@@ -181,8 +196,7 @@
     cx,
     cy,
     out,
-    last,
-    leading,
+    token,
     diffuse,
     classes,
     slots,
@@ -202,10 +216,6 @@
         (conc.at[:, pl.ds(first, rows), pl.ds(k * LANES, LANES)], raw.at[k]) for k in (0, 1)
     ]
     pairs += [(diffuse_in, diffuse), (classes_in, classes), (slots_in, slots)]
-    for rim, at in ((last, total - EDGE), (leading, 0)):
-        pairs.append((conc.at[:, pl.ds(at, EDGE)], rim.at[pl.ds(0, group)]))
-        pairs.append((cx.at[pl.ds(at, EDGE)], rim.at[group]))
-        pairs.append((cy.at[pl.ds(at, EDGE)], rim.at[group + 1]))
     copies = [pltpu.make_async_copy(*pair, sems.at[k]) for k, pair in enumerate(pairs)]
     start_all(copies)
     wait_all(copies[4:7])
@@ -223,7 +233,7 @@
     three_sweeps(
         raw_access(raw), store_grouped(out, 0, group), coef, nu, one, two, rows, (18, 17, 16)
     )
-    wait_all(copies[7:])
+    token[...] = codes
 
 
 def edge_kernel(
@@ -234,10 +244,14 @@
     cy,
     before,
     after,
-    _log_table,
-    _reac,
-    _both,
+    _token,
+    log_rate,
+    reactants,
+    products,
     out,
+    log_table,
+    reac,
+    both,
     diffuse,
     raw,
     wx,
@@ -269,6 +283,7 @@
             copy(conc.at[:, pl.ds(own_first, own), lanes], dst.at[:, pl.ds(own_at, own)])
             copy(halo.at[pl.ds(0, group), :, lanes], dst.at[:, pl.ds(halo_at, EDGE)])
     start_all(copies)
+    table_kernel(log_rate, reactants, products, log_table, reac, both)
     wait_all(copies)
     nu = spread_species(diffuse, group)
 
@@ -317,6 +332,20 @@
         made_lost = table_dot(both, rates)
         g = (state + step * made_lost[:species]) / (1.0 + step * made_lost[species:] / g)
     return g
+
+
+def first_line(block, group):
+    return block * group if isinstance(block, int) else pl.multiple_of(block * group, group)
+
+
+def table_kernel(log_rate, reactants, products, log_table, reac, both):
+    species, reactions = reactants.shape
+    reactant = reactants[...].astype(f32)
+    reac[...] = reactant.T.astype(bf16)
+    both[:species] = products[...].astype(f32).T.astype(bf16)
+    both[species:] = reactant.astype(bf16)
+    for k in range(log_rate.shape[0]):
+        log_table[k] = jnp.broadcast_to(log_rate[k : k + 1, :], (LANES, reactions)).T
 
 
 def first_line(block, group):
@@ -504,12 +533,23 @@
     fields = in_hbm(concentrations, courant_x, courant_y)
     slab_rows = rows // 2 + 2 * EDGE
     rim = pltpu.VMEM((group + 2, EDGE, columns), f32)
-    middle, last, leading = pl.pallas_call(
+    last, leading = pl.pallas_call(
+        rim_kernel,
+        out_shape=(rim, rim),
+        in_specs=[hbm] * 3,
+        out_specs=(vmem, vmem),
+        scratch_shapes=[pltpu.SemaphoreType.DMA((6,))],
+        name="rims",
+    )(*fields)
+    before = lax.ppermute(last, "region", up)
+    after = lax.ppermute(leading, "region", down)
+
+    middle, token = pl.pallas_call(
         middle_kernel,
         grid=(1,),
-        out_shape=(pltpu.HBM((peers, lines + EDGE, LANES), f32), rim, rim),
+        out_shape=(pltpu.HBM((peers, lines + EDGE, LANES), f32), pltpu.VMEM((EDGE, LANES), f32)),
         in_specs=[hbm] * 6,
-        out_specs=(pl.BlockSpec((peers, lines + EDGE, LANES), lambda i: (0, 0, 0)), vmem, vmem),
+        out_specs=(pl.BlockSpec((peers, lines + EDGE, LANES), lambda i: (0, 0, 0)), vmem),
         scratch_shapes=[
             pltpu.SMEM((group,), f32),
             pltpu.SMEM((2 * EDGE,), jnp.int32),
@@ -518,23 +558,27 @@
             pltpu.VMEM((slab_rows, columns), f32),
             pltpu.VMEM((slab_rows, columns), f32),
             *buffers(slab_rows),
-            pltpu.SemaphoreType.DMA((13,)),
+            pltpu.SemaphoreType.DMA((7,)),
         ],
         compiler_params=pltpu.CompilerParams(vmem_limit_bytes=16 << 20),
         name="middle",
     )(*in_hbm(diffusion, block_class, send_slot), *fields)
 
-    before = lax.ppermute(last, "region", up)
-    after = lax.ppermute(leading, "region", down)
-    tables = tables_of(*in_hbm(log_rate, reactants, products))
     place = jnp.stack([lax.axis_index("region"), jnp.int32(regions)]).astype(jnp.int32)
     slab_rows = rows // 4 + 2 * EDGE
-    edges = pl.pallas_call(
+    edges, *tables = pl.pallas_call(
         edge_kernel,
         grid=(1,),
-        out_shape=pltpu.HBM((peers, lines, LANES), f32),
-        in_specs=[smem] + [hbm] * 4 + [vmem] * 5,
-        out_specs=pl.BlockSpec((peers, lines, LANES), lambda i: (0, 0, 0)),
+        out_shape=(
+            pltpu.HBM((peers, lines, LANES), f32),
+            pltpu.VMEM((log_rate.shape[0], reactions, LANES), f32),
+            pltpu.VMEM((reactions, species), bf16),
+            pltpu.VMEM((2 * species, reactions), bf16),
+        ),
+        in_specs=[smem] + [hbm] * 4 + [vmem] * 3 + [
+            pl.BlockSpec(v.shape, lambda i: (0, 0)) for v in (log_rate, reactants, products)
+        ],
+        out_specs=(pl.BlockSpec((peers, lines, LANES), lambda i: (0, 0, 0)), vmem, vmem, vmem),
         scratch_shapes=[
             pltpu.SMEM((group,), f32),
             pltpu.VMEM((2, 2, group, slab_rows, LANES), f32),
@@ -543,9 +587,12 @@
             *buffers(slab_rows),
             pltpu.SemaphoreType.DMA((17,)),
         ],
-        compiler_params=pltpu.CompilerParams(vmem_limit_bytes=16 << 20),
+        compiler_params=pltpu.CompilerParams(vmem_limit_bytes=24 << 20),
+        cost_estimate=pl.CostEstimate(
+            flops=20 * 10**9, transcendentals=0, bytes_accessed=10 << 20
+        ),
         name="edges",
-    )(place, *in_hbm(diffusion), *fields, *in_vmem(before, after), *in_vmem(*tables))
+    )(place, *in_hbm(diffusion), *fields, *in_vmem(before, after), *in_vmem(token), *in_hbm(log_rate, reactants, products))
 
     mine = lax.axis_index("species").astype(jnp.int32)
     exchange = functools.partial(

time: 110 us -> 110 us (level)
  the two profiles are of different devices: /device:TPU:2 before, /device:TPU:0 now
where the time goes in v5:
time: 110 us; the launch traced here: 109 us
  Pallas kernels  46.6 us (42%)
  waiting for transfers between devices  32.4 us (29%)
  starting transfers between devices  23.5 us (21%)
  local copies, waits for them, and re-layouts  5.95 us (5%)
    pallas_call x2, Pallas kernels, chemistry(): pl.pallas_call(chemistry_kernel, out_shape=pltpu.HBM((species * blocks, L...  23.2 us
    all_to_all x2, waiting for transfers between devices, per_device(): done.append(exchange(reacted.reshape(peers, group, EDGE, LANES)))  21.3 us
    all_to_all x2, starting transfers between devices, per_device(): gathered = exchange(slab)  13.4 us
    pallas_call x1, Pallas kernels, per_device(): pl.pallas_call(edge_kernel, grid=(1,), out_shape=(pltpu.HBM((peers, lines...  11.5 us
    all_to_all x2, waiting for transfers between devices, per_device(): gathered = exchange(slab)  11.1 us
    pallas_call x1, Pallas kernels, per_device(): pl.pallas_call(middle_kernel, grid=(1,), out_shape=(pltpu.HBM((peers, lin...  8.73 us
    all_to_all x2, starting transfers between devices, per_device(): done.append(exchange(reacted.reshape(peers, group, EDGE, LANES)))  7.49 us
    unnamed x14, local copies, waits for them, and re-layouts  5.87 us
  transfers between devices with their start and end apart: 6, of which 4 were waited for; matrix products, arithmetic and copies ran while one was open for 0% of the time, Pallas kernels for 41%

profile of v5, /device:TPU:0, one launch (start us, length us, event | category | flops | bytes accessed | tf_op | source)
XLA Modules:
  0.0 108.9 jit_solution(15233763148268880218)
XLA Ops:
  0.0 1.1 rims.1
  1.1 1.3 %collective-permute-start = (f32[18,8,256]{2,1,0:T(8,128)S(1)}, f32[18,8,256]{2,1,0:T(8,128)S(1)}, u32[]{:S(2)}, u32[]{:S(2)}) collective-permute-start(f32[18,8,256]{2,1,0:T(8,128)S(1)} %get-tuple-element.14), channel_id=1, source_target_pairs={{0,16},{16,32},{32,48},{48,64},{64,80},{80,96},{96,112},{1,17},{17... | collective-permute-start | bytes 442376 | tf_op jit(solution)/shard_map/ppermute | solution.py:544
  2.4 1.3 %collective-permute-start.1 = (f32[18,8,256]{2,1,0:T(8,128)S(1)}, f32[18,8,256]{2,1,0:T(8,128)S(1)}, u32[]{:S(2)}, u32[]{:S(2)}) collective-permute-start(f32[18,8,256]{2,1,0:T(8,128)S(1)} %get-tuple-element.15), channel_id=1, source_target_pairs={{16,0},{32,16},{48,32},{64,48},{80,64},{96,80},{112,96},{17,1},{33... | collective-permute-start | bytes 442376 | tf_op jit(solution)/shard_map/ppermute | solution.py:545
  3.7 8.7 %middle.1 = (f32[16,136,128]{2,1,0:T(8,128)}, f32[8,128]{1,0:T(8,128)S(1)}) custom-call(f32[16]{0:T(128)} %diffuse_in.3, s32[16]{0:T(128)} %classes_in.1, s32[16]{0:T(128)} %slots_in.1, f32[16,128,256]{2,1,0:T(8,128)} %conc.5, f32[128,256]{1,0:T(8,128)} %cx.5, f32[128,256]{1,0:T(8,128)} %cy.5), custom_call_target="tpu_custom_call" | custom-call | tf_op jit(solution)/shard_map/middle/pallas_call | solution.py:547
  12.4 8.6 %all-to-all-start = ((f32[16,136,128]{2,1,0:T(8,128)}), f32[16,136,128]{2,1,0:T(8,128)S(1)}, u32[]{:S(2)}, u32[]{:S(2)}) async-start(f32[16,136,128]{2,1,0:T(8,128)} %get-tuple-element.13), calls=%async_computation | async-start | bytes 2228224 | tf_op jit(solution)/shard_map/all_to_all | solution.py:609
  21.1 0.7 copy-done.3
  21.8 0.7 copy-done.5
  22.4 0.9 copy-done.4
  23.3 0.9 copy-done.6
  24.2 11.5 %edges.1 = (f32[16,128,128]{2,1,0:T(8,128)}, f32[4,768,128]{2,1,0:T(8,128)S(1)}, bf16[768,256]{1,0:T(8,128)(2,1)S(1)}, bf16[512,768]{1,0:T(8,128)(2,1)S(1)}) custom-call(s32[2]{0:T(128)S(1)} %pad_add_fusion.place, f32[16]{0:T(128)} %diffuse_in.3, f32[16,128,256]{2,1,0:T(8,128)} %conc.5, f32[128,256]{1,0:T(8,128)} %cx.5, f32[128,256]{1,0:T(8,128)} %cy.5, ...), custom_call_target="tpu_custom_call" | custom-call | flops 20000000000 | bytes 10485760 | tf_op jit(solution)/shard_map/edges/pallas_call | solution.py:569
  35.7 0.7 copy-done
  36.5 2.7 %all-to-all-done.x = f32[16,136,128]{2,1,0:T(8,128)S(1)} async-done(((f32[16,136,128]{2,1,0:T(8,128)}), f32[16,136,128]{2,1,0:T(8,128)S(1)}, u32[]{:S(2)}, u32[]{:S(2)}) %all-to-all-start) | async-done | bytes 1114144 | tf_op jit(solution)/shard_map/all_to_all | solution.py:609
  39.2 4.8 %all-to-all-start.1 = ((f32[16,128,128]{2,1,0:T(8,128)}), f32[16,128,128]{2,1,0:T(8,128)}, u32[]{:S(2)}, u32[]{:S(2)}) async-start(f32[16,128,128]{2,1,0:T(8,128)} %get-tuple-element.17), calls=%async_computation.1 | async-start | bytes 2097152 | tf_op jit(solution)/shard_map/all_to_all | solution.py:609
  44.1 1.0 copy-done.1
  45.1 11.2 %chemistry.3 = f32[2048,128]{1,0:T(8,128)} custom-call(s32[256]{0:T(256)S(1)} %convert_element_type.8.info, s32[8]{0:T(128)S(1)} %multiply_add_fusion.start, f32[16,136,128]{2,1,0:T(8,128)S(1)} %all-to-all-done.x, f32[4,768,128]{2,1,0:T(8,128)S(1)} %get-tuple-element.18.log_table, bf16[768,256]{1,0:T(8,128)(2,1)S(1)} %copy-done.1, ...), custom_call_target="tpu_custom_call" | custom-call | tf_op jit(solution)/shard_map/chemistry/pallas_call | solution.py:444
  56.4 8.4 %all-to-all-done.1.x = f32[16,128,128]{2,1,0:T(8,128)} async-done(((f32[16,128,128]{2,1,0:T(8,128)}), f32[16,128,128]{2,1,0:T(8,128)}, u32[]{:S(2)}, u32[]{:S(2)}) %all-to-all-start.1) | async-done | bytes 1048608 | tf_op jit(solution)/shard_map/all_to_all | solution.py:609
  64.8 3.8 %all-to-all-start.3 = ((f32[16,16,8,128]{3,2,1,0:T(8,128)}), f32[16,16,8,128]{3,2,1,0:T(8,128)S(1)}, u32[]{:S(2)}, u32[]{:S(2)}) async-start(f32[16,16,8,128]{3,2,1,0:T(8,128)} %bitcast.3), calls=%async_computation.3 | async-start | bytes 2097152 | tf_op jit(solution)/shard_map/all_to_all | solution.py:614
  68.6 1.0 copy-done.2
  69.6 12.0 %chemistry.2 = f32[2048,128]{1,0:T(8,128)} custom-call(s32[256]{0:T(256)S(1)} %convert_element_type.8.info, s32[8]{0:T(128)S(1)} %fusion.2.start, f32[16,128,128]{2,1,0:T(8,128)} %all-to-all-done.1.x, f32[4,768,128]{2,1,0:T(8,128)S(1)} %get-tuple-element.18.log_table, bf16[768,256]{1,0:T(8,128)(2,1)S(1)} %copy-done.2, ...), custom_call_target="tpu_custom_call" | custom-call | tf_op jit(solution)/shard_map/chemistry/pallas_call | solution.py:444
  81.6 5.1 %all-to-all-done.3.parts = f32[16,16,8,128]{3,2,1,0:T(8,128)S(1)} async-done(((f32[16,16,8,128]{3,2,1,0:T(8,128)}), f32[16,16,8,128]{3,2,1,0:T(8,128)S(1)}, u32[]{:S(2)}, u32[]{:S(2)}) %all-to-all-start.3) | async-done | bytes 1048608 | tf_op jit(solution)/shard_map/all_to_all | solution.py:614
  86.7 3.7 %all-to-all-start.2 = ((f32[16,16,8,128]{3,2,1,0:T(8,128)}), f32[16,16,8,128]{3,2,1,0:T(8,128)S(1)}, u32[]{:S(2)}, u32[]{:S(2)}) async-start(f32[16,16,8,128]{3,2,1,0:T(8,128)} %bitcast.4), calls=%async_computation.2 | async-start | bytes 2097152 | tf_op jit(solution)/shard_map/all_to_all | solution.py:614
  90.4 1.1 %place.2.rest_0_ = f32[16,128,256]{2,1,0:T(8,128)} custom-call(f32[16,16,8,128]{3,2,1,0:T(8,128)S(1)} %all-to-all-done.3.parts), custom_call_target="tpu_custom_call" | custom-call | tf_op jit(solution)/shard_map/place/pallas_call | solution.py:486
  91.5 16.2 %all-to-all-done.2.parts = f32[16,16,8,128]{3,2,1,0:T(8,128)S(1)} async-done(((f32[16,16,8,128]{3,2,1,0:T(8,128)}), f32[16,16,8,128]{3,2,1,0:T(8,128)S(1)}, u32[]{:S(2)}, u32[]{:S(2)}) %all-to-all-start.2) | async-done | bytes 1048608 | tf_op jit(solution)/shard_map/all_to_all | solution.py:614
  107.7 1.1 place.3
  (14 shorter events, 0.2 us)
Async XLA Ops:
  1.1 20.0 %collective-permute-start = (f32[18,8,256]{2,1,0:T(8,128)S(1)}, f32[18,8,256]{2,1,0:T(8,128)S(1)}, u32[]{:S(2)}, u32[]{:S(2)}) collective-permute-start(f32[18,8,256]{2,1,0:T(8,128)S(1)} %get-tuple-element.14), channel_id=1, source_target_pairs={{0,16},{16,32},{32,48},{48,64},{64,80},{80,96},{96,112},{1,17},{17... | collective-permute-start | bytes 442376 | tf_op jit(solution)/shard_map/ppermute | solution.py:544
  2.4 19.4 %collective-permute-start.1 = (f32[18,8,256]{2,1,0:T(8,128)S(1)}, f32[18,8,256]{2,1,0:T(8,128)S(1)}, u32[]{:S(2)}, u32[]{:S(2)}) collective-permute-start(f32[18,8,256]{2,1,0:T(8,128)S(1)} %get-tuple-element.15), channel_id=1, source_target_pairs={{16,0},{32,16},{48,32},{64,48},{80,64},{96,80},{112,96},{17,1},{33... | collective-permute-start | bytes 442376 | tf_op jit(solution)/shard_map/ppermute | solution.py:545
  12.4 26.8 %all-to-all-start = ((f32[16,136,128]{2,1,0:T(8,128)}), f32[16,136,128]{2,1,0:T(8,128)S(1)}, u32[]{:S(2)}, u32[]{:S(2)}) async-start(f32[16,136,128]{2,1,0:T(8,128)} %get-tuple-element.13), calls=%async_computation | async-start | bytes 2228224 | tf_op jit(solution)/shard_map/all_to_all | solution.py:609
  21.1 0.7 copy-start.3
  21.8 0.7 copy-start.5
  22.4 0.9 copy-start.4
  23.3 0.9 copy-start.6
  35.7 0.7 copy-start
  39.2 25.6 %all-to-all-start.1 = ((f32[16,128,128]{2,1,0:T(8,128)}), f32[16,128,128]{2,1,0:T(8,128)}, u32[]{:S(2)}, u32[]{:S(2)}) async-start(f32[16,128,128]{2,1,0:T(8,128)} %get-tuple-element.17), calls=%async_computation.1 | async-start | bytes 2097152 | tf_op jit(solution)/shard_map/all_to_all | solution.py:609
  44.1 1.0 copy-start.1
  64.8 22.0 %all-to-all-start.3 = ((f32[16,16,8,128]{3,2,1,0:T(8,128)}), f32[16,16,8,128]{3,2,1,0:T(8,128)S(1)}, u32[]{:S(2)}, u32[]{:S(2)}) async-start(f32[16,16,8,128]{3,2,1,0:T(8,128)} %bitcast.3), calls=%async_computation.3 | async-start | bytes 2097152 | tf_op jit(solution)/shard_map/all_to_all | solution.py:614
  68.6 1.0 copy-start.2
  86.7 20.9 %all-to-all-start.2 = ((f32[16,16,8,128]{3,2,1,0:T(8,128)}), f32[16,16,8,128]{3,2,1,0:T(8,128)S(1)}, u32[]{:S(2)}, u32[]{:S(2)}) async-start(f32[16,16,8,128]{3,2,1,0:T(8,128)} %bitcast.4), calls=%async_computation.2 | async-start | bytes 2097152 | tf_op jit(solution)/shard_map/all_to_all | solution.py:614

commit v6 on v5

--- a/solution.py
+++ b/solution.py
@@ -250,7 +250,6 @@
     products,
     out,
     log_table,
-    reac,
     both,
     diffuse,
     raw,
@@ -283,7 +282,7 @@
             copy(conc.at[:, pl.ds(own_first, own), lanes], dst.at[:, pl.ds(own_at, own)])
             copy(halo.at[pl.ds(0, group), :, lanes], dst.at[:, pl.ds(halo_at, EDGE)])
     start_all(copies)
-    table_kernel(log_rate, reactants, products, log_table, reac, both)
+    table_kernel(log_rate, reactants, products, log_table, both)
     wait_all(copies)
     nu = spread_species(diffuse, group)
 
@@ -324,11 +323,27 @@
     )
 
 
-def euler(state, logs, step, reac, both):
+def blocks_dot(blocks, x):
+    size = x.shape[0]
+    high, low = split(x)
+    parts = [blocks[:, k : k + size] for k in range(0, blocks.shape[1], size)]
+    return jnp.concatenate(
+        [
+            jnp.dot(part, high, preferred_element_type=f32)
+            + jnp.dot(part, low, preferred_element_type=f32)
+            for part in parts
+        ],
+        axis=0,
+    )
+
+
+def euler(state, logs, step, both):
     species = state.shape[0]
+    reac = both[2 * species :]
+    both = both[: 2 * species]
     g = state
     for _ in range(ITERS):
-        rates = jnp.exp(logs + table_dot(reac, jnp.log(g)))
+        rates = jnp.exp(logs + blocks_dot(reac, jnp.log(g)))
         made_lost = table_dot(both, rates)
         g = (state + step * made_lost[:species]) / (1.0 + step * made_lost[species:] / g)
     return g
@@ -338,12 +353,13 @@
     return block * group if isinstance(block, int) else pl.multiple_of(block * group, group)
 
 
-def table_kernel(log_rate, reactants, products, log_table, reac, both):
+def table_kernel(log_rate, reactants, products, log_table, both):
     species, reactions = reactants.shape
     reactant = reactants[...].astype(f32)
-    reac[...] = reactant.T.astype(bf16)
     both[:species] = products[...].astype(f32).T.astype(bf16)
-    both[species:] = reactant.astype(bf16)
+    both[species : 2 * species] = reactant.astype(bf16)
+    for k in range(0, reactions, species):
+        both[2 * species :, k : k + species] = reactant[:, k : k + species].T.astype(bf16)
     for k in range(log_rate.shape[0]):
         log_table[k] = jnp.broadcast_to(log_rate[k : k + 1, :], (LANES, reactions)).T
 
@@ -352,12 +368,13 @@
     return block * group if isinstance(block, int) else pl.multiple_of(block * group, group)
 
 
-def table_kernel(log_rate, reactants, products, log_table, reac, both):
+def table_kernel(log_rate, reactants, products, log_table, both):
     species, reactions = reactants.shape
     reactant = reactants[...].astype(f32)
-    reac[...] = reactant.T.astype(bf16)
     both[:species] = products[...].astype(f32).T.astype(bf16)
-    both[species:] = reactant.astype(bf16)
+    both[species : 2 * species] = reactant.astype(bf16)
+    for k in range(0, reactions, species):
+        both[2 * species :, k : k + species] = reactant[:, k : k + species].T.astype(bf16)
     for k in range(log_rate.shape[0]):
         log_table[k] = jnp.broadcast_to(log_rate[k : k + 1, :], (LANES, reactions)).T
 
@@ -371,8 +388,7 @@
         grid=(1,),
         out_shape=[
             pltpu.VMEM((classes, reactions, LANES), f32),
-            pltpu.VMEM((reactions, species), bf16),
-            pltpu.VMEM((2 * species, reactions), bf16),
+            pltpu.VMEM((3 * species, reactions), bf16),
         ],
         in_specs=[
             pl.BlockSpec((classes, reactions), lambda i: (0, 0)),
@@ -385,9 +401,9 @@
     )(log_rate, reactants, products)
 
 
-def chemistry_kernel(info, start, x, log_table, reac, both, out, result, answer, listed, sem):
+def chemistry_kernel(info, start, x, log_table, both, out, result, answer, listed, sem):
     peers, blocks = x.shape[0], EDGE
-    species = reac.shape[1]
+    species = both.shape[0] // 3
     group = species // peers
     codes = [info[start[b]] for b in range(blocks)]
     count = jnp.int32(0)
@@ -412,7 +428,6 @@
             jnp.concatenate(states, axis=1),
             jnp.concatenate(logs, axis=1),
             jnp.concatenate(lengths, axis=1),
-            reac[...],
             both[...],
         )
         for i, b in enumerate(chosen):
@@ -437,14 +452,14 @@
     copy.wait()
 
 
-def chemistry(x, info, start, log_table, reac, both):
-    species, blocks = reac.shape[1], EDGE
+def chemistry(x, info, start, log_table, both):
+    species, blocks = both.shape[0] // 3, EDGE
     vmem = pl.BlockSpec(memory_space=pltpu.VMEM)
     smem = pl.BlockSpec(memory_space=pltpu.SMEM)
     return pl.pallas_call(
         chemistry_kernel,
         out_shape=pltpu.HBM((species * blocks, LANES), f32),
-        in_specs=[smem, smem, vmem, vmem, vmem, vmem],
+        in_specs=[smem, smem, vmem, vmem, vmem],
         out_specs=pl.BlockSpec(memory_space=pltpu.HBM),
         scratch_shapes=[
             pltpu.VMEM((blocks, species, LANES), f32),
@@ -454,7 +469,7 @@
         ],
         compiler_params=pltpu.CompilerParams(vmem_limit_bytes=14 << 20),
         name="chemistry",
-    )(info, start, x, log_table, reac, both)
+    )(info, start, x, log_table, both)
 
 
 def place_kernel(firsts, parts, *rest):
@@ -572,13 +587,12 @@
         out_shape=(
             pltpu.HBM((peers, lines, LANES), f32),
             pltpu.VMEM((log_rate.shape[0], reactions, LANES), f32),
-            pltpu.VMEM((reactions, species), bf16),
-            pltpu.VMEM((2 * species, reactions), bf16),
+            pltpu.VMEM((3 * species, reactions), bf16),
         ),
         in_specs=[smem] + [hbm] * 4 + [vmem] * 3 + [
             pl.BlockSpec(v.shape, lambda i: (0, 0)) for v in (log_rate, reactants, products)
         ],
-        out_specs=(pl.BlockSpec((peers, lines, LANES), lambda i: (0, 0, 0)), vmem, vmem, vmem),
+        out_specs=(pl.BlockSpec((peers, lines, LANES), lambda i: (0, 0, 0)), vmem, vmem),
         scratch_shapes=[
             pltpu.SMEM((group,), f32),
             pltpu.VMEM((2, 2, group, slab_rows, LANES), f32),
@@ -592,7 +606,7 @@
             flops=20 * 10**9, transcendentals=0, bytes_accessed=10 << 20
         ),
         name="edges",
-    )(place, *in_hbm(diffusion), *fields, *in_vmem(before, after), *in_vmem(token), *in_hbm(log_rate, reactants, products))
+    )(place, *in_hbm(diffusion), *fields, before, after, *in_vmem(token), *in_hbm(log_rate, reactants, products))
 
     mine = lax.axis_index("species").astype(jnp.int32)
     exchange = functools.partial(

time: 110 us -> 111 us (level)
  waiting for transfers between devices: 32.4 us -> 39.6 us
  local copies, waits for them, and re-layouts: 5.95 us -> 0.08 us
  Pallas kernels: 46.6 us -> 44.7 us
    unnamed x14 -> x0, local copies, waits for them, and re-layouts: 5.87 us -> none
    all_to_all x2, waiting for transfers between devices: 11.1 us -> 15 us  [per_device(): gathered = exchange(slab)]
    all_to_all x2, waiting for transfers between devices: 21.3 us -> 24.5 us  [per_device(): done.append(exchange(reacted.reshape(peers, group, EDGE, LANES)))]
    pallas_call x2, Pallas kernels: 23.2 us -> 20.1 us  [chemistry(): pl.pallas_call(chemistry_kernel, out_shape=pltpu.HBM((species * blocks, L...]
    pallas_call x2, Pallas kernels: 2.18 us -> 3.41 us  [place_rows(): pl.pallas_call(functools.partial(place_kernel, firsts), out_shape=pltpu.H...]
  transfers between devices with their start and end apart: 6 -> 6, of which waited for: 4 -> 4; matrix products, arithmetic and copies ran while one was open for 0% -> 1% of each run, Pallas kernels for 41% -> 39%
where the time goes in v6:
time: 111 us; the launch traced here: 110 us
  Pallas kernels  44.7 us (40%)
  waiting for transfers between devices  39.6 us (36%)
  starting transfers between devices  24.2 us (22%)
    all_to_all x2, waiting for transfers between devices, per_device(): done.append(exchange(reacted.reshape(peers, group, EDGE, LANES)))  24.5 us
    pallas_call x2, Pallas kernels, chemistry(): pl.pallas_call(chemistry_kernel, out_shape=pltpu.HBM((species * blocks, L...  20.1 us
    all_to_all x2, waiting for transfers between devices, per_device(): gathered = exchange(slab)  15 us
    all_to_all x2, starting transfers between devices, per_device(): gathered = exchange(slab)  13.4 us
    pallas_call x1, Pallas kernels, per_device(): pl.pallas_call(edge_kernel, grid=(1,), out_shape=(pltpu.HBM((peers, lines...  11.4 us
    pallas_call x1, Pallas kernels, per_device(): pl.pallas_call(middle_kernel, grid=(1,), out_shape=(pltpu.HBM((peers, lin...  8.73 us
    all_to_all x2, starting transfers between devices, per_device(): done.append(exchange(reacted.reshape(peers, group, EDGE, LANES)))  8.18 us
    pallas_call x2, Pallas kernels, place_rows(): pl.pallas_call(functools.partial(place_kernel, firsts), out_shape=pltpu.H...  3.41 us
  transfers between devices with their start and end apart: 6, of which 4 were waited for; matrix products, arithmetic and copies ran while one was open for 1% of the time, Pallas kernels for 39%

profile of v6, /device:TPU:0, one launch (start us, length us, event | category | flops | bytes accessed | tf_op | source)
XLA Modules:
  0.0 109.8 jit_solution(4416429140071583822)
XLA Ops:
  0.0 1.1 rims.1
  1.1 1.3 %collective-permute-start = (f32[18,8,256]{2,1,0:T(8,128)S(1)}, f32[18,8,256]{2,1,0:T(8,128)S(1)}, u32[]{:S(2)}, u32[]{:S(2)}) collective-permute-start(f32[18,8,256]{2,1,0:T(8,128)S(1)} %get-tuple-element.13), channel_id=1, source_target_pairs={{0,16},{16,32},{32,48},{48,64},{64,80},{80,96},{96,112},{1,17},{17... | collective-permute-start | bytes 442376 | tf_op jit(solution)/shard_map/ppermute | solution.py:559
  2.4 1.3 %collective-permute-start.1 = (f32[18,8,256]{2,1,0:T(8,128)S(1)}, f32[18,8,256]{2,1,0:T(8,128)S(1)}, u32[]{:S(2)}, u32[]{:S(2)}) collective-permute-start(f32[18,8,256]{2,1,0:T(8,128)S(1)} %get-tuple-element.14), channel_id=1, source_target_pairs={{16,0},{32,16},{48,32},{64,48},{80,64},{96,80},{112,96},{17,1},{33... | collective-permute-start | bytes 442376 | tf_op jit(solution)/shard_map/ppermute | solution.py:560
  3.7 8.7 %middle.1 = (f32[16,136,128]{2,1,0:T(8,128)}, f32[8,128]{1,0:T(8,128)S(1)}) custom-call(f32[16]{0:T(128)} %diffuse_in.3, s32[16]{0:T(128)} %classes_in.1, s32[16]{0:T(128)} %slots_in.1, f32[16,128,256]{2,1,0:T(8,128)} %conc.5, f32[128,256]{1,0:T(8,128)} %cx.5, f32[128,256]{1,0:T(8,128)} %cy.5), custom_call_target="tpu_custom_call" | custom-call | tf_op jit(solution)/shard_map/middle/pallas_call | solution.py:562
  12.4 8.6 %all-to-all-start = ((f32[16,136,128]{2,1,0:T(8,128)}), f32[16,136,128]{2,1,0:T(8,128)}, u32[]{:S(2)}, u32[]{:S(2)}) async-start(f32[16,136,128]{2,1,0:T(8,128)} %get-tuple-element.12), calls=%async_computation | async-start | bytes 2228224 | tf_op jit(solution)/shard_map/all_to_all | solution.py:623
  21.1 0.1 pad_add_fusion.place
  21.1 0.0 collective-permute-done.before
  21.1 0.0 collective-permute-done.1.after
  21.1 11.4 %edges.1 = (f32[16,128,128]{2,1,0:T(8,128)}, f32[4,768,128]{2,1,0:T(8,128)S(1)}, bf16[768,768]{1,0:T(8,128)(2,1)S(1)}) custom-call(s32[2]{0:T(128)S(1)} %pad_add_fusion.place, f32[16]{0:T(128)} %diffuse_in.3, f32[16,128,256]{2,1,0:T(8,128)} %conc.5, f32[128,256]{1,0:T(8,128)} %cx.5, f32[128,256]{1,0:T(8,128)} %cy.5, ...), custom_call_target="tpu_custom_call" | custom-call | flops 20000000000 | bytes 10485760 | tf_op jit(solution)/shard_map/edges/pallas_call | solution.py:584
  32.6 6.7 %all-to-all-done.x = f32[16,136,128]{2,1,0:T(8,128)} async-done(((f32[16,136,128]{2,1,0:T(8,128)}), f32[16,136,128]{2,1,0:T(8,128)}, u32[]{:S(2)}, u32[]{:S(2)}) %all-to-all-start) | async-done | bytes 1114144 | tf_op jit(solution)/shard_map/all_to_all | solution.py:623
  39.3 4.8 %all-to-all-start.1 = ((f32[16,128,128]{2,1,0:T(8,128)}), f32[16,128,128]{2,1,0:T(8,128)}, u32[]{:S(2)}, u32[]{:S(2)}) async-start(f32[16,128,128]{2,1,0:T(8,128)} %get-tuple-element.16), calls=%async_computation.1 | async-start | bytes 2097152 | tf_op jit(solution)/shard_map/all_to_all | solution.py:623
  44.1 0.9 fusion
  45.0 0.1 convert_element_type.8.info
  45.1 11.6 %chemistry.3 = f32[2048,128]{1,0:T(8,128)} custom-call(s32[256]{0:T(256)S(1)} %convert_element_type.8.info, s32[8]{0:T(128)S(1)} %multiply_add_fusion.start, f32[16,136,128]{2,1,0:T(8,128)} %all-to-all-done.x, f32[4,768,128]{2,1,0:T(8,128)S(1)} %get-tuple-element.17.log_table, bf16[768,768]{1,0:T(8,128)(2,1)S(1)} %get-tuple-element.18.both), custom_call_target="tpu_custom_call" | custom-call | tf_op jit(solution)/shard_map/chemistry/pallas_call | solution.py:459
  56.7 8.4 %all-to-all-done.1.x = f32[16,128,128]{2,1,0:T(8,128)} async-done(((f32[16,128,128]{2,1,0:T(8,128)}), f32[16,128,128]{2,1,0:T(8,128)}, u32[]{:S(2)}, u32[]{:S(2)}) %all-to-all-start.1) | async-done | bytes 1048608 | tf_op jit(solution)/shard_map/all_to_all | solution.py:623
  65.0 4.5 %all-to-all-start.3 = ((f32[16,16,8,128]{3,2,1,0:T(8,128)}), f32[16,16,8,128]{3,2,1,0:T(8,128)}, u32[]{:S(2)}, u32[]{:S(2)}) async-start(f32[16,16,8,128]{3,2,1,0:T(8,128)} %bitcast.3), calls=%async_computation.3 | async-start | bytes 2097152 | tf_op jit(solution)/shard_map/all_to_all | solution.py:628
  69.6 8.4 %chemistry.2 = f32[2048,128]{1,0:T(8,128)} custom-call(s32[256]{0:T(256)S(1)} %convert_element_type.8.info, s32[8]{0:T(128)S(1)} %fusion.2.start, f32[16,128,128]{2,1,0:T(8,128)} %all-to-all-done.1.x, f32[4,768,128]{2,1,0:T(8,128)S(1)} %get-tuple-element.17.log_table, bf16[768,768]{1,0:T(8,128)(2,1)S(1)} %get-tuple-element.18.both), custom_call_target="tpu_custom_call" | custom-call | tf_op jit(solution)/shard_map/chemistry/pallas_call | solution.py:459
  78.0 9.5 %all-to-all-done.3.parts = f32[16,16,8,128]{3,2,1,0:T(8,128)} async-done(((f32[16,16,8,128]{3,2,1,0:T(8,128)}), f32[16,16,8,128]{3,2,1,0:T(8,128)}, u32[]{:S(2)}, u32[]{:S(2)}) %all-to-all-start.3) | async-done | bytes 1048608 | tf_op jit(solution)/shard_map/all_to_all | solution.py:628
  87.5 3.7 %all-to-all-start.2 = ((f32[16,16,8,128]{3,2,1,0:T(8,128)}), f32[16,16,8,128]{3,2,1,0:T(8,128)S(1)}, u32[]{:S(2)}, u32[]{:S(2)}) async-start(f32[16,16,8,128]{3,2,1,0:T(8,128)} %bitcast.4), calls=%async_computation.2 | async-start | bytes 2097152 | tf_op jit(solution)/shard_map/all_to_all | solution.py:628
  91.2 2.3 %place.2.rest_0_ = f32[16,128,256]{2,1,0:T(8,128)} custom-call(f32[16,16,8,128]{3,2,1,0:T(8,128)} %all-to-all-done.3.parts), custom_call_target="tpu_custom_call" | custom-call | tf_op jit(solution)/shard_map/place/pallas_call | solution.py:501
  93.5 15.1 %all-to-all-done.2.parts = f32[16,16,8,128]{3,2,1,0:T(8,128)S(1)} async-done(((f32[16,16,8,128]{3,2,1,0:T(8,128)}), f32[16,16,8,128]{3,2,1,0:T(8,128)S(1)}, u32[]{:S(2)}, u32[]{:S(2)}) %all-to-all-start.2) | async-done | bytes 1048608 | tf_op jit(solution)/shard_map/all_to_all | solution.py:628
  108.6 1.1 place.3
  (2 shorter events, 0.0 us)
Async XLA Ops:
  1.1 20.1 %collective-permute-start = (f32[18,8,256]{2,1,0:T(8,128)S(1)}, f32[18,8,256]{2,1,0:T(8,128)S(1)}, u32[]{:S(2)}, u32[]{:S(2)}) collective-permute-start(f32[18,8,256]{2,1,0:T(8,128)S(1)} %get-tuple-element.13), channel_id=1, source_target_pairs={{0,16},{16,32},{32,48},{48,64},{64,80},{80,96},{96,112},{1,17},{17... | collective-permute-start | bytes 442376 | tf_op jit(solution)/shard_map/ppermute | solution.py:559
  2.4 18.8 %collective-permute-start.1 = (f32[18,8,256]{2,1,0:T(8,128)S(1)}, f32[18,8,256]{2,1,0:T(8,128)S(1)}, u32[]{:S(2)}, u32[]{:S(2)}) collective-permute-start(f32[18,8,256]{2,1,0:T(8,128)S(1)} %get-tuple-element.14), channel_id=1, source_target_pairs={{16,0},{32,16},{48,32},{64,48},{80,64},{96,80},{112,96},{17,1},{33... | collective-permute-start | bytes 442376 | tf_op jit(solution)/shard_map/ppermute | solution.py:560
  12.4 26.9 %all-to-all-start = ((f32[16,136,128]{2,1,0:T(8,128)}), f32[16,136,128]{2,1,0:T(8,128)}, u32[]{:S(2)}, u32[]{:S(2)}) async-start(f32[16,136,128]{2,1,0:T(8,128)} %get-tuple-element.12), calls=%async_computation | async-start | bytes 2228224 | tf_op jit(solution)/shard_map/all_to_all | solution.py:623
  39.3 25.8 %all-to-all-start.1 = ((f32[16,128,128]{2,1,0:T(8,128)}), f32[16,128,128]{2,1,0:T(8,128)}, u32[]{:S(2)}, u32[]{:S(2)}) async-start(f32[16,128,128]{2,1,0:T(8,128)} %get-tuple-element.16), calls=%async_computation.1 | async-start | bytes 2097152 | tf_op jit(solution)/shard_map/all_to_all | solution.py:623
  65.0 22.5 %all-to-all-start.3 = ((f32[16,16,8,128]{3,2,1,0:T(8,128)}), f32[16,16,8,128]{3,2,1,0:T(8,128)}, u32[]{:S(2)}, u32[]{:S(2)}) async-start(f32[16,16,8,128]{3,2,1,0:T(8,128)} %bitcast.3), calls=%async_computation.3 | async-start | bytes 2097152 | tf_op jit(solution)/shard_map/all_to_all | solution.py:628
  87.5 21.1 %all-to-all-start.2 = ((f32[16,16,8,128]{3,2,1,0:T(8,128)}), f32[16,16,8,128]{3,2,1,0:T(8,128)S(1)}, u32[]{:S(2)}, u32[]{:S(2)}) async-start(f32[16,16,8,128]{3,2,1,0:T(8,128)} %bitcast.4), calls=%async_computation.2 | async-start | bytes 2097152 | tf_op jit(solution)/shard_map/all_to_all | solution.py:628

commit v7 on v6

--- a/solution.py
+++ b/solution.py
@@ -579,6 +579,8 @@
         name="middle",
     )(*in_hbm(diffusion, block_class, send_slot), *fields)
 
+    turn = lax.ppermute(token, "region", [(k, k + 1) for k in range(0, regions - 1, 2)])
+    first_part, turn = lax.optimization_barrier((middle, turn))
     place = jnp.stack([lax.axis_index("region"), jnp.int32(regions)]).astype(jnp.int32)
     slab_rows = rows // 4 + 2 * EDGE
     edges, *tables = pl.pallas_call(
@@ -606,7 +608,7 @@
             flops=20 * 10**9, transcendentals=0, bytes_accessed=10 << 20
         ),
         name="edges",
-    )(place, *in_hbm(diffusion), *fields, before, after, *in_vmem(token), *in_hbm(log_rate, reactants, products))
+    )(place, *in_hbm(diffusion), *fields, before, after, turn, *in_hbm(log_rate, reactants, products))
 
     mine = lax.axis_index("species").astype(jnp.int32)
     exchange = functools.partial(
@@ -617,7 +619,7 @@
     order = jnp.arange(EDGE, dtype=jnp.int32)
     half = peers // 2
     for slab, source in (
-        (middle, order + half // 2),
+        (first_part, order + half // 2),
         (edges, jnp.where(order < half // 2, order, order + half)),
     ):
         gathered = exchange(slab)

time: 111 us -> 108 us (0.973)
  waiting for transfers between devices: 39.6 us -> 33.1 us
  starting transfers between devices: 24.2 us -> 28 us
    ppermute x0 -> x1, starting transfers between devices: none -> 4.83 us  [per_device(): lax.ppermute(token, 'region', [(k, k + 1) for k in range(0, regions - 1,...]
    all_to_all x2, waiting for transfers between devices: 24.5 us -> 20.7 us  [per_device(): done.append(exchange(reacted.reshape(peers, group, EDGE, LANES)))]
    all_to_all x2, waiting for transfers between devices: 15 us -> 11.6 us  [per_device(): gathered = exchange(slab)]
  transfers between devices with their start and end apart: 6 -> 7, of which waited for: 4 -> 5; matrix products, arithmetic and copies ran while one was open for 1% -> 1% of each run, Pallas kernels for 39% -> 40%
where the time goes in v7:
time: 108 us; the launch traced here: 107 us
  Pallas kernels  44.7 us (41%)
  waiting for transfers between devices  33.1 us (31%)
  starting transfers between devices  28 us (26%)
    all_to_all x2, waiting for transfers between devices, per_device(): done.append(exchange(reacted.reshape(peers, group, EDGE, LANES)))  20.7 us
    pallas_call x2, Pallas kernels, chemistry(): pl.pallas_call(chemistry_kernel, out_shape=pltpu.HBM((species * blocks, L...  20.1 us
    all_to_all x2, starting transfers between devices, per_device(): gathered = exchange(slab)  12.4 us
    all_to_all x2, waiting for transfers between devices, per_device(): gathered = exchange(slab)  11.6 us
    pallas_call x1, Pallas kernels, per_device(): pl.pallas_call(edge_kernel, grid=(1,), out_shape=(pltpu.HBM((peers, lines...  11.5 us
    pallas_call x1, Pallas kernels, per_device(): pl.pallas_call(middle_kernel, grid=(1,), out_shape=(pltpu.HBM((peers, lin...  8.73 us
    all_to_all x2, starting transfers between devices, per_device(): done.append(exchange(reacted.reshape(peers, group, EDGE, LANES)))  8.17 us
    ppermute x1, starting transfers between devices, per_device(): lax.ppermute(token, 'region', [(k, k + 1) for k in range(0, regions - 1,...  4.83 us
  transfers between devices with their start and end apart: 7, of which 5 were waited for; matrix products, arithmetic and copies ran while one was open for 1% of the time, Pallas kernels for 40%

profile of v7, /device:TPU:0, one launch (start us, length us, event | category | flops | bytes accessed | tf_op | source)
XLA Modules:
  0.0 107.1 jit_solution(8263276944679915895)
XLA Ops:
  0.0 1.1 rims.1
  1.1 1.3 %collective-permute-start.1 = (f32[18,8,256]{2,1,0:T(8,128)S(1)}, f32[18,8,256]{2,1,0:T(8,128)S(1)}, u32[]{:S(2)}, u32[]{:S(2)}) collective-permute-start(f32[18,8,256]{2,1,0:T(8,128)S(1)} %get-tuple-element.17), channel_id=1, source_target_pairs={{0,16},{16,32},{32,48},{48,64},{64,80},{80,96},{96,112},{1,17},{17... | collective-permute-start | bytes 442376 | tf_op jit(solution)/shard_map/ppermute | solution.py:559
  2.4 1.3 %collective-permute-start.2 = (f32[18,8,256]{2,1,0:T(8,128)S(1)}, f32[18,8,256]{2,1,0:T(8,128)S(1)}, u32[]{:S(2)}, u32[]{:S(2)}) collective-permute-start(f32[18,8,256]{2,1,0:T(8,128)S(1)} %get-tuple-element.18), channel_id=1, source_target_pairs={{16,0},{32,16},{48,32},{64,48},{80,64},{96,80},{112,96},{17,1},{33... | collective-permute-start | bytes 442376 | tf_op jit(solution)/shard_map/ppermute | solution.py:560
  3.7 8.7 %middle.1 = (f32[16,136,128]{2,1,0:T(8,128)}, f32[8,128]{1,0:T(8,128)S(1)}) custom-call(f32[16]{0:T(128)} %diffuse_in.3, s32[16]{0:T(128)} %classes_in.1, s32[16]{0:T(128)} %slots_in.1, f32[16,128,256]{2,1,0:T(8,128)} %conc.5, f32[128,256]{1,0:T(8,128)} %cx.5, f32[128,256]{1,0:T(8,128)} %cy.5), custom_call_target="tpu_custom_call" | custom-call | tf_op jit(solution)/shard_map/middle/pallas_call | solution.py:562
  12.4 4.8 %collective-permute-start = (f32[8,128]{1,0:T(8,128)S(1)}, f32[8,128]{1,0:T(8,128)S(1)}, u32[]{:S(2)}, u32[]{:S(2)}) collective-permute-start(f32[8,128]{1,0:T(8,128)S(1)} %get-tuple-element.15), channel_id=1, source_target_pairs={{0,16},{32,48},{64,80},{96,112},{1,17},{33,49},{65,81},{97,113},{2... | collective-permute-start | bytes 12296 | tf_op jit(solution)/shard_map/ppermute | solution.py:582
  17.3 0.1 pad_add_fusion.place
  17.3 0.7 collective-permute-done._token
  18.1 8.1 %all-to-all-start = ((f32[16,136,128]{2,1,0:T(8,128)}), f32[16,136,128]{2,1,0:T(8,128)}, u32[]{:S(2)}, u32[]{:S(2)}) async-start(f32[16,136,128]{2,1,0:T(8,128)} %get-tuple-element.16), calls=%async_computation | async-start | bytes 2228224 | tf_op jit(solution)/shard_map/all_to_all | solution.py:625
  26.2 0.0 collective-permute-done.1.before
  26.2 0.0 collective-permute-done.2.after
  26.2 11.5 %edges.1 = (f32[16,128,128]{2,1,0:T(8,128)}, f32[4,768,128]{2,1,0:T(8,128)S(1)}, bf16[768,768]{1,0:T(8,128)(2,1)S(1)}) custom-call(s32[2]{0:T(128)S(1)} %pad_add_fusion.place, f32[16]{0:T(128)} %diffuse_in.3, f32[16,128,256]{2,1,0:T(8,128)} %conc.5, f32[128,256]{1,0:T(8,128)} %cx.5, f32[128,256]{1,0:T(8,128)} %cy.5, ...), custom_call_target="tpu_custom_call" | custom-call | flops 20000000000 | bytes 10485760 | tf_op jit(solution)/shard_map/edges/pallas_call | solution.py:586
  37.6 7.7 %all-to-all-done.x = f32[16,136,128]{2,1,0:T(8,128)} async-done(((f32[16,136,128]{2,1,0:T(8,128)}), f32[16,136,128]{2,1,0:T(8,128)}, u32[]{:S(2)}, u32[]{:S(2)}) %all-to-all-start) | async-done | bytes 1114144 | tf_op jit(solution)/shard_map/all_to_all | solution.py:625
  45.4 4.3 %all-to-all-start.1 = ((f32[16,128,128]{2,1,0:T(8,128)}), f32[16,128,128]{2,1,0:T(8,128)}, u32[]{:S(2)}, u32[]{:S(2)}) async-start(f32[16,128,128]{2,1,0:T(8,128)} %get-tuple-element.20), calls=%async_computation.1 | async-start | bytes 2097152 | tf_op jit(solution)/shard_map/all_to_all | solution.py:625
  49.7 0.9 fusion
  50.6 0.1 convert_element_type.8.info
  50.7 11.6 %chemistry.3 = f32[2048,128]{1,0:T(8,128)} custom-call(s32[256]{0:T(256)S(1)} %convert_element_type.8.info, s32[8]{0:T(128)S(1)} %multiply_add_fusion.start, f32[16,136,128]{2,1,0:T(8,128)} %all-to-all-done.x, f32[4,768,128]{2,1,0:T(8,128)S(1)} %get-tuple-element.21.log_table, bf16[768,768]{1,0:T(8,128)(2,1)S(1)} %get-tuple-element.22.both), custom_call_target="tpu_custom_call" | custom-call | tf_op jit(solution)/shard_map/chemistry/pallas_call | solution.py:459
  62.3 3.9 %all-to-all-done.1.x = f32[16,128,128]{2,1,0:T(8,128)} async-done(((f32[16,128,128]{2,1,0:T(8,128)}), f32[16,128,128]{2,1,0:T(8,128)}, u32[]{:S(2)}, u32[]{:S(2)}) %all-to-all-start.1) | async-done | bytes 1048608 | tf_op jit(solution)/shard_map/all_to_all | solution.py:625
  66.2 4.5 %all-to-all-start.3 = ((f32[16,16,8,128]{3,2,1,0:T(8,128)}), f32[16,16,8,128]{3,2,1,0:T(8,128)}, u32[]{:S(2)}, u32[]{:S(2)}) async-start(f32[16,16,8,128]{3,2,1,0:T(8,128)} %bitcast.3), calls=%async_computation.3 | async-start | bytes 2097152 | tf_op jit(solution)/shard_map/all_to_all | solution.py:630
  70.7 8.4 %chemistry.2 = f32[2048,128]{1,0:T(8,128)} custom-call(s32[256]{0:T(256)S(1)} %convert_element_type.8.info, s32[8]{0:T(128)S(1)} %fusion.2.start, f32[16,128,128]{2,1,0:T(8,128)} %all-to-all-done.1.x, f32[4,768,128]{2,1,0:T(8,128)S(1)} %get-tuple-element.21.log_table, bf16[768,768]{1,0:T(8,128)(2,1)S(1)} %get-tuple-element.22.both), custom_call_target="tpu_custom_call" | custom-call | tf_op jit(solution)/shard_map/chemistry/pallas_call | solution.py:459
  79.2 7.5 %all-to-all-done.3.parts = f32[16,16,8,128]{3,2,1,0:T(8,128)} async-done(((f32[16,16,8,128]{3,2,1,0:T(8,128)}), f32[16,16,8,128]{3,2,1,0:T(8,128)}, u32[]{:S(2)}, u32[]{:S(2)}) %all-to-all-start.3) | async-done | bytes 1048608 | tf_op jit(solution)/shard_map/all_to_all | solution.py:630
  86.7 3.7 %all-to-all-start.2 = ((f32[16,16,8,128]{3,2,1,0:T(8,128)}), f32[16,16,8,128]{3,2,1,0:T(8,128)S(1)}, u32[]{:S(2)}, u32[]{:S(2)}) async-start(f32[16,16,8,128]{3,2,1,0:T(8,128)} %bitcast.4), calls=%async_computation.2 | async-start | bytes 2097152 | tf_op jit(solution)/shard_map/all_to_all | solution.py:630
  90.3 2.3 %place.2.rest_0_ = f32[16,128,256]{2,1,0:T(8,128)} custom-call(f32[16,16,8,128]{3,2,1,0:T(8,128)} %all-to-all-done.3.parts), custom_call_target="tpu_custom_call" | custom-call | tf_op jit(solution)/shard_map/place/pallas_call | solution.py:501
  92.7 13.2 %all-to-all-done.2.parts = f32[16,16,8,128]{3,2,1,0:T(8,128)S(1)} async-done(((f32[16,16,8,128]{3,2,1,0:T(8,128)}), f32[16,16,8,128]{3,2,1,0:T(8,128)S(1)}, u32[]{:S(2)}, u32[]{:S(2)}) %all-to-all-start.2) | async-done | bytes 1048608 | tf_op jit(solution)/shard_map/all_to_all | solution.py:630
  105.9 1.1 place.3
  (2 shorter events, 0.0 us)
Async XLA Ops:
  1.1 25.1 %collective-permute-start.1 = (f32[18,8,256]{2,1,0:T(8,128)S(1)}, f32[18,8,256]{2,1,0:T(8,128)S(1)}, u32[]{:S(2)}, u32[]{:S(2)}) collective-permute-start(f32[18,8,256]{2,1,0:T(8,128)S(1)} %get-tuple-element.17), channel_id=1, source_target_pairs={{0,16},{16,32},{32,48},{48,64},{64,80},{80,96},{96,112},{1,17},{17... | collective-permute-start | bytes 442376 | tf_op jit(solution)/shard_map/ppermute | solution.py:559
  2.4 23.8 %collective-permute-start.2 = (f32[18,8,256]{2,1,0:T(8,128)S(1)}, f32[18,8,256]{2,1,0:T(8,128)S(1)}, u32[]{:S(2)}, u32[]{:S(2)}) collective-permute-start(f32[18,8,256]{2,1,0:T(8,128)S(1)} %get-tuple-element.18), channel_id=1, source_target_pairs={{16,0},{32,16},{48,32},{64,48},{80,64},{96,80},{112,96},{17,1},{33... | collective-permute-start | bytes 442376 | tf_op jit(solution)/shard_map/ppermute | solution.py:560
  12.4 5.6 %collective-permute-start = (f32[8,128]{1,0:T(8,128)S(1)}, f32[8,128]{1,0:T(8,128)S(1)}, u32[]{:S(2)}, u32[]{:S(2)}) collective-permute-start(f32[8,128]{1,0:T(8,128)S(1)} %get-tuple-element.15), channel_id=1, source_target_pairs={{0,16},{32,48},{64,80},{96,112},{1,17},{33,49},{65,81},{97,113},{2... | collective-permute-start | bytes 12296 | tf_op jit(solution)/shard_map/ppermute | solution.py:582
  18.1 27.3 %all-to-all-start = ((f32[16,136,128]{2,1,0:T(8,128)}), f32[16,136,128]{2,1,0:T(8,128)}, u32[]{:S(2)}, u32[]{:S(2)}) async-start(f32[16,136,128]{2,1,0:T(8,128)} %get-tuple-element.16), calls=%async_computation | async-start | bytes 2228224 | tf_op jit(solution)/shard_map/all_to_all | solution.py:625
  45.4 20.8 %all-to-all-start.1 = ((f32[16,128,128]{2,1,0:T(8,128)}), f32[16,128,128]{2,1,0:T(8,128)}, u32[]{:S(2)}, u32[]{:S(2)}) async-start(f32[16,128,128]{2,1,0:T(8,128)} %get-tuple-element.20), calls=%async_computation.1 | async-start | bytes 2097152 | tf_op jit(solution)/shard_map/all_to_all | solution.py:625
  66.2 20.5 %all-to-all-start.3 = ((f32[16,16,8,128]{3,2,1,0:T(8,128)}), f32[16,16,8,128]{3,2,1,0:T(8,128)}, u32[]{:S(2)}, u32[]{:S(2)}) async-start(f32[16,16,8,128]{3,2,1,0:T(8,128)} %bitcast.3), calls=%async_computation.3 | async-start | bytes 2097152 | tf_op jit(solution)/shard_map/all_to_all | solution.py:630
  86.7 19.2 %all-to-all-start.2 = ((f32[16,16,8,128]{3,2,1,0:T(8,128)}), f32[16,16,8,128]{3,2,1,0:T(8,128)S(1)}, u32[]{:S(2)}, u32[]{:S(2)}) async-start(f32[16,16,8,128]{3,2,1,0:T(8,128)} %bitcast.4), calls=%async_computation.2 | async-start | bytes 2097152 | tf_op jit(solution)/shard_map/all_to_all | solution.py:630

commit v8 on v7

--- a/solution.py
+++ b/solution.py
@@ -401,17 +401,43 @@
     )(log_rate, reactants, products)
 
 
-def chemistry_kernel(info, start, x, log_table, both, out, result, answer, listed, sem):
-    peers, blocks = x.shape[0], EDGE
-    species = both.shape[0] // 3
-    group = species // peers
-    codes = [info[start[b]] for b in range(blocks)]
+def code_class(code):
+    return sum((code >= float(k)).astype(jnp.int32) for k in (5, 6, 7))
+
+
+def chemistry_kernel(
+    sources, mine, x_in, coded, log_table, both, out, x, codes, result, answer, listed, sems
+):
+    peers, lines, _ = x.shape
+    blocks = EDGE
+    group = lines // blocks
+    species = peers * group
+    size = TILE * group
+
+    def part(i):
+        at = pl.ds(first_line(i, size), size)
+        return pltpu.make_async_copy(x_in.at[:, at, :], x.at[:, at, :], sems.at[i])
+
+    copies = []
+    for first, count, at in sources:
+        copies.append(
+            pltpu.make_async_copy(
+                coded.at[pl.ds(first, count), pl.ds(lines, EDGE), :],
+                codes.at[pl.ds(at, count)],
+                sems.at[blocks // TILE + len(copies)],
+            )
+        )
+    start_all(copies + [part(i) for i in range(blocks // TILE)])
+    wait_all(copies)
     count = jnp.int32(0)
     for b in range(blocks):
-        listed[1, b] = lax.bitwise_and(codes[b], 3)
-        listed[2, b] = lax.shift_right_logical(codes[b], 2)
+        code = codes[b, 0, mine[0]]
+        stiff = (code >= 4.0).astype(jnp.int32)
+        lower = sum((code >= float(k)).astype(jnp.int32) for k in (1, 2, 3))
+        listed[1, b] = jnp.where(code >= 4.0, code_class(code), lower)
+        listed[2, b] = stiff
         listed[0, count] = b
-        count = count + lax.shift_right_logical(codes[b], 2)
+        count = count + stiff
 
     def tile(chosen, first):
         states, logs, lengths = [], [], []
@@ -438,6 +464,7 @@
 
     @pl.loop(0, blocks // TILE)
     def _(i):
+        part(i).wait()
         tile([i * TILE + j for j in range(TILE)], True)
 
     for _ in range(SUB - 1):
@@ -447,29 +474,33 @@
             tile([listed[0, jnp.minimum(i * TILE + j, count - 1)] for j in range(TILE)], False)
 
 
-    copy = pltpu.make_async_copy(answer, out, sem)
+    copy = pltpu.make_async_copy(answer, out, sems.at[0])
     copy.start()
     copy.wait()
 
 
-def chemistry(x, info, start, log_table, both):
+def chemistry(x, coded, sources, mine, log_table, both):
+    peers = x.shape[0]
     species, blocks = both.shape[0] // 3, EDGE
     vmem = pl.BlockSpec(memory_space=pltpu.VMEM)
     smem = pl.BlockSpec(memory_space=pltpu.SMEM)
+    hbm = pl.BlockSpec(memory_space=pltpu.HBM)
     return pl.pallas_call(
-        chemistry_kernel,
+        functools.partial(chemistry_kernel, sources),
         out_shape=pltpu.HBM((species * blocks, LANES), f32),
-        in_specs=[smem, smem, vmem, vmem, vmem],
-        out_specs=pl.BlockSpec(memory_space=pltpu.HBM),
+        in_specs=[smem, hbm, hbm, vmem, vmem],
+        out_specs=hbm,
         scratch_shapes=[
+            pltpu.VMEM((peers, species // peers * blocks, LANES), f32),
+            pltpu.SMEM((blocks, EDGE, LANES), f32),
             pltpu.VMEM((blocks, species, LANES), f32),
             pltpu.VMEM((species * blocks, LANES), f32),
             pltpu.SMEM((3, blocks), jnp.int32),
-            pltpu.SemaphoreType.DMA,
+            pltpu.SemaphoreType.DMA((blocks // TILE + len(sources),)),
         ],
         compiler_params=pltpu.CompilerParams(vmem_limit_bytes=14 << 20),
         name="chemistry",
-    )(info, start, x, log_table, both)
+    )(mine, x, coded, log_table, both)
 
 
 def place_kernel(firsts, parts, *rest):
@@ -610,23 +641,21 @@
         name="edges",
     )(place, *in_hbm(diffusion), *fields, before, after, turn, *in_hbm(log_rate, reactants, products))
 
-    mine = lax.axis_index("species").astype(jnp.int32)
+    mine = lax.axis_index("species").astype(jnp.int32).reshape(1)
     exchange = functools.partial(
         lax.all_to_all, axis_name="species", split_axis=0, concat_axis=0, tiled=True
     )
-    info = None
     done = []
-    order = jnp.arange(EDGE, dtype=jnp.int32)
+    coded = None
     half = peers // 2
-    for slab, source in (
-        (first_part, order + half // 2),
-        (edges, jnp.where(order < half // 2, order, order + half)),
+    quarter = half // 2
+    for slab, sources in (
+        (first_part, ((quarter, half, 0),)),
+        (edges, ((0, quarter, 0), (half + quarter, quarter, quarter))),
     ):
-        gathered = exchange(slab)
-        if info is None:
-            info = gathered[:, lines, : 2 * EDGE].astype(jnp.int32).reshape(-1)
-        start = source * 2 * EDGE + mine
-        reacted = chemistry(*in_vmem(gathered), info, start, *in_vmem(*tables))
+        (gathered,) = in_hbm(exchange(slab))
+        coded = gathered if coded is None else coded
+        reacted = chemistry(gathered, coded, sources, mine, *in_vmem(*tables))
         done.append(exchange(reacted.reshape(peers, group, EDGE, LANES)))
     quarter = rows // 4
     filled = place_rows(done[0], (quarter,), rows)

time: 108 us -> 108 us (level)
  transfers between devices with their start and end apart: 7 -> 7, of which waited for: 5 -> 5; matrix products, arithmetic and copies ran while one was open for 1% -> 0% of each run, Pallas kernels for 40% -> 40%
where the time goes in v8:
time: 108 us; the launch traced here: 107 us
  Pallas kernels  44.8 us (41%)
  waiting for transfers between devices  33.9 us (31%)
  starting transfers between devices  28 us (26%)
    all_to_all x2, waiting for transfers between devices, per_device(): done.append(exchange(reacted.reshape(peers, group, EDGE, LANES)))  20.6 us
    pallas_call x2, Pallas kernels, chemistry(): pl.pallas_call(functools.partial(chemistry_kernel, sources), out_shape=pl...  20.1 us
    all_to_all x2, waiting for transfers between devices, per_device(): gathered, = in_hbm(exchange(slab))  12.6 us
    all_to_all x2, starting transfers between devices, per_device(): gathered, = in_hbm(exchange(slab))  12.4 us
    pallas_call x1, Pallas kernels, per_device(): pl.pallas_call(edge_kernel, grid=(1,), out_shape=(pltpu.HBM((peers, lines...  11.4 us
    pallas_call x1, Pallas kernels, per_device(): pl.pallas_call(middle_kernel, grid=(1,), out_shape=(pltpu.HBM((peers, lin...  8.73 us
    all_to_all x2, starting transfers between devices, per_device(): done.append(exchange(reacted.reshape(peers, group, EDGE, LANES)))  8.18 us
    ppermute x1, starting transfers between devices, per_device(): lax.ppermute(token, 'region', [(k, k + 1) for k in range(0, regions - 1,...  4.83 us
  transfers between devices with their start and end apart: 7, of which 5 were waited for; matrix products, arithmetic and copies ran while one was open for 0% of the time, Pallas kernels for 40%

profile of v8, /device:TPU:0, one launch (start us, length us, event | category | flops | bytes accessed | tf_op | source)
XLA Modules:
  0.0 107.1 jit_solution(10640334604727806553)
XLA Ops:
  0.0 1.1 rims.1
  1.1 1.3 %collective-permute-start = (f32[18,8,256]{2,1,0:T(8,128)S(1)}, f32[18,8,256]{2,1,0:T(8,128)S(1)}, u32[]{:S(2)}, u32[]{:S(2)}) collective-permute-start(f32[18,8,256]{2,1,0:T(8,128)S(1)} %get-tuple-element.14), channel_id=1, source_target_pairs={{0,16},{16,32},{32,48},{48,64},{64,80},{80,96},{96,112},{1,17},{17... | collective-permute-start | bytes 442376 | tf_op jit(solution)/shard_map/ppermute | solution.py:590
  2.4 1.3 %collective-permute-start.1 = (f32[18,8,256]{2,1,0:T(8,128)S(1)}, f32[18,8,256]{2,1,0:T(8,128)S(1)}, u32[]{:S(2)}, u32[]{:S(2)}) collective-permute-start(f32[18,8,256]{2,1,0:T(8,128)S(1)} %get-tuple-element.15), channel_id=1, source_target_pairs={{16,0},{32,16},{48,32},{64,48},{80,64},{96,80},{112,96},{17,1},{33... | collective-permute-start | bytes 442376 | tf_op jit(solution)/shard_map/ppermute | solution.py:591
  3.7 8.7 %middle.1 = (f32[16,136,128]{2,1,0:T(8,128)}, f32[8,128]{1,0:T(8,128)S(1)}) custom-call(f32[16]{0:T(128)} %diffuse_in.3, s32[16]{0:T(128)} %classes_in.1, s32[16]{0:T(128)} %slots_in.1, f32[16,128,256]{2,1,0:T(8,128)} %conc.5, f32[128,256]{1,0:T(8,128)} %cx.5, f32[128,256]{1,0:T(8,128)} %cy.5), custom_call_target="tpu_custom_call" | custom-call | tf_op jit(solution)/shard_map/middle/pallas_call | solution.py:593
  12.4 4.8 %collective-permute-start.2 = (f32[8,128]{1,0:T(8,128)S(1)}, f32[8,128]{1,0:T(8,128)S(1)}, u32[]{:S(2)}, u32[]{:S(2)}) collective-permute-start(f32[8,128]{1,0:T(8,128)S(1)} %get-tuple-element.17), channel_id=1, source_target_pairs={{0,16},{32,48},{64,80},{96,112},{1,17},{33,49},{65,81},{97,113},{2... | collective-permute-start | bytes 12296 | tf_op jit(solution)/shard_map/ppermute | solution.py:613
  17.3 0.1 pad_add_fusion.place
  17.3 0.7 collective-permute-done.2._token
  18.1 8.1 %all-to-all-start.1 = ((f32[16,136,128]{2,1,0:T(8,128)}), f32[16,136,128]{2,1,0:T(8,128)}, u32[]{:S(2)}, u32[]{:S(2)}) async-start(f32[16,136,128]{2,1,0:T(8,128)} %get-tuple-element.20), calls=%async_computation.1 | async-start | bytes 2228224 | tf_op jit(solution)/shard_map/all_to_all | solution.py:656
  26.2 0.0 collective-permute-done.before
  26.2 0.0 collective-permute-done.1.after
  26.2 11.4 %edges.1 = (f32[16,128,128]{2,1,0:T(8,128)}, f32[4,768,128]{2,1,0:T(8,128)S(1)}, bf16[768,768]{1,0:T(8,128)(2,1)S(1)}) custom-call(s32[2]{0:T(128)S(1)} %pad_add_fusion.place, f32[16]{0:T(128)} %diffuse_in.3, f32[16,128,256]{2,1,0:T(8,128)} %conc.5, f32[128,256]{1,0:T(8,128)} %cx.5, f32[128,256]{1,0:T(8,128)} %cy.5, ...), custom_call_target="tpu_custom_call" | custom-call | flops 20000000000 | bytes 10485760 | tf_op jit(solution)/shard_map/edges/pallas_call | solution.py:617
  37.6 7.8 %all-to-all-done.1.coded.x_in = f32[16,136,128]{2,1,0:T(8,128)} async-done(((f32[16,136,128]{2,1,0:T(8,128)}), f32[16,136,128]{2,1,0:T(8,128)}, u32[]{:S(2)}, u32[]{:S(2)}) %all-to-all-start.1) | async-done | bytes 1114144 | tf_op jit(solution)/shard_map/all_to_all | solution.py:656
  45.4 4.3 %all-to-all-start = ((f32[16,128,128]{2,1,0:T(8,128)}), f32[16,128,128]{2,1,0:T(8,128)}, u32[]{:S(2)}, u32[]{:S(2)}) async-start(f32[16,128,128]{2,1,0:T(8,128)} %get-tuple-element.19), calls=%async_computation | async-start | bytes 2097152 | tf_op jit(solution)/shard_map/all_to_all | solution.py:656
  49.7 11.6 %chemistry.3 = f32[2048,128]{1,0:T(8,128)} custom-call(s32[1]{0:T(128)} %bitcast.mine, f32[16,136,128]{2,1,0:T(8,128)} %all-to-all-done.1.coded.x_in, f32[16,136,128]{2,1,0:T(8,128)} %all-to-all-done.1.coded.x_in, f32[4,768,128]{2,1,0:T(8,128)S(1)} %get-tuple-element.21.log_table, bf16[768,768]{1,0:T(8,128)(2,1)S(1)} %get-tuple-element.22.both), custom_call_target="tpu_custom_call" | custom-call | tf_op jit(solution)/shard_map/chemistry/pallas_call | solution.py:488
  61.4 4.8 %all-to-all-done.x_in = f32[16,128,128]{2,1,0:T(8,128)} async-done(((f32[16,128,128]{2,1,0:T(8,128)}), f32[16,128,128]{2,1,0:T(8,128)}, u32[]{:S(2)}, u32[]{:S(2)}) %all-to-all-start) | async-done | bytes 1048608 | tf_op jit(solution)/shard_map/all_to_all | solution.py:656
  66.2 4.5 %all-to-all-start.3 = ((f32[16,16,8,128]{3,2,1,0:T(8,128)}), f32[16,16,8,128]{3,2,1,0:T(8,128)}, u32[]{:S(2)}, u32[]{:S(2)}) async-start(f32[16,16,8,128]{3,2,1,0:T(8,128)} %bitcast.5), calls=%async_computation.3 | async-start | bytes 2097152 | tf_op jit(solution)/shard_map/all_to_all | solution.py:659
  70.7 8.5 %chemistry.2 = f32[2048,128]{1,0:T(8,128)} custom-call(s32[1]{0:T(128)} %bitcast.mine, f32[16,128,128]{2,1,0:T(8,128)} %all-to-all-done.x_in, f32[16,136,128]{2,1,0:T(8,128)} %all-to-all-done.1.coded.x_in, f32[4,768,128]{2,1,0:T(8,128)S(1)} %get-tuple-element.21.log_table, bf16[768,768]{1,0:T(8,128)(2,1)S(1)} %get-tuple-element.22.both), custom_call_target="tpu_custom_call" | custom-call | tf_op jit(solution)/shard_map/chemistry/pallas_call | solution.py:488
  79.3 7.4 %all-to-all-done.3.parts = f32[16,16,8,128]{3,2,1,0:T(8,128)} async-done(((f32[16,16,8,128]{3,2,1,0:T(8,128)}), f32[16,16,8,128]{3,2,1,0:T(8,128)}, u32[]{:S(2)}, u32[]{:S(2)}) %all-to-all-start.3) | async-done | bytes 1048608 | tf_op jit(solution)/shard_map/all_to_all | solution.py:659
  86.7 3.7 %all-to-all-start.2 = ((f32[16,16,8,128]{3,2,1,0:T(8,128)}), f32[16,16,8,128]{3,2,1,0:T(8,128)S(1)}, u32[]{:S(2)}, u32[]{:S(2)}) async-start(f32[16,16,8,128]{3,2,1,0:T(8,128)} %bitcast.4), calls=%async_computation.2 | async-start | bytes 2097152 | tf_op jit(solution)/shard_map/all_to_all | solution.py:659
  90.3 2.3 %place.2.rest_0_ = f32[16,128,256]{2,1,0:T(8,128)} custom-call(f32[16,16,8,128]{3,2,1,0:T(8,128)} %all-to-all-done.3.parts), custom_call_target="tpu_custom_call" | custom-call | tf_op jit(solution)/shard_map/place/pallas_call | solution.py:532
  92.7 13.2 %all-to-all-done.2.parts = f32[16,16,8,128]{3,2,1,0:T(8,128)S(1)} async-done(((f32[16,16,8,128]{3,2,1,0:T(8,128)}), f32[16,16,8,128]{3,2,1,0:T(8,128)S(1)}, u32[]{:S(2)}, u32[]{:S(2)}) %all-to-all-start.2) | async-done | bytes 1048608 | tf_op jit(solution)/shard_map/all_to_all | solution.py:659
  105.9 1.1 place.3
Async XLA Ops:
  1.1 25.1 %collective-permute-start = (f32[18,8,256]{2,1,0:T(8,128)S(1)}, f32[18,8,256]{2,1,0:T(8,128)S(1)}, u32[]{:S(2)}, u32[]{:S(2)}) collective-permute-start(f32[18,8,256]{2,1,0:T(8,128)S(1)} %get-tuple-element.14), channel_id=1, source_target_pairs={{0,16},{16,32},{32,48},{48,64},{64,80},{80,96},{96,112},{1,17},{17... | collective-permute-start | bytes 442376 | tf_op jit(solution)/shard_map/ppermute | solution.py:590
  2.4 23.8 %collective-permute-start.1 = (f32[18,8,256]{2,1,0:T(8,128)S(1)}, f32[18,8,256]{2,1,0:T(8,128)S(1)}, u32[]{:S(2)}, u32[]{:S(2)}) collective-permute-start(f32[18,8,256]{2,1,0:T(8,128)S(1)} %get-tuple-element.15), channel_id=1, source_target_pairs={{16,0},{32,16},{48,32},{64,48},{80,64},{96,80},{112,96},{17,1},{33... | collective-permute-start | bytes 442376 | tf_op jit(solution)/shard_map/ppermute | solution.py:591
  12.4 5.6 %collective-permute-start.2 = (f32[8,128]{1,0:T(8,128)S(1)}, f32[8,128]{1,0:T(8,128)S(1)}, u32[]{:S(2)}, u32[]{:S(2)}) collective-permute-start(f32[8,128]{1,0:T(8,128)S(1)} %get-tuple-element.17), channel_id=1, source_target_pairs={{0,16},{32,48},{64,80},{96,112},{1,17},{33,49},{65,81},{97,113},{2... | collective-permute-start | bytes 12296 | tf_op jit(solution)/shard_map/ppermute | solution.py:613
  18.1 27.3 %all-to-all-start.1 = ((f32[16,136,128]{2,1,0:T(8,128)}), f32[16,136,128]{2,1,0:T(8,128)}, u32[]{:S(2)}, u32[]{:S(2)}) async-start(f32[16,136,128]{2,1,0:T(8,128)} %get-tuple-element.20), calls=%async_computation.1 | async-start | bytes 2228224 | tf_op jit(solution)/shard_map/all_to_all | solution.py:656
  45.4 20.8 %all-to-all-start = ((f32[16,128,128]{2,1,0:T(8,128)}), f32[16,128,128]{2,1,0:T(8,128)}, u32[]{:S(2)}, u32[]{:S(2)}) async-start(f32[16,128,128]{2,1,0:T(8,128)} %get-tuple-element.19), calls=%async_computation | async-start | bytes 2097152 | tf_op jit(solution)/shard_map/all_to_all | solution.py:656
  66.2 20.5 %all-to-all-start.3 = ((f32[16,16,8,128]{3,2,1,0:T(8,128)}), f32[16,16,8,128]{3,2,1,0:T(8,128)}, u32[]{:S(2)}, u32[]{:S(2)}) async-start(f32[16,16,8,128]{3,2,1,0:T(8,128)} %bitcast.5), calls=%async_computation.3 | async-start | bytes 2097152 | tf_op jit(solution)/shard_map/all_to_all | solution.py:659
  86.7 19.2 %all-to-all-start.2 = ((f32[16,16,8,128]{3,2,1,0:T(8,128)}), f32[16,16,8,128]{3,2,1,0:T(8,128)S(1)}, u32[]{:S(2)}, u32[]{:S(2)}) async-start(f32[16,16,8,128]{3,2,1,0:T(8,128)} %bitcast.4), calls=%async_computation.2 | async-start | bytes 2097152 | tf_op jit(solution)/shard_map/all_to_all | solution.py:659

commit v9 on v8

--- a/solution.py
+++ b/solution.py
@@ -248,6 +248,8 @@
     log_rate,
     reactants,
     products,
+    early_log_table,
+    early_both,
     out,
     log_table,
     both,
@@ -282,7 +284,20 @@
             copy(conc.at[:, pl.ds(own_first, own), lanes], dst.at[:, pl.ds(own_at, own)])
             copy(halo.at[pl.ds(0, group), :, lanes], dst.at[:, pl.ds(halo_at, EDGE)])
     start_all(copies)
-    table_kernel(log_rate, reactants, products, log_table, both)
+
+    @pl.when(lax.rem(place[0], 2) == 1)
+    def _():
+        table_kernel(log_rate, reactants, products, log_table, both)
+
+    @pl.when(lax.rem(place[0], 2) == 0)
+    def _():
+        early = [
+            pltpu.make_async_copy(src, dst, sems.at[len(copies) + k])
+            for k, (src, dst) in enumerate(((early_log_table, log_table), (early_both, both)))
+        ]
+        start_all(early)
+        wait_all(early)
+
     wait_all(copies)
     nu = spread_species(diffuse, group)
 
@@ -349,6 +364,28 @@
     return g
 
 
+def turn_kernel(place, _turn, log_rate_in, reactants_in, products_in, log_table, both, *rest):
+    buffers, made, sems = rest[:3], rest[3:5], rest[5]
+
+    @pl.when(lax.rem(place[0], 2) == 0)
+    def _():
+        copies = [
+            pltpu.make_async_copy(src, dst, sems.at[k])
+            for k, (src, dst) in enumerate(
+                zip((log_rate_in, reactants_in, products_in), buffers)
+            )
+        ]
+        start_all(copies)
+        wait_all(copies)
+        table_kernel(*buffers, *made)
+        copies = [
+            pltpu.make_async_copy(src, dst, sems.at[k])
+            for k, (src, dst) in enumerate(zip(made, (log_table, both)))
+        ]
+        start_all(copies)
+        wait_all(copies)
+
+
 def first_line(block, group):
     return block * group if isinstance(block, int) else pl.multiple_of(block * group, group)
 
@@ -362,6 +399,28 @@
         both[2 * species :, k : k + species] = reactant[:, k : k + species].T.astype(bf16)
     for k in range(log_rate.shape[0]):
         log_table[k] = jnp.broadcast_to(log_rate[k : k + 1, :], (LANES, reactions)).T
+
+
+def turn_kernel(place, _turn, log_rate_in, reactants_in, products_in, log_table, both, *rest):
+    buffers, made, sems = rest[:3], rest[3:5], rest[5]
+
+    @pl.when(lax.rem(place[0], 2) == 0)
+    def _():
+        copies = [
+            pltpu.make_async_copy(src, dst, sems.at[k])
+            for k, (src, dst) in enumerate(
+                zip((log_rate_in, reactants_in, products_in), buffers)
+            )
+        ]
+        start_all(copies)
+        wait_all(copies)
+        table_kernel(*buffers, *made)
+        copies = [
+            pltpu.make_async_copy(src, dst, sems.at[k])
+            for k, (src, dst) in enumerate(zip(made, (log_table, both)))
+        ]
+        start_all(copies)
+        wait_all(copies)
 
 
 def first_line(block, group):
@@ -610,21 +669,40 @@
         name="middle",
     )(*in_hbm(diffusion, block_class, send_slot), *fields)
 
-    turn = lax.ppermute(token, "region", [(k, k + 1) for k in range(0, regions - 1, 2)])
-    first_part, turn = lax.optimization_barrier((middle, turn))
+    turn = lax.ppermute(token, "region", [(k + 1, k) for k in range(0, regions - 1, 2)])
     place = jnp.stack([lax.axis_index("region"), jnp.int32(regions)]).astype(jnp.int32)
+    table_inputs = in_hbm(log_rate, reactants, products)
+    table_shapes = (
+        pltpu.VMEM((log_rate.shape[0], reactions, LANES), f32),
+        pltpu.VMEM((3 * species, reactions), bf16),
+    )
+    early = pl.pallas_call(
+        turn_kernel,
+        out_shape=(
+            pltpu.HBM((log_rate.shape[0], reactions, LANES), f32),
+            pltpu.HBM((3 * species, reactions), bf16),
+        ),
+        in_specs=[smem, vmem, hbm, hbm, hbm],
+        out_specs=(hbm, hbm),
+        scratch_shapes=[
+            *[pltpu.VMEM(v.shape, v.dtype) for v in (log_rate, reactants, products)],
+            *table_shapes,
+            pltpu.SemaphoreType.DMA((3,)),
+        ],
+        name="turn",
+    )(place, *in_vmem(turn), *table_inputs)
+    first_part, *early = lax.optimization_barrier((middle, *early))
     slab_rows = rows // 4 + 2 * EDGE
     edges, *tables = pl.pallas_call(
         edge_kernel,
         grid=(1,),
         out_shape=(
             pltpu.HBM((peers, lines, LANES), f32),
-            pltpu.VMEM((log_rate.shape[0], reactions, LANES), f32),
-            pltpu.VMEM((3 * species, reactions), bf16),
+            *table_shapes,
         ),
         in_specs=[smem] + [hbm] * 4 + [vmem] * 3 + [
             pl.BlockSpec(v.shape, lambda i: (0, 0)) for v in (log_rate, reactants, products)
-        ],
+        ] + [hbm, hbm],
         out_specs=(pl.BlockSpec((peers, lines, LANES), lambda i: (0, 0, 0)), vmem, vmem),
         scratch_shapes=[
             pltpu.SMEM((group,), f32),
@@ -632,14 +710,14 @@
             pltpu.VMEM((2, slab_rows, columns), f32),
             pltpu.VMEM((2, slab_rows, columns), f32),
             *buffers(slab_rows),
-            pltpu.SemaphoreType.DMA((17,)),
+            pltpu.SemaphoreType.DMA((19,)),
         ],
         compiler_params=pltpu.CompilerParams(vmem_limit_bytes=24 << 20),
         cost_estimate=pl.CostEstimate(
             flops=20 * 10**9, transcendentals=0, bytes_accessed=10 << 20
         ),
         name="edges",
-    )(place, *in_hbm(diffusion), *fields, before, after, turn, *in_hbm(log_rate, reactants, products))
+    )(place, *in_hbm(diffusion), *fields, before, after, token, *table_inputs, *in_hbm(*early))
 
     mine = lax.axis_index("species").astype(jnp.int32).reshape(1)
     exchange = functools.partial(

time: 108 us -> 104 us (0.963)
  the two profiles are of different devices: /device:TPU:0 before, /device:TPU:2 now
where the time goes in v9:
time: 104 us; the launch traced here: 103 us
  Pallas kernels  53.7 us (52%)
  starting transfers between devices  30.9 us (30%)
  waiting for transfers between devices  17.9 us (17%)
    pallas_call x2, Pallas kernels, chemistry(): pl.pallas_call(functools.partial(chemistry_kernel, sources), out_shape=pl...  23.7 us
    all_to_all x2, starting transfers between devices, per_device(): gathered, = in_hbm(exchange(slab))  12.5 us
    all_to_all x2, waiting for transfers between devices, per_device(): done.append(exchange(reacted.reshape(peers, group, EDGE, LANES)))  12.5 us
    pallas_call x1, Pallas kernels, per_device(): pl.pallas_call(edge_kernel, grid=(1,), out_shape=(pltpu.HBM((peers, lines...  12.4 us
    all_to_all x2, starting transfers between devices, per_device(): done.append(exchange(reacted.reshape(peers, group, EDGE, LANES)))  11.5 us
    pallas_call x1, Pallas kernels, per_device(): pl.pallas_call(middle_kernel, grid=(1,), out_shape=(pltpu.HBM((peers, lin...  8.75 us
    pallas_call x1, Pallas kernels, per_device(): pl.pallas_call(turn_kernel, out_shape=(pltpu.HBM((log_rate.shape[0], reac...  4.31 us
    all_to_all x2, waiting for transfers between devices, per_device(): gathered, = in_hbm(exchange(slab))  4.26 us
  transfers between devices with their start and end apart: 7, of which 5 were waited for; matrix products, arithmetic and copies ran while one was open for 1% of the time, Pallas kernels for 50%

profile of v9, /device:TPU:2, one launch (start us, length us, event | category | flops | bytes accessed | tf_op | source)
XLA Modules:
  0.0 103.3 jit_solution(17605745130333898708)
XLA Ops:
  0.0 1.1 %rims.1 = (f32[18,8,256]{2,1,0:T(8,128)S(1)}, f32[18,8,256]{2,1,0:T(8,128)S(1)}) custom-call(f32[16,128,256]{2,1,0:T(8,128)} %conc.5, f32[128,256]{1,0:T(8,128)} %cx.5, f32[128,256]{1,0:T(8,128)} %cy.5), custom_call_target="tpu_custom_call" | custom-call | tf_op jit(solution)/shard_map/rims/pallas_call | solution.py:641
  1.1 1.9 %collective-permute-start = (f32[18,8,256]{2,1,0:T(8,128)S(1)}, f32[18,8,256]{2,1,0:T(8,128)S(1)}, u32[]{:S(2)}, u32[]{:S(2)}) collective-permute-start(f32[18,8,256]{2,1,0:T(8,128)S(1)} %get-tuple-element.17), channel_id=1, source_target_pairs={{0,16},{16,32},{32,48},{48,64},{64,80},{80,96},{96,112},{1,17},{17... | collective-permute-start | bytes 442376 | tf_op jit(solution)/shard_map/ppermute | solution.py:649
  3.0 3.6 %collective-permute-start.1 = (f32[18,8,256]{2,1,0:T(8,128)S(1)}, f32[18,8,256]{2,1,0:T(8,128)S(1)}, u32[]{:S(2)}, u32[]{:S(2)}) collective-permute-start(f32[18,8,256]{2,1,0:T(8,128)S(1)} %get-tuple-element.18), channel_id=1, source_target_pairs={{16,0},{32,16},{48,32},{64,48},{80,64},{96,80},{112,96},{17,1},{33... | collective-permute-start | bytes 442376 | tf_op jit(solution)/shard_map/ppermute | solution.py:650
  6.6 8.8 %middle.1 = (f32[16,136,128]{2,1,0:T(8,128)}, f32[8,128]{1,0:T(8,128)S(1)}) custom-call(f32[16]{0:T(128)} %diffuse_in.3, s32[16]{0:T(128)} %classes_in.1, s32[16]{0:T(128)} %slots_in.1, f32[16,128,256]{2,1,0:T(8,128)} %conc.5, f32[128,256]{1,0:T(8,128)} %cx.5, f32[128,256]{1,0:T(8,128)} %cy.5), custom_call_target="tpu_custom_call" | custom-call | tf_op jit(solution)/shard_map/middle/pallas_call | solution.py:652
  15.4 1.3 %collective-permute-start.2 = (f32[8,128]{1,0:T(8,128)S(1)}, f32[8,128]{1,0:T(8,128)S(1)}, u32[]{:S(2)}, u32[]{:S(2)}) collective-permute-start(f32[8,128]{1,0:T(8,128)S(1)} %get-tuple-element.19._token), channel_id=1, source_target_pairs={{16,0},{48,32},{80,64},{112,96},{17,1},{49,33},{81,65},{113,97},{1... | collective-permute-start | bytes 12296 | tf_op jit(solution)/shard_map/ppermute | solution.py:672
  16.7 0.6 pad_add_fusion.place
  17.3 1.2 %collective-permute-done.2._turn = f32[8,128]{1,0:T(8,128)S(1)} collective-permute-done((f32[8,128]{1,0:T(8,128)S(1)}, f32[8,128]{1,0:T(8,128)S(1)}, u32[]{:S(2)}, u32[]{:S(2)}) %collective-permute-start.2) | collective-permute-done | bytes 4128 | tf_op jit(solution)/shard_map/ppermute | solution.py:672
  18.5 4.3 %turn.1 = (f32[4,768,128]{2,1,0:T(8,128)}, bf16[768,768]{1,0:T(8,128)(2,1)}) custom-call(s32[2]{0:T(128)} %pad_add_fusion.place, f32[8,128]{1,0:T(8,128)S(1)} %collective-permute-done.2._turn, f32[4,768]{1,0:T(4,128)} %log_rate.1, s32[256,768]{1,0:T(8,128)} %reactants.1, s32[768,256]{1,0:T(8,128)} %products.1), custom_call_target="tpu_custom_call" | custom-call | tf_op jit(solution)/shard_map/turn/pallas_call | solution.py:679
  22.8 8.1 %all-to-all-start.1 = ((f32[16,136,128]{2,1,0:T(8,128)}), f32[16,136,128]{2,1,0:T(8,128)}, u32[]{:S(2)}, u32[]{:S(2)}) async-start(f32[16,136,128]{2,1,0:T(8,128)} %get-tuple-element.26), calls=%async_computation.1 | async-start | bytes 2228224 | tf_op jit(solution)/shard_map/all_to_all | solution.py:734
  30.9 0.0 collective-permute-done.before
  30.9 0.0 collective-permute-done.1.after
  30.9 0.0 copy-done
  30.9 12.4 %edges.1 = (f32[16,128,128]{2,1,0:T(8,128)}, f32[4,768,128]{2,1,0:T(8,128)S(1)}, bf16[768,768]{1,0:T(8,128)(2,1)S(1)}) custom-call(s32[2]{0:T(128)S(1)} %copy-done, f32[16]{0:T(128)} %diffuse_in.3, f32[16,128,256]{2,1,0:T(8,128)} %conc.5, f32[128,256]{1,0:T(8,128)} %cx.5, f32[128,256]{1,0:T(8,128)} %cy.5, f32[18,8,256]{2,1,0:T(8,128)S(1)} %collective-permute-done.before, ...), custom_call_target="tpu_custom_call" | custom-call | flops 20000000000 | bytes 10485760 | tf_op jit(solution)/shard_map/edges/pallas_call | solution.py:696
  43.3 2.8 %all-to-all-done.1.coded.x_in = f32[16,136,128]{2,1,0:T(8,128)} async-done(((f32[16,136,128]{2,1,0:T(8,128)}), f32[16,136,128]{2,1,0:T(8,128)}, u32[]{:S(2)}, u32[]{:S(2)}) %all-to-all-start.1) | async-done | bytes 1114144 | tf_op jit(solution)/shard_map/all_to_all | solution.py:734
  46.2 4.4 %all-to-all-start = ((f32[16,128,128]{2,1,0:T(8,128)}), f32[16,128,128]{2,1,0:T(8,128)}, u32[]{:S(2)}, u32[]{:S(2)}) async-start(f32[16,128,128]{2,1,0:T(8,128)} %get-tuple-element.25), calls=%async_computation | async-start | bytes 2097152 | tf_op jit(solution)/shard_map/all_to_all | solution.py:734
  50.6 11.9 %chemistry.3 = f32[2048,128]{1,0:T(8,128)} custom-call(s32[1]{0:T(128)} %bitcast.mine, f32[16,136,128]{2,1,0:T(8,128)} %all-to-all-done.1.coded.x_in, f32[16,136,128]{2,1,0:T(8,128)} %all-to-all-done.1.coded.x_in, f32[4,768,128]{2,1,0:T(8,128)S(1)} %get-tuple-element.27.log_table, bf16[768,768]{1,0:T(8,128)(2,1)S(1)} %get-tuple-element.28.both), custom_call_target="tpu_custom_call" | custom-call | tf_op jit(solution)/shard_map/chemistry/pallas_call | solution.py:547
  62.4 1.4 %all-to-all-done.x_in = f32[16,128,128]{2,1,0:T(8,128)} async-done(((f32[16,128,128]{2,1,0:T(8,128)}), f32[16,128,128]{2,1,0:T(8,128)}, u32[]{:S(2)}, u32[]{:S(2)}) %all-to-all-start) | async-done | bytes 1048608 | tf_op jit(solution)/shard_map/all_to_all | solution.py:734
  63.9 5.8 %all-to-all-start.3 = ((f32[16,16,8,128]{3,2,1,0:T(8,128)}), f32[16,16,8,128]{3,2,1,0:T(8,128)}, u32[]{:S(2)}, u32[]{:S(2)}) async-start(f32[16,16,8,128]{3,2,1,0:T(8,128)} %bitcast.5), calls=%async_computation.3 | async-start | bytes 2097152 | tf_op jit(solution)/shard_map/all_to_all | solution.py:737
  69.7 11.9 %chemistry.2 = f32[2048,128]{1,0:T(8,128)} custom-call(s32[1]{0:T(128)} %bitcast.mine, f32[16,128,128]{2,1,0:T(8,128)} %all-to-all-done.x_in, f32[16,136,128]{2,1,0:T(8,128)} %all-to-all-done.1.coded.x_in, f32[4,768,128]{2,1,0:T(8,128)S(1)} %get-tuple-element.27.log_table, bf16[768,768]{1,0:T(8,128)(2,1)S(1)} %get-tuple-element.28.both), custom_call_target="tpu_custom_call" | custom-call | tf_op jit(solution)/shard_map/chemistry/pallas_call | solution.py:547
  81.6 1.5 %all-to-all-done.3.parts = f32[16,16,8,128]{3,2,1,0:T(8,128)} async-done(((f32[16,16,8,128]{3,2,1,0:T(8,128)}), f32[16,16,8,128]{3,2,1,0:T(8,128)}, u32[]{:S(2)}, u32[]{:S(2)}) %all-to-all-start.3) | async-done | bytes 1048608 | tf_op jit(solution)/shard_map/all_to_all | solution.py:737
  83.1 5.7 %all-to-all-start.2 = ((f32[16,16,8,128]{3,2,1,0:T(8,128)}), f32[16,16,8,128]{3,2,1,0:T(8,128)S(1)}, u32[]{:S(2)}, u32[]{:S(2)}) async-start(f32[16,16,8,128]{3,2,1,0:T(8,128)} %bitcast.4), calls=%async_computation.2 | async-start | bytes 2097152 | tf_op jit(solution)/shard_map/all_to_all | solution.py:737
  88.8 2.3 %place.2.rest_0_ = f32[16,128,256]{2,1,0:T(8,128)} custom-call(f32[16,16,8,128]{3,2,1,0:T(8,128)} %all-to-all-done.3.parts), custom_call_target="tpu_custom_call" | custom-call | tf_op jit(solution)/shard_map/place/pallas_call | solution.py:591
  91.1 11.0 %all-to-all-done.2.parts = f32[16,16,8,128]{3,2,1,0:T(8,128)S(1)} async-done(((f32[16,16,8,128]{3,2,1,0:T(8,128)}), f32[16,16,8,128]{3,2,1,0:T(8,128)S(1)}, u32[]{:S(2)}, u32[]{:S(2)}) %all-to-all-start.2) | async-done | bytes 1048608 | tf_op jit(solution)/shard_map/all_to_all | solution.py:737
  102.1 1.1 %place.3 = f32[16,128,256]{2,1,0:T(8,128)} custom-call(f32[16,16,8,128]{3,2,1,0:T(8,128)S(1)} %all-to-all-done.2.parts, f32[16,128,256]{2,1,0:T(8,128)} %place.2.rest_0_), custom_call_target="tpu_custom_call", output_to_operand_aliasing={{}: (1, {})} | custom-call | tf_op jit(solution)/shard_map/place/pallas_call | solution.py:591
  (1 shorter events, 0.0 us)
Async XLA Ops:
  1.1 29.8 %collective-permute-start = (f32[18,8,256]{2,1,0:T(8,128)S(1)}, f32[18,8,256]{2,1,0:T(8,128)S(1)}, u32[]{:S(2)}, u32[]{:S(2)}) collective-permute-start(f32[18,8,256]{2,1,0:T(8,128)S(1)} %get-tuple-element.17), channel_id=1, source_target_pairs={{0,16},{16,32},{32,48},{48,64},{64,80},{80,96},{96,112},{1,17},{17... | collective-permute-start | bytes 442376 | tf_op jit(solution)/shard_map/ppermute | solution.py:649
  3.0 27.9 %collective-permute-start.1 = (f32[18,8,256]{2,1,0:T(8,128)S(1)}, f32[18,8,256]{2,1,0:T(8,128)S(1)}, u32[]{:S(2)}, u32[]{:S(2)}) collective-permute-start(f32[18,8,256]{2,1,0:T(8,128)S(1)} %get-tuple-element.18), channel_id=1, source_target_pairs={{16,0},{32,16},{48,32},{64,48},{80,64},{96,80},{112,96},{17,1},{33... | collective-permute-start | bytes 442376 | tf_op jit(solution)/shard_map/ppermute | solution.py:650
  15.4 3.1 %collective-permute-start.2 = (f32[8,128]{1,0:T(8,128)S(1)}, f32[8,128]{1,0:T(8,128)S(1)}, u32[]{:S(2)}, u32[]{:S(2)}) collective-permute-start(f32[8,128]{1,0:T(8,128)S(1)} %get-tuple-element.19._token), channel_id=1, source_target_pairs={{16,0},{48,32},{80,64},{112,96},{17,1},{49,33},{81,65},{113,97},{1... | collective-permute-start | bytes 12296 | tf_op jit(solution)/shard_map/ppermute | solution.py:672
  17.3 13.6 %copy-start = (s32[2]{0:T(128)S(1)}, s32[2]{0:T(128)}, u32[]{:S(2)}) copy-start(s32[2]{0:T(128)} %pad_add_fusion.place) | copy-start | bytes 28
  22.8 23.4 %all-to-all-start.1 = ((f32[16,136,128]{2,1,0:T(8,128)}), f32[16,136,128]{2,1,0:T(8,128)}, u32[]{:S(2)}, u32[]{:S(2)}) async-start(f32[16,136,128]{2,1,0:T(8,128)} %get-tuple-element.26), calls=%async_computation.1 | async-start | bytes 2228224 | tf_op jit(solution)/shard_map/all_to_all | solution.py:734
  46.2 17.7 %all-to-all-start = ((f32[16,128,128]{2,1,0:T(8,128)}), f32[16,128,128]{2,1,0:T(8,128)}, u32[]{:S(2)}, u32[]{:S(2)}) async-start(f32[16,128,128]{2,1,0:T(8,128)} %get-tuple-element.25), calls=%async_computation | async-start | bytes 2097152 | tf_op jit(solution)/shard_map/all_to_all | solution.py:734
  63.9 19.2 %all-to-all-start.3 = ((f32[16,16,8,128]{3,2,1,0:T(8,128)}), f32[16,16,8,128]{3,2,1,0:T(8,128)}, u32[]{:S(2)}, u32[]{:S(2)}) async-start(f32[16,16,8,128]{3,2,1,0:T(8,128)} %bitcast.5), calls=%async_computation.3 | async-start | bytes 2097152 | tf_op jit(solution)/shard_map/all_to_all | solution.py:737
  83.1 19.0 %all-to-all-start.2 = ((f32[16,16,8,128]{3,2,1,0:T(8,128)}), f32[16,16,8,128]{3,2,1,0:T(8,128)S(1)}, u32[]{:S(2)}, u32[]{:S(2)}) async-start(f32[16,16,8,128]{3,2,1,0:T(8,128)} %bitcast.4), calls=%async_computation.2 | async-start | bytes 2097152 | tf_op jit(solution)/shard_map/all_to_all | solution.py:737

commit v10 on v9

--- a/solution.py
+++ b/solution.py
@@ -245,14 +245,17 @@
     before,
     after,
     _token,
-    log_rate,
-    reactants,
-    products,
+    log_rate_in,
+    reactants_in,
+    products_in,
     early_log_table,
     early_both,
     out,
     log_table,
     both,
+    log_rate,
+    reactants,
+    products,
     diffuse,
     raw,
     wx,
@@ -287,6 +290,14 @@
 
     @pl.when(lax.rem(place[0], 2) == 1)
     def _():
+        inputs = [
+            pltpu.make_async_copy(src, dst, sems.at[len(copies) + k])
+            for k, (src, dst) in enumerate(
+                ((log_rate_in, log_rate), (reactants_in, reactants), (products_in, products))
+            )
+        ]
+        start_all(inputs)
+        wait_all(inputs)
         table_kernel(log_rate, reactants, products, log_table, both)
 
     @pl.when(lax.rem(place[0], 2) == 0)
@@ -700,17 +711,16 @@
             pltpu.HBM((peers, lines, LANES), f32),
             *table_shapes,
         ),
-        in_specs=[smem] + [hbm] * 4 + [vmem] * 3 + [
-            pl.BlockSpec(v.shape, lambda i: (0, 0)) for v in (log_rate, reactants, products)
-        ] + [hbm, hbm],
+        in_specs=[smem] + [hbm] * 4 + [vmem] * 3 + [hbm] * 5,
         out_specs=(pl.BlockSpec((peers, lines, LANES), lambda i: (0, 0, 0)), vmem, vmem),
         scratch_shapes=[
+            *[pltpu.VMEM(v.shape, v.dtype) for v in (log_rate, reactants, products)],
             pltpu.SMEM((group,), f32),
             pltpu.VMEM((2, 2, group, slab_rows, LANES), f32),
             pltpu.VMEM((2, slab_rows, columns), f32),
             pltpu.VMEM((2, slab_rows, columns), f32),
             *buffers(slab_rows),
-            pltpu.SemaphoreType.DMA((19,)),
+            pltpu.SemaphoreType.DMA((20,)),
         ],
         compiler_params=pltpu.CompilerParams(vmem_limit_bytes=24 << 20),
         cost_estimate=pl.CostEstimate(

time: 104 us -> 104 us (level)
  the two profiles are of different devices: /device:TPU:2 before, /device:TPU:4 now
where the time goes in v10:
time: 104 us; the launch traced here: 103 us
  Pallas kernels  53 us (51%)
  starting transfers between devices  30 us (29%)
  waiting for transfers between devices  19 us (18%)
    pallas_call x2, Pallas kernels, chemistry(): pl.pallas_call(functools.partial(chemistry_kernel, sources), out_shape=pl...  23.7 us
    all_to_all x2, starting transfers between devices, per_device(): gathered, = in_hbm(exchange(slab))  12.4 us
    all_to_all x2, waiting for transfers between devices, per_device(): done.append(exchange(reacted.reshape(peers, group, EDGE, LANES)))  12.3 us
    pallas_call x1, Pallas kernels, per_device(): pl.pallas_call(edge_kernel, grid=(1,), out_shape=(pltpu.HBM((peers, lines...  11.7 us
    all_to_all x2, starting transfers between devices, per_device(): done.append(exchange(reacted.reshape(peers, group, EDGE, LANES)))  10.7 us
    pallas_call x1, Pallas kernels, per_device(): pl.pallas_call(middle_kernel, grid=(1,), out_shape=(pltpu.HBM((peers, lin...  8.75 us
    all_to_all x2, waiting for transfers between devices, per_device(): gathered, = in_hbm(exchange(slab))  5.6 us
    pallas_call x1, Pallas kernels, per_device(): pl.pallas_call(turn_kernel, out_shape=(pltpu.HBM((log_rate.shape[0], reac...  4.31 us
  transfers between devices with their start and end apart: 7, of which 5 were waited for; matrix products, arithmetic and copies ran while one was open for 1% of the time, Pallas kernels for 49%

profile of v10, /device:TPU:4, one launch (start us, length us, event | category | flops | bytes accessed | tf_op | source)
XLA Modules:
  0.0 103.0 jit_solution(7411651175311763701)
XLA Ops:
  0.0 1.1 %rims.1 = (f32[18,8,256]{2,1,0:T(8,128)S(1)}, f32[18,8,256]{2,1,0:T(8,128)S(1)}) custom-call(f32[16,128,256]{2,1,0:T(8,128)} %conc.5, f32[128,256]{1,0:T(8,128)} %cx.5, f32[128,256]{1,0:T(8,128)} %cy.5), custom_call_target="tpu_custom_call" | custom-call | tf_op jit(solution)/shard_map/rims/pallas_call | solution.py:652
  1.1 1.9 %collective-permute-start = (f32[18,8,256]{2,1,0:T(8,128)S(1)}, f32[18,8,256]{2,1,0:T(8,128)S(1)}, u32[]{:S(2)}, u32[]{:S(2)}) collective-permute-start(f32[18,8,256]{2,1,0:T(8,128)S(1)} %get-tuple-element.17), channel_id=1, source_target_pairs={{0,16},{16,32},{32,48},{48,64},{64,80},{80,96},{96,112},{1,17},{17... | collective-permute-start | bytes 442376 | tf_op jit(solution)/shard_map/ppermute | solution.py:660
  3.0 3.6 %collective-permute-start.1 = (f32[18,8,256]{2,1,0:T(8,128)S(1)}, f32[18,8,256]{2,1,0:T(8,128)S(1)}, u32[]{:S(2)}, u32[]{:S(2)}) collective-permute-start(f32[18,8,256]{2,1,0:T(8,128)S(1)} %get-tuple-element.18), channel_id=1, source_target_pairs={{16,0},{32,16},{48,32},{64,48},{80,64},{96,80},{112,96},{17,1},{33... | collective-permute-start | bytes 442376 | tf_op jit(solution)/shard_map/ppermute | solution.py:661
  6.6 8.8 %middle.1 = (f32[16,136,128]{2,1,0:T(8,128)}, f32[8,128]{1,0:T(8,128)S(1)}) custom-call(f32[16]{0:T(128)} %diffuse_in.3, s32[16]{0:T(128)} %classes_in.1, s32[16]{0:T(128)} %slots_in.1, f32[16,128,256]{2,1,0:T(8,128)} %conc.5, f32[128,256]{1,0:T(8,128)} %cx.5, f32[128,256]{1,0:T(8,128)} %cy.5), custom_call_target="tpu_custom_call" | custom-call | tf_op jit(solution)/shard_map/middle/pallas_call | solution.py:663
  15.4 1.3 %collective-permute-start.2 = (f32[8,128]{1,0:T(8,128)S(1)}, f32[8,128]{1,0:T(8,128)S(1)}, u32[]{:S(2)}, u32[]{:S(2)}) collective-permute-start(f32[8,128]{1,0:T(8,128)S(1)} %get-tuple-element.19._token), channel_id=1, source_target_pairs={{16,0},{48,32},{80,64},{112,96},{17,1},{49,33},{81,65},{113,97},{1... | collective-permute-start | bytes 12296 | tf_op jit(solution)/shard_map/ppermute | solution.py:683
  16.7 0.6 pad_add_fusion.place
  17.3 1.2 %collective-permute-done.2._turn = f32[8,128]{1,0:T(8,128)S(1)} collective-permute-done((f32[8,128]{1,0:T(8,128)S(1)}, f32[8,128]{1,0:T(8,128)S(1)}, u32[]{:S(2)}, u32[]{:S(2)}) %collective-permute-start.2) | collective-permute-done | bytes 4128 | tf_op jit(solution)/shard_map/ppermute | solution.py:683
  18.5 4.3 %turn.1 = (f32[4,768,128]{2,1,0:T(8,128)}, bf16[768,768]{1,0:T(8,128)(2,1)}) custom-call(s32[2]{0:T(128)} %pad_add_fusion.place, f32[8,128]{1,0:T(8,128)S(1)} %collective-permute-done.2._turn, f32[4,768]{1,0:T(4,128)} %log_rate_in.3, s32[256,768]{1,0:T(8,128)} %reactants_in.3, s32[768,256]{1,0:T(8,128)} %products_in.3), custom_call_target="tpu_custom_call" | custom-call | tf_op jit(solution)/shard_map/turn/pallas_call | solution.py:690
  22.8 8.1 %all-to-all-start.1 = ((f32[16,136,128]{2,1,0:T(8,128)}), f32[16,136,128]{2,1,0:T(8,128)}, u32[]{:S(2)}, u32[]{:S(2)}) async-start(f32[16,136,128]{2,1,0:T(8,128)} %get-tuple-element.26), calls=%async_computation.1 | async-start | bytes 2228224 | tf_op jit(solution)/shard_map/all_to_all | solution.py:744
  30.9 0.0 collective-permute-done.before
  30.9 0.0 collective-permute-done.1.after
  30.9 0.0 copy-done
  30.9 11.7 %edges.1 = (f32[16,128,128]{2,1,0:T(8,128)}, f32[4,768,128]{2,1,0:T(8,128)S(1)}, bf16[768,768]{1,0:T(8,128)(2,1)S(1)}) custom-call(s32[2]{0:T(128)S(1)} %copy-done, f32[16]{0:T(128)} %diffuse_in.3, f32[16,128,256]{2,1,0:T(8,128)} %conc.5, f32[128,256]{1,0:T(8,128)} %cx.5, f32[128,256]{1,0:T(8,128)} %cy.5, f32[18,8,256]{2,1,0:T(8,128)S(1)} %collective-permute-done.before, ...), custom_call_target="tpu_custom_call" | custom-call | flops 20000000000 | bytes 10485760 | tf_op jit(solution)/shard_map/edges/pallas_call | solution.py:707
  42.7 3.5 %all-to-all-done.1.coded.x_in = f32[16,136,128]{2,1,0:T(8,128)} async-done(((f32[16,136,128]{2,1,0:T(8,128)}), f32[16,136,128]{2,1,0:T(8,128)}, u32[]{:S(2)}, u32[]{:S(2)}) %all-to-all-start.1) | async-done | bytes 1114144 | tf_op jit(solution)/shard_map/all_to_all | solution.py:744
  46.2 4.3 %all-to-all-start = ((f32[16,128,128]{2,1,0:T(8,128)}), f32[16,128,128]{2,1,0:T(8,128)}, u32[]{:S(2)}, u32[]{:S(2)}) async-start(f32[16,128,128]{2,1,0:T(8,128)} %get-tuple-element.25), calls=%async_computation | async-start | bytes 2097152 | tf_op jit(solution)/shard_map/all_to_all | solution.py:744
  50.5 11.9 %chemistry.3 = f32[2048,128]{1,0:T(8,128)} custom-call(s32[1]{0:T(128)} %bitcast.mine, f32[16,136,128]{2,1,0:T(8,128)} %all-to-all-done.1.coded.x_in, f32[16,136,128]{2,1,0:T(8,128)} %all-to-all-done.1.coded.x_in, f32[4,768,128]{2,1,0:T(8,128)S(1)} %get-tuple-element.27.log_table, bf16[768,768]{1,0:T(8,128)(2,1)S(1)} %get-tuple-element.28.both), custom_call_target="tpu_custom_call" | custom-call | tf_op jit(solution)/shard_map/chemistry/pallas_call | solution.py:558
  62.4 2.1 %all-to-all-done.x_in = f32[16,128,128]{2,1,0:T(8,128)} async-done(((f32[16,128,128]{2,1,0:T(8,128)}), f32[16,128,128]{2,1,0:T(8,128)}, u32[]{:S(2)}, u32[]{:S(2)}) %all-to-all-start) | async-done | bytes 1048608 | tf_op jit(solution)/shard_map/all_to_all | solution.py:744
  64.5 4.8 %all-to-all-start.3 = ((f32[16,16,8,128]{3,2,1,0:T(8,128)}), f32[16,16,8,128]{3,2,1,0:T(8,128)}, u32[]{:S(2)}, u32[]{:S(2)}) async-start(f32[16,16,8,128]{3,2,1,0:T(8,128)} %bitcast.5), calls=%async_computation.3 | async-start | bytes 2097152 | tf_op jit(solution)/shard_map/all_to_all | solution.py:747
  69.3 11.9 %chemistry.2 = f32[2048,128]{1,0:T(8,128)} custom-call(s32[1]{0:T(128)} %bitcast.mine, f32[16,128,128]{2,1,0:T(8,128)} %all-to-all-done.x_in, f32[16,136,128]{2,1,0:T(8,128)} %all-to-all-done.1.coded.x_in, f32[4,768,128]{2,1,0:T(8,128)S(1)} %get-tuple-element.27.log_table, bf16[768,768]{1,0:T(8,128)(2,1)S(1)} %get-tuple-element.28.both), custom_call_target="tpu_custom_call" | custom-call | tf_op jit(solution)/shard_map/chemistry/pallas_call | solution.py:558
  81.2 1.3 %all-to-all-done.3.parts = f32[16,16,8,128]{3,2,1,0:T(8,128)} async-done(((f32[16,16,8,128]{3,2,1,0:T(8,128)}), f32[16,16,8,128]{3,2,1,0:T(8,128)}, u32[]{:S(2)}, u32[]{:S(2)}) %all-to-all-start.3) | async-done | bytes 1048608 | tf_op jit(solution)/shard_map/all_to_all | solution.py:747
  82.4 5.9 %all-to-all-start.2 = ((f32[16,16,8,128]{3,2,1,0:T(8,128)}), f32[16,16,8,128]{3,2,1,0:T(8,128)S(1)}, u32[]{:S(2)}, u32[]{:S(2)}) async-start(f32[16,16,8,128]{3,2,1,0:T(8,128)} %bitcast.4), calls=%async_computation.2 | async-start | bytes 2097152 | tf_op jit(solution)/shard_map/all_to_all | solution.py:747
  88.4 2.3 %place.2.rest_0_ = f32[16,128,256]{2,1,0:T(8,128)} custom-call(f32[16,16,8,128]{3,2,1,0:T(8,128)} %all-to-all-done.3.parts), custom_call_target="tpu_custom_call" | custom-call | tf_op jit(solution)/shard_map/place/pallas_call | solution.py:602
  90.7 11.0 %all-to-all-done.2.parts = f32[16,16,8,128]{3,2,1,0:T(8,128)S(1)} async-done(((f32[16,16,8,128]{3,2,1,0:T(8,128)}), f32[16,16,8,128]{3,2,1,0:T(8,128)S(1)}, u32[]{:S(2)}, u32[]{:S(2)}) %all-to-all-start.2) | async-done | bytes 1048608 | tf_op jit(solution)/shard_map/all_to_all | solution.py:747
  101.7 1.1 %place.3 = f32[16,128,256]{2,1,0:T(8,128)} custom-call(f32[16,16,8,128]{3,2,1,0:T(8,128)S(1)} %all-to-all-done.2.parts, f32[16,128,256]{2,1,0:T(8,128)} %place.2.rest_0_), custom_call_target="tpu_custom_call", output_to_operand_aliasing={{}: (1, {})} | custom-call | tf_op jit(solution)/shard_map/place/pallas_call | solution.py:602
  (1 shorter events, 0.0 us)
Async XLA Ops:
  1.1 29.8 %collective-permute-start = (f32[18,8,256]{2,1,0:T(8,128)S(1)}, f32[18,8,256]{2,1,0:T(8,128)S(1)}, u32[]{:S(2)}, u32[]{:S(2)}) collective-permute-start(f32[18,8,256]{2,1,0:T(8,128)S(1)} %get-tuple-element.17), channel_id=1, source_target_pairs={{0,16},{16,32},{32,48},{48,64},{64,80},{80,96},{96,112},{1,17},{17... | collective-permute-start | bytes 442376 | tf_op jit(solution)/shard_map/ppermute | solution.py:660
  3.0 27.9 %collective-permute-start.1 = (f32[18,8,256]{2,1,0:T(8,128)S(1)}, f32[18,8,256]{2,1,0:T(8,128)S(1)}, u32[]{:S(2)}, u32[]{:S(2)}) collective-permute-start(f32[18,8,256]{2,1,0:T(8,128)S(1)} %get-tuple-element.18), channel_id=1, source_target_pairs={{16,0},{32,16},{48,32},{64,48},{80,64},{96,80},{112,96},{17,1},{33... | collective-permute-start | bytes 442376 | tf_op jit(solution)/shard_map/ppermute | solution.py:661
  15.4 3.1 %collective-permute-start.2 = (f32[8,128]{1,0:T(8,128)S(1)}, f32[8,128]{1,0:T(8,128)S(1)}, u32[]{:S(2)}, u32[]{:S(2)}) collective-permute-start(f32[8,128]{1,0:T(8,128)S(1)} %get-tuple-element.19._token), channel_id=1, source_target_pairs={{16,0},{48,32},{80,64},{112,96},{17,1},{49,33},{81,65},{113,97},{1... | collective-permute-start | bytes 12296 | tf_op jit(solution)/shard_map/ppermute | solution.py:683
  17.3 13.6 %copy-start = (s32[2]{0:T(128)S(1)}, s32[2]{0:T(128)}, u32[]{:S(2)}) copy-start(s32[2]{0:T(128)} %pad_add_fusion.place) | copy-start | bytes 28
  22.8 23.4 %all-to-all-start.1 = ((f32[16,136,128]{2,1,0:T(8,128)}), f32[16,136,128]{2,1,0:T(8,128)}, u32[]{:S(2)}, u32[]{:S(2)}) async-start(f32[16,136,128]{2,1,0:T(8,128)} %get-tuple-element.26), calls=%async_computation.1 | async-start | bytes 2228224 | tf_op jit(solution)/shard_map/all_to_all | solution.py:744
  46.2 18.3 %all-to-all-start = ((f32[16,128,128]{2,1,0:T(8,128)}), f32[16,128,128]{2,1,0:T(8,128)}, u32[]{:S(2)}, u32[]{:S(2)}) async-start(f32[16,128,128]{2,1,0:T(8,128)} %get-tuple-element.25), calls=%async_computation | async-start | bytes 2097152 | tf_op jit(solution)/shard_map/all_to_all | solution.py:744
  64.5 17.9 %all-to-all-start.3 = ((f32[16,16,8,128]{3,2,1,0:T(8,128)}), f32[16,16,8,128]{3,2,1,0:T(8,128)}, u32[]{:S(2)}, u32[]{:S(2)}) async-start(f32[16,16,8,128]{3,2,1,0:T(8,128)} %bitcast.5), calls=%async_computation.3 | async-start | bytes 2097152 | tf_op jit(solution)/shard_map/all_to_all | solution.py:747
  82.4 19.3 %all-to-all-start.2 = ((f32[16,16,8,128]{3,2,1,0:T(8,128)}), f32[16,16,8,128]{3,2,1,0:T(8,128)S(1)}, u32[]{:S(2)}, u32[]{:S(2)}) async-start(f32[16,16,8,128]{3,2,1,0:T(8,128)} %bitcast.4), calls=%async_computation.2 | async-start | bytes 2097152 | tf_op jit(solution)/shard_map/all_to_all | solution.py:747
